TPU v7x, 32 devices: a whole 2x2x4 slice. The times are simulated.
32 devices in a mesh: dp: 4 (over x, core), seq: 8 (over z, y).
Axes of the slice: x: 2, y: 2, z: 4, core: 2. Of those that a mesh axis runs over, the one named last changes fastest.
Arguments:
- tokens: bfloat16 [4, 2, 1024, 1024], P('dp', None, 'seq'), may hold values from -6 to 6
- cotangent: bfloat16 [4, 2, 1024, 1024], P('dp', None, 'seq'), may hold values from -6 to 6
- node_lengths: int32 [4, 2, 13], P('dp'), may hold values from 1 to 512, 1024 in all within a row
- parents: int32 [4, 2, 13], P('dp'), may hold values from 0 to 11, as said below
- w_query: bfloat16 [1024, 2048], P(('dp', 'seq')), may hold values from -0.1875 to 0.1875
- w_key: bfloat16 [1024, 1024], P(('dp', 'seq')), may hold values from -0.1875 to 0.1875
- w_value: bfloat16 [1024, 1024], P(('dp', 'seq')), may hold values from -0.1875 to 0.1875
- w_output: bfloat16 [2048, 1024], P(('dp', 'seq')), may hold values from -1.5 to 1.5
- w_gate: bfloat16 [1024, 3072], P(('dp', 'seq')), may hold values from -0.1875 to 0.1875
- w_up: bfloat16 [1024, 3072], P(('dp', 'seq')), may hold values from -0.1875 to 0.1875
- w_down: bfloat16 [3072, 1024], P(('dp', 'seq')), may hold values from -0.109375 to 0.109375
- attn_gain: bfloat16 [1024], P(('dp', 'seq')), may hold values from 0.5 to 1.5
- ffn_gain: bfloat16 [1024], P(('dp', 'seq')), may hold values from 0.5 to 1.5
- query_gain: bfloat16 [128], P(('dp', 'seq')), may hold values from 0.5 to 1.5
- key_gain: bfloat16 [128], P(('dp', 'seq')), may hold values from 0.5 to 1.5
Outputs:
- outputs: bfloat16 [4, 2, 1024, 1024], P('dp', None, 'seq')
- input_grad: float32 [4, 2, 1024, 1024], P('dp', None, 'seq')
- grad_query: float32 [1024, 2048], P(('dp', 'seq'))
- grad_key: float32 [1024, 1024], P(('dp', 'seq'))
- grad_value: float32 [1024, 1024], P(('dp', 'seq'))
- grad_output: float32 [2048, 1024], P(('dp', 'seq'))
- grad_gate: float32 [1024, 3072], P(('dp', 'seq'))
- grad_up: float32 [1024, 3072], P(('dp', 'seq'))
- grad_down: float32 [3072, 1024], P(('dp', 'seq'))
- grad_attn_gain: float32 [1024], P(('dp', 'seq'))
- grad_ffn_gain: float32 [1024], P(('dp', 'seq'))
- grad_query_gain: float32 [128], P(('dp', 'seq'))
- grad_key_gain: float32 [128], P(('dp', 'seq'))
Inputs may be any that keep to these rules, and one draw needn't show every extreme that they name: `node_lengths`: each tree's 13 node lengths sum to 1024. `parents`: node 0 is the root and its entry is 0; every other node's parent is a node below it.
All inputs are finite; a program needn't handle non-finite values.
Results may differ from a plain program's by a relative error of at most 0.023.
Values may be sent and summed in bfloat16 or wider, within the bound.
A program may use at most 320 MiB of HBM per device.

v0:
```python
import jax
import jax.numpy as jnp
from jax import lax
from jax.sharding import PartitionSpec as P

D = 1024
HEADS = 16
KV_HEADS = 8
HEAD_DIM = 128
FF = 3072
MICRO = 2


EPSILON = 1e-06
THETA = 1000000.0
NEGATIVE = -1e30
PRECISE = lax.Precision.HIGHEST


def norm_rows(values, row_gain):
    return (
        values * lax.rsqrt(jnp.mean(values * values, axis=-1, keepdims=True) + EPSILON) * row_gain
    )


def rope_tables(position, head_dim):
    half_dim = head_dim // 2
    inv_freq = THETA ** (-(jnp.arange(half_dim, dtype=jnp.float32) * (2.0 / head_dim)))
    angles = position.astype(jnp.float32)[:, None] * inv_freq[None, :]
    cosine_table = jnp.cos(angles)
    sine_table = jnp.sin(angles)
    return (
        jnp.concatenate([cosine_table, cosine_table], axis=1),
        jnp.concatenate([sine_table, sine_table], axis=1),
    )


def rotate(values, cosine_table, sine_table):
    half_dim = values.shape[-1] // 2
    turned = jnp.concatenate([-values[..., half_dim:], values[..., :half_dim]], axis=-1)
    return values * cosine_table[:, None, :] + turned * sine_table[:, None, :]


def tree_tables(lengths, parent_row):
    node_count = lengths.shape[0]
    labels = jnp.arange(node_count, dtype=jnp.int32)
    parent_hot = ((parent_row[:, None] == labels[None, :]) & (labels[:, None] > 0)).astype(
        jnp.int32
    )

    def extend(depth_step, state_pair):
        reached, covered = state_pair
        reached = jnp.sum(reached[:, :, None] * parent_hot[None, :, :], axis=1)
        return (reached, covered + reached)

    reached, covered = lax.fori_loop(0, node_count, extend, (parent_hot, parent_hot))
    ancestry = (covered > 0).astype(jnp.float32)
    starts = jnp.cumsum(lengths) - lengths
    path_base = jnp.sum(jnp.where(covered > 0, lengths[None, :], 0), axis=1)
    return (labels, starts, path_base, ancestry)


def token_nodes(token_index, labels, starts, path_base):
    node_id = jnp.sum((token_index[:, None] >= starts[None, 1:]).astype(jnp.int32), axis=1)
    member = node_id[:, None] == labels[None, :]
    offset = jnp.sum(jnp.where(member, (path_base - starts)[None, :], 0), axis=1)
    return (member.astype(jnp.float32), token_index + offset)


def visible(query_member, query_index, key_member, key_index, ancestry):
    numbers = (((1,), (1,)), ((), ()))
    lifted = jnp.dot(query_member, ancestry, precision=PRECISE)
    above = lax.dot_general(lifted, key_member, numbers, precision=PRECISE)
    same_node = lax.dot_general(query_member, key_member, numbers, precision=PRECISE)
    return (above > 0.5) | (same_node > 0.5) & (key_index[None, :] <= query_index[:, None])


def product(left_side, right_side):
    return jnp.dot(left_side, right_side, preferred_element_type=jnp.float32)


def against(left_side, right_side):
    return lax.dot_general(
        left_side, right_side, (((1,), (1,)), ((), ())), preferred_element_type=jnp.float32
    )


def across(left_side, right_side):
    return lax.dot_general(
        left_side, right_side, (((0,), (0,)), ((), ())), preferred_element_type=jnp.float32
    )


def shards(
    tokens,
    cotangent,
    node_lengths,
    parents,
    w_query,
    w_key,
    w_value,
    w_output,
    w_gate,
    w_up,
    w_down,
    attn_gain,
    ffn_gain,
    query_gain,
    key_gain,
):
    rows_here = tokens.shape[2]
    length = lax.axis_size("seq") * rows_here
    group_size = HEADS // KV_HEADS
    pair_count = KV_HEADS // 2
    width_query = 2 * group_size * HEAD_DIM
    width_key = 2 * HEAD_DIM
    score_scale = HEAD_DIM ** (-0.5)
    local_index = lax.axis_index("seq") * rows_here + jnp.arange(rows_here, dtype=jnp.int32)
    full_index = jnp.arange(length, dtype=jnp.int32)
    pair_ids = jnp.arange(pair_count, dtype=jnp.int32)
    float_type = jnp.float32
    brain_type = jnp.bfloat16
    sums = (
        jnp.zeros((D, HEADS * HEAD_DIM), float_type),
        jnp.zeros((D, KV_HEADS * HEAD_DIM), float_type),
        jnp.zeros((D, KV_HEADS * HEAD_DIM), float_type),
        jnp.zeros((HEADS * HEAD_DIM, D), float_type),
        jnp.zeros((D, FF), float_type),
        jnp.zeros((D, FF), float_type),
        jnp.zeros((FF, D), float_type),
        jnp.zeros((D,), float_type),
        jnp.zeros((D,), float_type),
        jnp.zeros((HEAD_DIM,), float_type),
        jnp.zeros((HEAD_DIM,), float_type),
    )
    out_list = []
    grad_list = []
    for batch_index in range(MICRO):
        attn_fwd = (
            lax.all_gather(w_query, ("dp", "seq"), axis=0, tiled=True),
            lax.all_gather(w_key, ("dp", "seq"), axis=0, tiled=True),
            lax.all_gather(w_value, ("dp", "seq"), axis=0, tiled=True),
            lax.all_gather(w_output, ("dp", "seq"), axis=0, tiled=True),
            lax.all_gather(attn_gain, ("dp", "seq"), axis=0, tiled=True),
            lax.all_gather(query_gain, ("dp", "seq"), axis=0, tiled=True),
            lax.all_gather(key_gain, ("dp", "seq"), axis=0, tiled=True),
        )
        ffn_fwd = (
            lax.all_gather(w_gate, ("dp", "seq"), axis=0, tiled=True),
            lax.all_gather(w_up, ("dp", "seq"), axis=0, tiled=True),
            lax.all_gather(w_down, ("dp", "seq"), axis=0, tiled=True),
            lax.all_gather(ffn_gain, ("dp", "seq"), axis=0, tiled=True),
        )
        query_w, key_w, value_w, output_w, attn_g, query_g, key_g = attn_fwd
        gate_w, up_w, down_w, ffn_g = ffn_fwd
        labels, starts, path_base, ancestry = tree_tables(
            node_lengths[0, batch_index], parents[0, batch_index]
        )
        member_here, position = token_nodes(local_index, labels, starts, path_base)
        member_all, unused_position = token_nodes(full_index, labels, starts, path_base)
        keep_mask = visible(member_here, local_index, member_all, full_index, ancestry)
        cosine_table, sine_table = rope_tables(position, HEAD_DIM)
        rows_in = tokens[0, batch_index].astype(float_type)
        attn_g32 = attn_g.astype(float_type)
        query_g32 = query_g.astype(float_type)
        key_g32 = key_g.astype(float_type)
        normed_in = norm_rows(rows_in, attn_g32).astype(brain_type)
        query_heads = product(normed_in, query_w).reshape(rows_here, HEADS, HEAD_DIM)
        key_heads = product(normed_in, key_w).reshape(rows_here, KV_HEADS, HEAD_DIM)
        value_low = product(normed_in, value_w).astype(brain_type)
        query_rot = (
            rotate(norm_rows(query_heads, query_g32), cosine_table, sine_table)
            .astype(brain_type)
            .reshape(rows_here, HEADS * HEAD_DIM)
        )
        key_rot = (
            rotate(norm_rows(key_heads, key_g32), cosine_table, sine_table)
            .astype(brain_type)
            .reshape(rows_here, KV_HEADS * HEAD_DIM)
        )
        key_all, value_all = (
            lax.all_gather(key_rot, "seq", axis=0, tiled=True),
            lax.all_gather(value_low, "seq", axis=0, tiled=True),
        )

        def attend_pair(pair_id):
            query_pair = lax.dynamic_slice_in_dim(
                query_rot, pair_id * width_query, width_query, 1
            ).reshape(rows_here, 2, group_size, HEAD_DIM)
            key_pair = lax.dynamic_slice_in_dim(key_all, pair_id * width_key, width_key, 1).reshape(
                length, 2, HEAD_DIM
            )
            value_pair = lax.dynamic_slice_in_dim(
                value_all, pair_id * width_key, width_key, 1
            ).reshape(length, 2, HEAD_DIM)
            raw_score = jnp.einsum(
                "qhgd,khd->hgqk", query_pair, key_pair, preferred_element_type=jnp.float32
            )
            scores = jnp.where(keep_mask[None, None], raw_score * score_scale, NEGATIVE)
            row_top = jnp.max(scores, axis=-1, keepdims=True)
            weight = jnp.exp(scores - row_top)
            row_total = jnp.sum(weight, axis=-1, keepdims=True)
            soft_low = (weight / row_total).astype(jnp.bfloat16)
            mixed = jnp.einsum(
                "hgqk,khd->qhgd", soft_low, value_pair, preferred_element_type=jnp.float32
            )
            return (mixed, row_top + jnp.log(row_total))

        mixed_pairs, log_totals = lax.map(attend_pair, pair_ids)
        attended = (
            mixed_pairs.transpose(1, 0, 2, 3, 4)
            .reshape(rows_here, HEADS * HEAD_DIM)
            .astype(brain_type)
        )
        middle = rows_in + product(attended, output_w)
        ffn_g32 = ffn_g.astype(float_type)
        normed_mid = norm_rows(middle, ffn_g32).astype(brain_type)
        gate_lin = product(normed_mid, gate_w)
        up_lin = product(normed_mid, up_w)
        activated = (jax.nn.silu(gate_lin) * up_lin).astype(brain_type)
        out_list.append((middle + product(activated, down_w)).astype(brain_type))
        attn_back = (
            lax.all_gather(w_query, ("dp", "seq"), axis=0, tiled=True),
            lax.all_gather(w_key, ("dp", "seq"), axis=0, tiled=True),
            lax.all_gather(w_value, ("dp", "seq"), axis=0, tiled=True),
            lax.all_gather(w_output, ("dp", "seq"), axis=0, tiled=True),
            lax.all_gather(attn_gain, ("dp", "seq"), axis=0, tiled=True),
            lax.all_gather(query_gain, ("dp", "seq"), axis=0, tiled=True),
            lax.all_gather(key_gain, ("dp", "seq"), axis=0, tiled=True),
        )
        ffn_back = (
            lax.all_gather(w_gate, ("dp", "seq"), axis=0, tiled=True),
            lax.all_gather(w_up, ("dp", "seq"), axis=0, tiled=True),
            lax.all_gather(w_down, ("dp", "seq"), axis=0, tiled=True),
            lax.all_gather(ffn_gain, ("dp", "seq"), axis=0, tiled=True),
        )
        key_back, value_back = (
            lax.all_gather(key_rot, "seq", axis=0, tiled=True),
            lax.all_gather(value_low, "seq", axis=0, tiled=True),
        )
        query_wb, key_wb, value_wb, output_wb, attn_gb, query_gb, key_gb = attn_back
        gate_wb, up_wb, down_wb, ffn_gb = ffn_back
        cot_rows = cotangent[0, batch_index]
        grad_down = across(activated, cot_rows)
        d_activated = against(cot_rows, down_wb)
        sigma_gate = jax.nn.sigmoid(gate_lin)
        d_gate = (d_activated * up_lin * sigma_gate * (1.0 + gate_lin * (1.0 - sigma_gate))).astype(
            brain_type
        )
        d_up = (d_activated * gate_lin * sigma_gate).astype(brain_type)
        grad_gate = across(normed_mid, d_gate)
        grad_up = across(normed_mid, d_up)
        d_normed_mid = against(d_gate, gate_wb) + against(d_up, up_wb)
        unused_mid, pull_ffn = jax.vjp(norm_rows, middle, ffn_gb.astype(float_type))
        d_mid_norm, grad_ffn_gain = pull_ffn(d_normed_mid)
        d_middle = cot_rows.astype(float_type) + d_mid_norm
        d_middle_low = d_middle.astype(brain_type)
        grad_output = across(attended, d_middle_low)
        d_attended = against(d_middle_low, output_wb).astype(brain_type)

        def back_pair(pair_id):
            query_pair = lax.dynamic_slice_in_dim(
                query_rot, pair_id * width_query, width_query, 1
            ).reshape(rows_here, 2, group_size, HEAD_DIM)
            grad_pair = lax.dynamic_slice_in_dim(
                d_attended, pair_id * width_query, width_query, 1
            ).reshape(rows_here, 2, group_size, HEAD_DIM)
            key_pair = lax.dynamic_slice_in_dim(
                key_back, pair_id * width_key, width_key, 1
            ).reshape(length, 2, HEAD_DIM)
            value_pair = lax.dynamic_slice_in_dim(
                value_back, pair_id * width_key, width_key, 1
            ).reshape(length, 2, HEAD_DIM)
            raw_score = jnp.einsum(
                "qhgd,khd->hgqk", query_pair, key_pair, preferred_element_type=jnp.float32
            )
            scores = jnp.where(keep_mask[None, None], raw_score * score_scale, NEGATIVE)
            soft_prob = jnp.exp(scores - log_totals[pair_id])
            soft_low = soft_prob.astype(jnp.bfloat16)
            d_prob = jnp.einsum(
                "qhgd,khd->hgqk", grad_pair, value_pair, preferred_element_type=jnp.float32
            )
            d_score = soft_prob * (d_prob - jnp.sum(soft_prob * d_prob, axis=-1, keepdims=True))
            d_raw = (d_score * score_scale).astype(jnp.bfloat16)
            d_query = jnp.einsum(
                "hgqk,khd->qhgd", d_raw, key_pair, preferred_element_type=jnp.float32
            )
            d_key = jnp.einsum(
                "hgqk,qhgd->khd", d_raw, query_pair, preferred_element_type=jnp.float32
            )
            d_value = jnp.einsum(
                "hgqk,qhgd->khd", soft_low, grad_pair, preferred_element_type=jnp.float32
            )
            return (
                d_query,
                jnp.concatenate(
                    [d_key.reshape(length, width_key), d_value.reshape(length, width_key)], axis=1
                ),
            )

        d_query_pairs, kv_terms = lax.map(back_pair, pair_ids)
        kv_share = lax.psum_scatter(
            kv_terms.astype(jnp.bfloat16), "seq", scatter_dimension=1, tiled=True
        ).astype(jnp.float32)
        d_key_rot = (
            kv_share[:, :, :width_key]
            .reshape(pair_count, rows_here, 2, HEAD_DIM)
            .transpose(1, 0, 2, 3)
            .reshape(rows_here, KV_HEADS, HEAD_DIM)
        )
        d_value_low = (
            kv_share[:, :, width_key:]
            .transpose(1, 0, 2)
            .reshape(rows_here, KV_HEADS * HEAD_DIM)
            .astype(brain_type)
        )
        d_query_rot = d_query_pairs.transpose(1, 0, 2, 3, 4).reshape(rows_here, HEADS, HEAD_DIM)

        def turn_rows(heads_in, gain_in):
            return rotate(norm_rows(heads_in, gain_in), cosine_table, sine_table)

        unused_query, pull_query = jax.vjp(turn_rows, query_heads, query_gb.astype(float_type))
        d_query_heads, grad_query_gain = pull_query(d_query_rot)
        unused_key, pull_key = jax.vjp(turn_rows, key_heads, key_gb.astype(float_type))
        d_key_heads, grad_key_gain = pull_key(d_key_rot)
        d_query_low = d_query_heads.reshape(rows_here, HEADS * HEAD_DIM).astype(brain_type)
        d_key_low = d_key_heads.reshape(rows_here, KV_HEADS * HEAD_DIM).astype(brain_type)
        grad_query = across(normed_in, d_query_low)
        grad_key = across(normed_in, d_key_low)
        grad_value = across(normed_in, d_value_low)
        d_normed_in = (
            against(d_query_low, query_wb)
            + against(d_key_low, key_wb)
            + against(d_value_low, value_wb)
        )
        unused_in, pull_attn = jax.vjp(norm_rows, rows_in, attn_gb.astype(float_type))
        d_in_norm, grad_attn_gain = pull_attn(d_normed_in)
        grad_list.append(d_middle + d_in_norm)
        fresh = (
            grad_query,
            grad_key,
            grad_value,
            grad_output,
            grad_gate,
            grad_up,
            grad_down,
            grad_attn_gain,
            grad_ffn_gain,
            grad_query_gain,
            grad_key_gain,
        )
        sums = tuple((old + new for old, new in zip(sums, fresh)))
    attn_parts = (
        lax.psum_scatter(sums[0], ("dp", "seq"), scatter_dimension=0, tiled=True),
        lax.psum_scatter(sums[1], ("dp", "seq"), scatter_dimension=0, tiled=True),
        lax.psum_scatter(sums[2], ("dp", "seq"), scatter_dimension=0, tiled=True),
        lax.psum_scatter(sums[3], ("dp", "seq"), scatter_dimension=0, tiled=True),
        lax.psum_scatter(sums[7], ("dp", "seq"), scatter_dimension=0, tiled=True),
        lax.psum_scatter(sums[9], ("dp", "seq"), scatter_dimension=0, tiled=True),
        lax.psum_scatter(sums[10], ("dp", "seq"), scatter_dimension=0, tiled=True),
    )
    ffn_parts = (
        lax.psum_scatter(sums[4], ("dp", "seq"), scatter_dimension=0, tiled=True),
        lax.psum_scatter(sums[5], ("dp", "seq"), scatter_dimension=0, tiled=True),
        lax.psum_scatter(sums[6], ("dp", "seq"), scatter_dimension=0, tiled=True),
        lax.psum_scatter(sums[8], ("dp", "seq"), scatter_dimension=0, tiled=True),
    )
    outputs = jnp.stack(out_list)[None]
    input_grad = jnp.stack(grad_list)[None]
    return (
        outputs,
        input_grad,
        attn_parts[0],
        attn_parts[1],
        attn_parts[2],
        attn_parts[3],
        ffn_parts[0],
        ffn_parts[1],
        ffn_parts[2],
        attn_parts[4],
        ffn_parts[3],
        attn_parts[5],
        attn_parts[6],
    )


def solution(mesh):
    return jax.shard_map(
        shards,
        mesh=mesh,
        in_specs=(
            P("dp", None, "seq", None),
            P("dp", None, "seq", None),
            P("dp", None, None),
            P("dp", None, None),
            P(("dp", "seq"), None),
            P(("dp", "seq"), None),
            P(("dp", "seq"), None),
            P(("dp", "seq"), None),
            P(("dp", "seq"), None),
            P(("dp", "seq"), None),
            P(("dp", "seq"), None),
            P(("dp", "seq")),
            P(("dp", "seq")),
            P(("dp", "seq")),
            P(("dp", "seq")),
        ),
        out_specs=(
            P("dp", None, "seq", None),
            P("dp", None, "seq", None),
            P(("dp", "seq"), None),
            P(("dp", "seq"), None),
            P(("dp", "seq"), None),
            P(("dp", "seq"), None),
            P(("dp", "seq"), None),
            P(("dp", "seq"), None),
            P(("dp", "seq"), None),
            P(("dp", "seq")),
            P(("dp", "seq")),
            P(("dp", "seq")),
            P(("dp", "seq")),
        ),
        check_vma=False,
    )
```

profile of v0, /device:TPU:21, one launch (start us, length us, event | category | flops | bytes accessed | tf_op | source)
XLA Modules:
  0.0 2176.0 jit_solution(14842388288279421055)
XLA Ops:
  12.1 39.7 %all-reduce.17 = (bf16[1024]{0:T(1024)(128)(2,1)S(1)}, bf16[128]{0:T(256)(128)(2,1)S(1)}, bf16[128]{0:T(256)(128)(2,1)}, bf16[1024]{0:T(1024)(128)(2,1)}) all-reduce(bf16[1024]{0:T(1024)(128)(2,1)S(1)} %dynamic-update-slice, bf16[128]{0:T(256)(128)(2,1)S(1)} %dynamic-update-slice.1, ...), channel_id=1, replica_groups=mesh['dp'=4,'seq'=8] {'dp','seq'}, use_global_device_ids=true, to_apply=%add.8 | all-reduce | flops 2304 | bytes 9216
  53.1 14.4 all-gather.12.cloned.1.call-done
  80.8 45.3 %all-gather.16.cloned.1.call-done = bf16[1024,1024]{1,0:T(8,128)(2,1)} async-done(((bf16[32,1024]{1,0:T(8,128)(2,1)}), bf16[1024,1024]{1,0:T(8,128)(2,1)}) %all-gather.16.cloned.1.call-update) | async-done | bytes 2097168 | tf_op jit(solution)/shard_map/all_gather | solution.py:141
  141.2 34.9 %all-gather.30.cloned.1.call-done = bf16[1024,1024]{1,0:T(8,128)(2,1)} async-done(((bf16[128,1024]{1,0:T(8,128)(2,1)}), bf16[1024,1024]{1,0:T(8,128)(2,1)}) %all-gather.30.cloned.1.call-update) | async-done | bytes 2097168 | tf_op jit(solution)/shard_map/all_gather | solution.py:183
  179.0 47.5 %all-gather.14.cloned.1.call-done = bf16[1024,1024]{1,0:T(8,128)(2,1)} async-done(((bf16[128,1024]{1,0:T(8,128)(2,1)}), bf16[1024,1024]{1,0:T(8,128)(2,1)}) %all-gather.14.cloned.1.call-update) | async-done | bytes 2097168 | tf_op jit(solution)/shard_map/all_gather | solution.py:183
  226.5 3.9 copy.142
  230.5 61.2 %all-gather.20.cloned.1.call-done = bf16[1024,2048]{1,0:T(8,128)(2,1)} async-done(((bf16[32,2048]{1,0:T(8,128)(2,1)}), bf16[1024,2048]{1,0:T(8,128)(2,1)}) %all-gather.20.cloned.1.call-update) | async-done | bytes 4194320 | tf_op jit(solution)/shard_map/all_gather | solution.py:140
  291.7 6.4 copy.141
  306.4 35.6 %all-gather.18.cloned.1.call-done = bf16[1024,1024]{0,1:T(8,128)(2,1)} async-done(((bf16[128,1024]{0,1:T(8,128)(2,1)}), bf16[1024,1024]{0,1:T(8,128)(2,1)}) %all-gather.18.cloned.1.call-update) | async-done | bytes 2097168 | tf_op jit(solution)/shard_map/all_gather | solution.py:182
  342.0 29.8 %while.74 = (s32[]{:T(128)}, bf16[4,128,2,2,128]{1,4,3,2,0:T(8,128)(2,1)}, f32[4,2,2,128,1]{3,2,1,4,0:T(2,128)S(1)}, s32[4]{0:T(128)S(1)}, bf16[1024,1024]{0,1:T...) while((s32[]{:T(128)}, ...), condition=%wide.region_14.15_spmd, body=%wide.region_11.14_spmd.sunk | while | flops 272629248 | bytes 16531801 | solution.py:209
  371.8 35.5 %all-gather.22.cloned.1.call-done = bf16[2048,1024]{1,0:T(8,128)(2,1)} async-done(((bf16[64,1024]{1,0:T(8,128)(2,1)}), bf16[2048,1024]{1,0:T(8,128)(2,1)}) %all-gather.22.cloned.1.call-update) | async-done | bytes 4194320 | tf_op jit(solution)/shard_map/all_gather | solution.py:143
  407.3 4.0 multiply_reduce_fusion.18
  413.1 44.6 %all-gather.32.cloned.1.call-done = bf16[1024,1024]{0,1:T(8,128)(2,1)} async-done(((bf16[128,1024]{0,1:T(8,128)(2,1)}), bf16[1024,1024]{0,1:T(8,128)(2,1)}) %all-gather.32.cloned.1.call-update) | async-done | bytes 2097168 | tf_op jit(solution)/shard_map/all_gather | solution.py:182
  457.7 29.2 %while.75 = (s32[]{:T(128)}, bf16[4,128,2,2,128]{1,4,3,2,0:T(8,128)(2,1)}, f32[4,2,2,128,1]{3,2,1,4,0:T(2,128)S(1)}, s32[4]{0:T(128)S(1)}, bf16[1024,1024]{0,1:T...) while((s32[]{:T(128)}, ...), condition=%wide.region_30.31_spmd, body=%wide.region_27.30_spmd.sunk | while | flops 272629248 | bytes 16531801 | solution.py:209
  487.0 4.7 multiply_reduce_fusion.16
  491.8 38.5 %all-gather.24.cloned.1.call-done = bf16[1024,3072]{1,0:T(8,128)(2,1)} async-done(((bf16[32,3072]{1,0:T(8,128)(2,1)}), bf16[1024,3072]{1,0:T(8,128)(2,1)}) %all-gather.24.cloned.1.call-update) | async-done | bytes 6291472 | tf_op jit(solution)/shard_map/all_gather | solution.py:149
  530.4 4.9 fusion.190
  535.3 65.8 %all-gather.26.cloned.1.call-done = bf16[1024,3072]{1,0:T(8,128)(2,1)} async-done(((bf16[32,3072]{1,0:T(8,128)(2,1)}), bf16[1024,3072]{1,0:T(8,128)(2,1)}) %all-gather.26.cloned.1.call-update) | async-done | bytes 6291472 | tf_op jit(solution)/shard_map/all_gather | solution.py:150
  601.2 4.9 fusion.191
  606.1 66.0 %all-gather.28.cloned.1.call-done = bf16[3072,1024]{1,0:T(8,128)(2,1)} async-done(((bf16[96,1024]{1,0:T(8,128)(2,1)}), bf16[3072,1024]{1,0:T(8,128)(2,1)}) %all-gather.28.cloned.1.call-update) | async-done | bytes 6291472 | tf_op jit(solution)/shard_map/all_gather | solution.py:151
  672.1 7.4 multiply_convert_fusion.2
  679.5 5.6 fusion.194
  707.3 95.8 %while.76 = (s32[]{:T(128)}, f32[4,128,2,2,128]{1,4,3,2,0:T(8,128)}, bf16[4,1024,512]{1,2,0:T(8,128)(2,1)}, s32[4]{0:T(128)S(1)}, bf16[1024,1024]{0,1:T(8,128)(2...) while((s32[]{:T(128)}, ...), condition=%wide.region_35.36_spmd, body=%wide.region_33.35_spmd.sunk | while | flops 680528896 | bytes 27924844 | solution.py:301
  725.2 3.9 fusion.356
  749.2 3.9 fusion.356
  773.1 3.9 fusion.356
  803.1 7.9 copy.192
  811.0 5.6 copy.198
  817.6 4.5 convolution_convert_fusion
  825.7 98.8 %while.77 = (s32[]{:T(128)}, f32[4,128,2,2,128]{1,4,3,2,0:T(8,128)}, bf16[4,1024,512]{1,2,0:T(8,128)(2,1)}, s32[4]{0:T(128)S(1)}, bf16[1024,1024]{0,1:T(8,128)(2...) while((s32[]{:T(128)}, ...), condition=%wide.region_43.44_spmd, body=%wide.region_41.43_spmd.sunk | while | flops 680528896 | bytes 27924844 | solution.py:301
  893.9 3.9 fusion.370
  924.6 7.9 copy.194
  932.4 5.6 copy.199
  945.9 4.7 convolution_add_fusion.4
  953.1 4.6 convolution_add_fusion.3
  960.7 6.4 convolution_add_fusion.2
  970.1 6.4 convolution_add_fusion.1
  980.7 6.5 convolution_add_fusion
  991.6 32.9 %reduce-scatter.30.cloned.1.call-done = bf16[128,2048]{1,0:T(8,128)(2,1)} async-done(((bf16[1024,2048]{1,0:T(8,128)(2,1)}), bf16[128,2048]{1,0:T(8,128)(2,1)}) %reduce-scatter.30.cloned.1.call-update) | async-done | bytes 524304
  1050.9 4.0 fusion.49
  1063.5 43.1 %all-reduce.16 = (f32[1024]{0:T(1024)S(1)}, f32[1024]{0:T(1024)S(1)}, f32[128]{0:T(128)S(1)}, f32[128]{0:T(128)S(1)}) all-reduce(f32[1024]{0:T(1024)S(1)} %add.393, f32[1024]{0:T(1024)S(1)} %add.394, f32[128]{0:T(128)S(1)} %add.395, f32[128]{0:T(128)S(1)} %add.396), channel_id=11, replica_groups=mesh['dp'=4,'seq'=8] {'dp','seq'}, use_global_device_ids=true, to_apply=%region_57.58.clone | all-reduce | flops 2304 | bytes 18432
  1110.3 101.9 %reduce-scatter.14.cloned.1.call-done = f32[32,2048]{1,0:T(8,128)} async-done(((f32[1024,2048]{1,0:T(8,128)}), f32[32,2048]{1,0:T(8,128)}) %reduce-scatter.14.cloned.1.call-update) | async-done | bytes 262160 | tf_op jit(solution)/shard_map/reduce_scatter | solution.py:354
  1212.2 186.8 %reduce-scatter.20.cloned.1.call-done = f32[64,1024]{1,0:T(8,128)} async-done(((f32[2048,1024]{1,0:T(8,128)}), f32[64,1024]{1,0:T(8,128)}) %reduce-scatter.20.cloned.1.call-update) | async-done | bytes 262160 | tf_op jit(solution)/shard_map/reduce_scatter | solution.py:357
  1399.0 160.0 %reduce-scatter.22.cloned.1.call-done = f32[32,3072]{1,0:T(8,128)} async-done(((f32[1024,3072]{1,0:T(8,128)}), f32[32,3072]{1,0:T(8,128)}) %reduce-scatter.22.cloned.1.call-update) | async-done | bytes 393232 | tf_op jit(solution)/shard_map/reduce_scatter | solution.py:363
  1559.0 162.3 %reduce-scatter.24.cloned.1.call-done = f32[32,3072]{1,0:T(8,128)} async-done(((f32[1024,3072]{1,0:T(8,128)}), f32[32,3072]{1,0:T(8,128)}) %reduce-scatter.24.cloned.1.call-update) | async-done | bytes 393232 | tf_op jit(solution)/shard_map/reduce_scatter | solution.py:364
  1721.3 161.4 %reduce-scatter.26.cloned.1.call-done = f32[96,1024]{1,0:T(8,128)} async-done(((f32[3072,1024]{1,0:T(8,128)}), f32[96,1024]{1,0:T(8,128)}) %reduce-scatter.26.cloned.1.call-update) | async-done | bytes 393232 | tf_op jit(solution)/shard_map/reduce_scatter | solution.py:365
  1882.6 142.6 %reduce-scatter.16.cloned.1.call-done = f32[32,1024]{1,0:T(8,128)} async-done(((f32[1024,1024]{1,0:T(8,128)}), f32[32,1024]{1,0:T(8,128)}) %reduce-scatter.16.cloned.1.call-update) | async-done | bytes 131088 | tf_op jit(solution)/shard_map/reduce_scatter | solution.py:355
  2025.3 143.7 %reduce-scatter.18.cloned.1.call-done = f32[32,1024]{1,0:T(8,128)} async-done(((f32[1024,1024]{1,0:T(8,128)}), f32[32,1024]{1,0:T(8,128)}) %reduce-scatter.18.cloned.1.call-update) | async-done | bytes 131088 | tf_op jit(solution)/shard_map/reduce_scatter | solution.py:356
  (760 shorter events, 341.8 us)
Async XLA Ops:
  7.2 63.4 %copy-start.2 = (bf16[1,2,128,1024]{3,2,1,0:T(8,128)(2,1)S(1)}, bf16[1,2,128,1024]{3,2,1,0:T(8,128)(2,1)}, u32[]{:S(2)}) copy-start(bf16[1,2,128,1024]{3,2,1,0:T(8,128)(2,1)} %param.27) | copy-start | bytes 1572868
  7.2 60.3 %all-gather.12.cloned.1.call-start = ((), (), s32[]{:S(2)}) async-start(), calls=%async_computation.9 | async-start | bytes 2162688 | tf_op jit(solution)/shard_map/all_gather | solution.py:142
  7.9 118.1 %all-gather.16.cloned.1.call-start = ((), (), s32[]{:S(2)}) async-start(), calls=%async_computation.11 | async-start | bytes 2162688 | tf_op jit(solution)/shard_map/all_gather | solution.py:141
  8.7 167.5 %all-gather.30.cloned.1.call-start = ((), (), s32[]{:S(2)}) async-start(), calls=%async_computation.18 | async-start | bytes 2359296 | tf_op jit(solution)/shard_map/all_gather | solution.py:183
  51.8 250.0 %copy-start.80 = (f32[1024]{0:T(1024)}, f32[1024]{0:T(1024)S(1)}, u32[]{:S(2)}) copy-start(f32[1024]{0:T(1024)S(1)} %convert_element_type.278) | copy-start | bytes 12292
  53.1 17.5 copy-start.114
  53.1 18.7 copy-start.112
  53.1 248.7 %copy-start.101 = (f32[128]{0:T(128)}, f32[128]{0:T(128)S(1)}, u32[]{:S(2)}) copy-start(f32[128]{0:T(128)S(1)} %fusion.165) | copy-start | bytes 1540
  70.5 156.0 %all-gather.14.cloned.1.call-start = ((), (), s32[]{:S(2)}) async-start(), calls=%async_computation.10 | async-start | bytes 2359296 | tf_op jit(solution)/shard_map/all_gather | solution.py:183
  70.6 227.5 %copy-start.95 = (f32[128]{0:T(128)}, f32[128]{0:T(128)S(1)}, u32[]{:S(2)}) copy-start(f32[128]{0:T(128)S(1)} %fusion.163) | copy-start | bytes 1540
  71.8 219.9 %all-gather.20.cloned.1.call-start = ((), (), s32[]{:S(2)}) async-start(), calls=%async_computation.13 | async-start | bytes 4325376 | tf_op jit(solution)/shard_map/all_gather | solution.py:140
  72.4 269.5 %all-gather.18.cloned.1.call-start = ((), (), s32[]{:S(2)}) async-start(), calls=%async_computation.12 | async-start | bytes 2359296 | tf_op jit(solution)/shard_map/all_gather | solution.py:182
  79.7 50.9 %copy-start.105 = (f32[128]{0:T(128)}, f32[128]{0:T(128)S(1)}, u32[]{:S(2)}) copy-start(f32[128]{0:T(128)S(1)} %convert_element_type.287) | copy-start | bytes 1540
  79.7 57.2 %copy-start.126 = (s32[128]{0:T(128)}, s32[128]{0:T(128)S(1)}, u32[]{:S(2)}) copy-start(s32[128]{0:T(128)S(1)} %iota_add_fusion) | copy-start | bytes 1540
  80.7 50.2 %copy-start.72 = (f32[128,128]{0,1:T(8,128)}, f32[128,128]{0,1:T(8,128)S(1)}, u32[]{:S(2)}) copy-start(f32[128,128]{0,1:T(8,128)S(1)} %pad_maximum_fusion.1) | copy-start | bytes 196612
  80.7 223.9 %copy-start.68 = (f32[128,128]{0,1:T(8,128)}, f32[128,128]{0,1:T(8,128)S(1)}, u32[]{:S(2)}) copy-start(f32[128,128]{0,1:T(8,128)S(1)} %pad_maximum_fusion) | copy-start | bytes 196612
  131.7 275.6 %all-gather.22.cloned.1.call-start = ((), (), s32[]{:S(2)}) async-start(), calls=%async_computation.14 | async-start | bytes 4325376 | tf_op jit(solution)/shard_map/all_gather | solution.py:143
  132.5 325.2 %all-gather.32.cloned.1.call-start = ((), (), s32[]{:S(2)}) async-start(), calls=%async_computation.19 | async-start | bytes 2359296 | tf_op jit(solution)/shard_map/all_gather | solution.py:182
  132.6 279.3 %copy-start.70 = (f32[128,128]{0,1:T(8,128)}, f32[128,128]{0,1:T(8,128)S(1)}, u32[]{:S(2)}) copy-start(f32[128,128]{0,1:T(8,128)S(1)} %pad_maximum_fusion.2) | copy-start | bytes 196612
  133.4 397.0 %all-gather.24.cloned.1.call-start = ((), (), s32[]{:S(2)}) async-start(), calls=%async_computation.15 | async-start | bytes 6488064 | tf_op jit(solution)/shard_map/all_gather | solution.py:149
  134.2 467.0 %all-gather.26.cloned.1.call-start = ((), (), s32[]{:S(2)}) async-start(), calls=%async_computation.16 | async-start | bytes 6488064 | tf_op jit(solution)/shard_map/all_gather | solution.py:150
  134.8 537.4 %all-gather.28.cloned.1.call-start = ((), (), s32[]{:S(2)}) async-start(), calls=%async_computation.17 | async-start | bytes 6488064 | tf_op jit(solution)/shard_map/all_gather | solution.py:151
  135.5 851.8 %reduce-scatter.28.cloned.1.call-start = ((), (), s32[]{:S(2)}) async-start(), calls=%async_computation.27 | async-start | bytes 4718592
  135.8 94.6 %copy-start.32 = (bf16[4,128,2,2,128]{1,4,3,2,0:T(8,128)(2,1)}, bf16[4,128,2,2,128]{1,4,3,2,0:T(8,128)(2,1)S(1)}, u32[]{:S(2)}) copy-start(bf16[4,128,2,2,128]{1,4,3,2,0:T(8,128)(2,1)S(1)} %fusion.185) | copy-start | bytes 1572868
  371.8 39.4 %copy-start.43 = (pred[128,1024]{0,1:T(8,128)(4,1)}, pred[128,1024]{0,1:T(8,128)(4,1)S(1)}, u32[]{:S(2)}) copy-start(pred[128,1024]{0,1:T(8,128)(4,1)S(1)} %get-tuple-element.1253) | copy-start | bytes 393220
  491.7 43.7 %copy-start.122 = (f32[128]{0:T(128)}, f32[128]{0:T(128)S(1)}, u32[]{:S(2)}) copy-start(f32[128]{0:T(128)S(1)} %get-tuple-element.646) | copy-start | bytes 1540
  491.8 109.4 %copy-start.19 = (bf16[128,1024]{1,0:T(8,128)(2,1)}, bf16[128,1024]{1,0:T(8,128)(2,1)S(1)}, u32[]{:S(2)}) copy-start(bf16[128,1024]{1,0:T(8,128)(2,1)S(1)} %multiply_convert_fusion.7) | copy-start | bytes 786436
  672.1 13.0 copy-start
  679.5 8.6 slice-start
  725.2 6.0 copy-start.45
  749.2 6.0 copy-start.45
  773.1 6.0 copy-start.45
  797.0 6.0 copy-start.45
  816.6 208.0 %reduce-scatter.30.cloned.1.call-start = ((), (), s32[]{:S(2)}) async-start(), calls=%async_computation.28 | async-start | bytes 4718592
  844.5 6.1 copy-start.42
  869.3 6.0 copy-start.42
  893.9 6.1 copy-start.42
  918.5 6.1 copy-start.42
  938.0 274.2 %reduce-scatter.14.cloned.1.call-start = ((), (), s32[]{:S(2)}) async-start(), calls=%async_computation.20 | async-start | bytes 8650752 | tf_op jit(solution)/shard_map/reduce_scatter | solution.py:354
  950.7 448.3 %reduce-scatter.20.cloned.1.call-start = ((), (), s32[]{:S(2)}) async-start(), calls=%async_computation.23 | async-start | bytes 8650752 | tf_op jit(solution)/shard_map/reduce_scatter | solution.py:357
  957.7 601.3 %reduce-scatter.22.cloned.1.call-start = ((), (), s32[]{:S(2)}) async-start(), calls=%async_computation.24 | async-start | bytes 12976128 | tf_op jit(solution)/shard_map/reduce_scatter | solution.py:363
  967.2 754.1 %reduce-scatter.24.cloned.1.call-start = ((), (), s32[]{:S(2)}) async-start(), calls=%async_computation.25 | async-start | bytes 12976128 | tf_op jit(solution)/shard_map/reduce_scatter | solution.py:364
  976.6 906.0 %reduce-scatter.26.cloned.1.call-start = ((), (), s32[]{:S(2)}) async-start(), calls=%async_computation.26 | async-start | bytes 12976128 | tf_op jit(solution)/shard_map/reduce_scatter | solution.py:365
  987.2 1038.1 %reduce-scatter.16.cloned.1.call-start = ((), (), s32[]{:S(2)}) async-start(), calls=%async_computation.21 | async-start | bytes 4325376 | tf_op jit(solution)/shard_map/reduce_scatter | solution.py:355
  990.4 40.4 %copy-start.75 = (f32[128,128]{0,1:T(8,128)S(1)}, f32[128,128]{0,1:T(8,128)}, u32[]{:S(2)}) copy-start(f32[128,128]{0,1:T(8,128)} %copy-done.72) | copy-start | bytes 196612
  1037.1 1131.9 %reduce-scatter.18.cloned.1.call-start = ((), (), s32[]{:S(2)}) async-start(), calls=%async_computation.22 | async-start | bytes 4325376 | tf_op jit(solution)/shard_map/reduce_scatter | solution.py:356
  1061.7 47.2 %copy-start.113 = (f32[128]{0:T(128)S(1)}, f32[128]{0:T(128)}, u32[]{:S(2)}) copy-start(f32[128]{0:T(128)} %copy-done.112) | copy-start | bytes 1540
  1061.7 47.2 %copy-start.115 = (f32[128]{0:T(128)S(1)}, f32[128]{0:T(128)}, u32[]{:S(2)}) copy-start(f32[128]{0:T(128)} %copy-done.114) | copy-start | bytes 1540
  (128 other events, 238.9 us)
Sparse Core Ops, SparseCore 0:
  11.0 56.4 all-gather.11
  70.4 55.5 all-gather.15
  128.7 47.4 all-gather.29
  178.7 47.7 all-gather.13
  229.5 62.1 all-gather.19
  294.2 47.7 all-gather.17
  345.1 62.1 all-gather.21
  409.9 47.7 all-gather.31
  460.6 69.7 all-gather.23
  533.1 67.9 all-gather.25
  604.1 67.9 all-gather.27
  816.7 86.4 reduce-scatter.27
  938.1 86.3 reduce-scatter.29
  1027.3 184.8 reduce-scatter.13
  1214.9 184.0 reduce-scatter.19
  1405.5 153.4 reduce-scatter.21
  1566.4 154.7 reduce-scatter.23
  1727.7 154.8 reduce-scatter.25
  1885.6 139.6 reduce-scatter.15
  2028.0 140.8 reduce-scatter.17
where the time goes:
time: 2190 us; the launch traced here: 2180 us
  waiting for transfers between devices  1590 us (73%)
  matrix products  228 us (10%)
  local copies, waits for them, and re-layouts  183 us (8%)
  blocking collectives  82.8 us (4%)
  other arithmetic  41 us (2%)
  loops' own time  38.4 us (2%)
    reduce_scatter x1, waiting for transfers between devices, shards(): lax.psum_scatter(sums[3], ('dp', 'seq'), scatter_dimension=0, tiled=True)  187 us
    reduce_scatter x1, waiting for transfers between devices, shards(): lax.psum_scatter(sums[5], ('dp', 'seq'), scatter_dimension=0, tiled=True)  162 us
    reduce_scatter x1, waiting for transfers between devices, shards(): lax.psum_scatter(sums[6], ('dp', 'seq'), scatter_dimension=0, tiled=True)  161 us
    reduce_scatter x1, waiting for transfers between devices, shards(): lax.psum_scatter(sums[4], ('dp', 'seq'), scatter_dimension=0, tiled=True)  160 us
    reduce_scatter x1, waiting for transfers between devices, shards(): lax.psum_scatter(sums[2], ('dp', 'seq'), scatter_dimension=0, tiled=True)  144 us
    reduce_scatter x1, waiting for transfers between devices, shards(): lax.psum_scatter(sums[1], ('dp', 'seq'), scatter_dimension=0, tiled=True)  143 us
    reduce_scatter x1, waiting for transfers between devices, shards(): lax.psum_scatter(sums[0], ('dp', 'seq'), scatter_dimension=0, tiled=True)  102 us
    unnamed x2, blocking collectives  82.8 us
  transfers between devices with their start and end apart: 20, of which 19 were waited for; matrix products, arithmetic and copies ran while one was open for 14% of the time, Pallas kernels for 0%

commit v1 on v0

--- a/solution.py
+++ b/solution.py
@@ -1,6 +1,10 @@
+import functools
+
 import jax
 import jax.numpy as jnp
 from jax import lax
+from jax.experimental import pallas as pl
+from jax.experimental.pallas import tpu as pltpu
 from jax.sharding import PartitionSpec as P
 
 D = 1024
@@ -91,7 +95,7 @@
     )
 
 
-def shards(
+def general_shards(
     tokens,
     cotangent,
     node_lengths,
@@ -384,9 +388,809 @@
     )
 
 
+MESH = pl.DeviceIdType.MESH
+NDP = 4
+NSEQ = 8
+BLOCKED = -65536.0
+
+
+def spot():
+    d = lax.axis_index("dp")
+    s = lax.axis_index("seq")
+    z, y = s // 2, s % 2
+    return d, s, z + y * (7 - 2 * z)
+
+
+def seq_at(position):
+    half = position // 4
+    z = position + half * (7 - 2 * position)
+    return 2 * z + half
+
+
+def greet_all(d, s):
+    barrier = pltpu.get_barrier_semaphore()
+    me = d * NSEQ + s
+
+    def signal(i, carry):
+        other = (me + i) % (NDP * NSEQ)
+        pl.semaphore_signal(
+            barrier, inc=1, device_id=(other // NSEQ, other % NSEQ), device_id_type=MESH
+        )
+        return carry
+
+    lax.fori_loop(1, NDP * NSEQ, signal, 0)
+    pl.semaphore_wait(barrier, NDP * NSEQ - 1)
+
+
+def greet_dp(d, s):
+    barrier = pltpu.get_barrier_semaphore()
+    for i in range(1, NDP):
+        pl.semaphore_signal(barrier, inc=1, device_id=((d + i) % NDP, s), device_id_type=MESH)
+    pl.semaphore_wait(barrier, NDP - 1)
+
+
+def remote(src, dst, send, recv, d, s):
+    return pltpu.make_async_remote_copy(
+        src_ref=src, dst_ref=dst, send_sem=send, recv_sem=recv, device_id=(d, s), device_id_type=MESH
+    )
+
+
+def ring_halves(ref, kind, j):
+    if kind == "cols":
+        return ref.at[pl.ds(0, 2), j], ref.at[pl.ds(2, 2), j]
+    rows = ref.shape[1] // 2
+    return ref.at[j, pl.ds(0, rows)], ref.at[j, pl.ds(rows, rows)]
+
+
+def spread_dp(out, d, s, ssem, rsem):
+    x, c = d // 2, d % 2
+    sib, far = 2 * x + 1 - c, 2 * (1 - x) + c
+    far_sib = 2 * (1 - x) + 1 - c
+    own = out.at[:, d]
+    to_far = remote(own, own, ssem.at[0], rsem.at[0], far, s)
+    to_sib = remote(own, own, ssem.at[1], rsem.at[1], sib, s)
+    to_far.start()
+    to_sib.start()
+    block = out.at[:, far]
+    remote(block, block, ssem.at[0], rsem.at[0], far, s).wait_recv()
+    forward = remote(block, block, ssem.at[2], rsem.at[2], sib, s)
+    forward.start()
+    block = out.at[:, sib]
+    remote(block, block, ssem.at[1], rsem.at[1], sib, s).wait_recv()
+    block = out.at[:, far_sib]
+    remote(block, block, ssem.at[2], rsem.at[2], sib, s).wait_recv()
+    to_far.wait_send()
+    to_sib.wait_send()
+    forward.wait_send()
+
+
+def gather_dp_sum(part, near, sent, got, d, s, ssem, rsem, finish):
+    x, c = d // 2, d % 2
+    sib, far = 2 * x + 1 - c, 2 * (1 - x) + c
+    first = remote(part.at[:, 2 * (1 - x) + 1 - c], near.at[0], ssem.at[0], rsem.at[0], sib, s)
+    second = remote(part.at[:, 2 * x + 1 - c], near.at[1], ssem.at[1], rsem.at[1], sib, s)
+    first.start()
+    second.start()
+    first.wait_recv()
+
+    def join(i, carry):
+        sent[i] = (part[i, far].astype(jnp.float32) + near[0, i].astype(jnp.float32)).astype(
+            jnp.bfloat16
+        )
+        return carry
+
+    lax.fori_loop(0, NSEQ, join, 0)
+    across_x = remote(sent, got, ssem.at[2], rsem.at[2], far, s)
+    across_x.start()
+    second.wait_recv()
+    across_x.wait_recv()
+
+    def close(i, carry):
+        rows = part[i, d].astype(jnp.float32) + near[1, i].astype(jnp.float32)
+        finish(i, rows + got[i].astype(jnp.float32))
+        return carry
+
+    lax.fori_loop(0, NSEQ, close, 0)
+    first.wait_send()
+    second.wait_send()
+    across_x.wait_send()
+
+
+def deliver_kernel(
+    tok, cot, small, wq, wk, wv, wo, wg, wu, wd, tree, tree_cot, smalls, wa, wb, wc, we,
+    loc, s_small, r_small, s_row, r_row, s_col, r_col, s_tok, r_tok, s_ring, r_ring, s_dp, r_dp,
+):
+    d, s, p = spot()
+    greet_all(d, s)
+    own_small = pltpu.make_async_copy(small, smalls.at[d, s], loc.at[0])
+    own_small.start()
+    own_small.wait()
+    pending = []
+    for i in range(1, NDP):
+        q = (d + i) % NDP
+        cp = remote(smalls.at[d, s], smalls.at[d, s], s_small.at[i], r_small.at[i], q, s)
+        cp.start()
+        pending.append(cp)
+    pieces = (
+        (wq, wa, 512, 0), (wk, wa, 256, 512), (wv, wa, 256, 768), (wg, wc, 768, 0), (wu, wc, 768, 768)
+    )
+    waits = []
+    for n, (src, dst, width, at) in enumerate(pieces):
+        cp = pltpu.make_async_copy(
+            src.at[:, pl.ds(pl.multiple_of(d * width, 128), width)],
+            dst.at[d, s, :, pl.ds(at, width)],
+            loc.at[1 + n],
+        )
+        cp.start()
+        waits.append(cp)
+        for i in range(1, NDP):
+            q = (d + i) % NDP
+            cp = remote(
+                src.at[:, pl.ds(pl.multiple_of(q * width, 128), width)],
+                dst.at[d, s, :, pl.ds(at, width)],
+                s_col.at[n, i],
+                r_col.at[n, i],
+                q,
+                s,
+            )
+            cp.start()
+            pending.append(cp)
+    for n, (src, dst) in enumerate(((wo, wb), (wd, we))):
+        cp = pltpu.make_async_copy(src, dst.at[s], loc.at[6 + n])
+        cp.start()
+        waits.append(cp)
+    for n, (src, dst) in enumerate(((tok, tree), (cot, tree_cot))):
+        for m in range(MICRO):
+            for i in range(NDP):
+                q = (d + i) % NDP
+                target = MICRO * d + m
+                piece = src.at[m, pl.ds(pl.multiple_of(q * 32, 32), 32)]
+                place = dst.at[s, q]
+                if i == 0:
+
+                    @pl.when(target == s)
+                    def _():
+                        pltpu.make_async_copy(piece, place, r_tok.at[n]).start()
+
+                    @pl.when(target != s)
+                    def _():
+                        remote(piece, place, s_tok.at[n, m, i], r_tok.at[n], q, target).start()
+                else:
+                    cp = remote(piece, place, s_tok.at[n, m, i], r_tok.at[n], q, target)
+                    cp.start()
+                    pending.append(cp)
+    for cp in waits:
+        cp.wait()
+    for n, (src, dst, width, at) in enumerate(pieces):
+        for i in range(1, NDP):
+            q = (d + NDP - i) % NDP
+            place = dst.at[q, s, :, pl.ds(at, width)]
+            remote(place, place, s_col.at[n, i], r_col.at[n, i], q, s).wait_recv()
+    up, down = seq_at((p + 1) % NSEQ), seq_at((p + 7) % NSEQ)
+    ring = ((wa, "cols"), (wb, "rows"), (wc, "cols"), (we, "rows"))
+
+    def pass_on(k, carry):
+        up_own, down_own = seq_at((p + NSEQ - k) % NSEQ), seq_at((p + k) % NSEQ)
+        for n, (ref, kind) in enumerate(ring):
+            rising = ring_halves(ref, kind, up_own)[0]
+            falling = ring_halves(ref, kind, down_own)[1]
+
+            @pl.when(k > 0)
+            def _():
+                remote(rising, rising, s_ring.at[n, 0, k - 1], r_ring.at[n, 0, k - 1], up, 0).wait_recv()
+
+            remote(rising, rising, s_ring.at[n, 0, k], r_ring.at[n, 0, k], d, up).start()
+
+            @pl.when(k > 0)
+            def _():
+                remote(falling, falling, s_ring.at[n, 1, k - 1], r_ring.at[n, 1, k - 1], down, 0).wait_recv()
+
+            remote(falling, falling, s_ring.at[n, 1, k], r_ring.at[n, 1, k], d, down).start()
+        return carry
+
+    for n, dst in enumerate((tree, tree_cot)):
+        everything = dst.at[:, d]
+        pltpu.make_async_copy(everything, everything, r_tok.at[n]).wait()
+    lax.fori_loop(0, 2, pass_on, 0)
+    for n, dst in enumerate((tree, tree_cot)):
+        spread_dp(dst, d, s, s_dp.at[n], r_dp.at[n])
+    lax.fori_loop(2, NSEQ - 1, pass_on, 0)
+    for i in range(1, NDP):
+        place = smalls.at[(d + NDP - i) % NDP, s]
+        remote(place, place, s_small.at[i], r_small.at[i], d, s).wait_recv()
+    for i in range(1, NSEQ):
+        j = (s + i) % NSEQ
+        place = smalls.at[:, s]
+        cp = remote(place, place, s_small.at[NDP + i], r_small.at[NDP + i], d, j)
+        cp.start()
+        pending.append(cp)
+    for i in range(1, NSEQ):
+        place = smalls.at[:, (s + NSEQ - i) % NSEQ]
+        remote(place, place, s_small.at[NDP + i], r_small.at[NDP + i], d, s).wait_recv()
+    for n, (ref, kind) in enumerate(ring):
+        last_up = ring_halves(ref, kind, seq_at((p + 1) % NSEQ))[0]
+        last_down = ring_halves(ref, kind, seq_at((p + 7) % NSEQ))[1]
+        remote(last_up, last_up, s_ring.at[n, 0, 6], r_ring.at[n, 0, 6], d, up).wait_recv()
+        remote(last_down, last_down, s_ring.at[n, 1, 6], r_ring.at[n, 1, 6], d, down).wait_recv()
+
+    def sent_ring(k, carry):
+        for n, (ref, kind) in enumerate(ring):
+            rising, falling = ring_halves(ref, kind, s)
+            remote(rising, rising, s_ring.at[n, 0, k], r_ring.at[n, 0, k], d, up).wait_send()
+            remote(falling, falling, s_ring.at[n, 1, k], r_ring.at[n, 1, k], d, down).wait_send()
+        return carry
+
+    lax.fori_loop(0, NSEQ - 1, sent_ring, 0)
+    for cp in pending:
+        cp.wait_send()
+    for n, (src, dst) in enumerate(((tok, tree), (cot, tree_cot))):
+        for m in range(MICRO):
+
+            @pl.when(MICRO * d + m != s)
+            def _():
+                place = dst.at[s, d]
+                remote(place, place, s_tok.at[n, m, 0], r_tok.at[n], d, s).wait_send()
+
+
+def deliver(tok, cot, small, wq, wk, wv, wo, wg, wu, wd):
+    bf, f32 = jnp.bfloat16, jnp.float32
+    dma = pltpu.SemaphoreType.DMA
+    shape = jax.ShapeDtypeStruct
+    anywhere = pl.BlockSpec(memory_space=pl.ANY)
+    return pl.pallas_call(
+        deliver_kernel,
+        out_shape=(
+            shape((NSEQ, NDP, 32, D), bf),
+            shape((NSEQ, NDP, 32, D), bf),
+            shape((NDP, NSEQ, 8, 128), f32),
+            shape((NDP, NSEQ, 32, 1024), bf),
+            shape((NSEQ, 64, D), bf),
+            shape((NDP, NSEQ, 32, 1536), bf),
+            shape((NSEQ, 96, D), bf),
+        ),
+        in_specs=[anywhere] * 10,
+        out_specs=[anywhere] * 7,
+        scratch_shapes=[
+            dma((8,)),
+            dma((12,)), dma((12,)),
+            dma((1,)), dma((1,)),
+            dma((5, NDP)), dma((5, NDP)),
+            dma((2, MICRO, NDP)), dma((2,)),
+            dma((4, 2, 7)), dma((4, 2, 7)),
+            dma((2, 3)), dma((2, 3)),
+        ],
+        compiler_params=pltpu.CompilerParams(collective_id=1, has_side_effects=True),
+        name="deliver",
+    )(tok, cot, small, wq, wk, wv, wo, wg, wu, wd)
+
+
+def middle_kernel(part, tree, gain, middle, normed, rows_in, near, sent, got, loc, ssem, rsem, s_dp, r_dp):
+    d, s, _ = spot()
+    greet_dp(d, s)
+    own = pltpu.make_async_copy(tree.at[:, d], rows_in, loc.at[0])
+    own.start()
+    own.wait()
+
+    def finish(i, rows):
+        rows = rows + rows_in[i].astype(jnp.float32)
+        middle[i] = rows
+        scale = lax.rsqrt(jnp.mean(rows * rows, axis=-1, keepdims=True) + EPSILON)
+        normed[i, d] = (rows * scale * gain[...]).astype(jnp.bfloat16)
+
+    gather_dp_sum(part, near, sent, got, d, s, ssem, rsem, finish)
+    spread_dp(normed, d, s, s_dp, r_dp)
+
+
+def sum_scratch():
+    bf = jnp.bfloat16
+    return [
+        pltpu.VMEM((2, NSEQ, 32, D), bf),
+        pltpu.VMEM((NSEQ, 32, D), bf),
+        pltpu.VMEM((NSEQ, 32, D), bf),
+    ]
+
+
+def middle_stage(part, tree, gain):
+    bf, f32 = jnp.bfloat16, jnp.float32
+    dma = pltpu.SemaphoreType.DMA
+    shape = jax.ShapeDtypeStruct
+    anywhere = pl.BlockSpec(memory_space=pl.ANY)
+    here = pl.BlockSpec(memory_space=pltpu.VMEM)
+    return pl.pallas_call(
+        middle_kernel,
+        out_shape=(shape((NSEQ, 32, D), f32), shape((NSEQ, NDP, 32, D), bf)),
+        in_specs=[here, anywhere, here],
+        out_specs=[here, here],
+        scratch_shapes=[pltpu.VMEM((NSEQ, 32, D), bf)]
+        + sum_scratch()
+        + [dma((1,)), dma((3,)), dma((3,)), dma((3,)), dma((3,))],
+        compiler_params=pltpu.CompilerParams(
+            collective_id=2, has_side_effects=True, vmem_limit_bytes=40 << 20
+        ),
+        name="middle",
+    )(part, tree, gain)
+
+
+def turn_kernel(
+    part, part_out, tree_cot, middle, gain, d_middle, d_low, outs, d_gain,
+    cot_rows, near, sent, got, near_out, sent_out, got_out,
+    loc, ssem, rsem, s_dp, r_dp, s_out, r_out,
+):
+    d, s, _ = spot()
+    greet_dp(d, s)
+    own = pltpu.make_async_copy(tree_cot.at[:, d], cot_rows, loc.at[0])
+    own.start()
+    own.wait()
+    d_gain[...] = jnp.zeros_like(d_gain)
+
+    def finish(i, rows):
+        mid = middle[i]
+        scale = lax.rsqrt(jnp.mean(mid * mid, axis=-1, keepdims=True) + EPSILON)
+        unit = mid * scale
+        lifted = gain[...] * rows
+        d_gain[...] += jnp.sum(rows * unit, axis=0, keepdims=True)
+        d_mid = cot_rows[i].astype(jnp.float32) + scale * (
+            lifted - unit * jnp.mean(unit * lifted, axis=-1, keepdims=True)
+        )
+        d_middle[i] = d_mid
+        d_low[i, d] = d_mid.astype(jnp.bfloat16)
+
+    gather_dp_sum(part, near, sent, got, d, s, ssem, rsem, finish)
+    spread_dp(d_low, d, s, s_dp, r_dp)
+
+    def finish_out(i, rows):
+        outs[i] = (middle[i] + rows).astype(jnp.bfloat16)
+
+    gather_dp_sum(part_out, near_out, sent_out, got_out, d, s, s_out, r_out, finish_out)
+
+
+def turn_stage(part, part_out, tree_cot, middle, gain):
+    bf, f32 = jnp.bfloat16, jnp.float32
+    dma = pltpu.SemaphoreType.DMA
+    shape = jax.ShapeDtypeStruct
+    anywhere = pl.BlockSpec(memory_space=pl.ANY)
+    here = pl.BlockSpec(memory_space=pltpu.VMEM)
+    return pl.pallas_call(
+        turn_kernel,
+        out_shape=(
+            shape((NSEQ, 32, D), f32),
+            shape((NSEQ, NDP, 32, D), bf),
+            shape((NSEQ, 32, D), bf),
+            shape((1, D), f32),
+        ),
+        in_specs=[here, here, anywhere, here, here],
+        out_specs=[here] * 4,
+        scratch_shapes=[pltpu.VMEM((NSEQ, 32, D), bf)]
+        + sum_scratch()
+        + sum_scratch()
+        + [dma((1,)), dma((3,)), dma((3,)), dma((3,)), dma((3,)), dma((3,)), dma((3,))],
+        compiler_params=pltpu.CompilerParams(
+            collective_id=3, has_side_effects=True, vmem_limit_bytes=40 << 20
+        ),
+        name="turn",
+    )(part, part_out, tree_cot, middle, gain)
+
+
+def return_kernel(
+    part, tree, d_middle, gain, outs, pack_in, ga, gb, gc, ge,
+    out_rows, grad_rows, pack_out, res_a, res_b, res_c, res_e,
+    rows_in, near, sent, got, grad_low, hop_a, hop_b, hop_c, hop_e, fin_a, fin_c,
+    pack_dp, pack_seq,
+    loc, ssem, rsem, s_back, r_back, s_ring, r_ring, s_col, r_col, s_pack, r_pack,
+):
+    d, s, p = spot()
+    greet_all(d, s)
+    bf, f32 = jnp.bfloat16, jnp.float32
+    own = pltpu.make_async_copy(tree.at[:, d], rows_in, loc.at[0])
+    own.start()
+    up, down = seq_at((p + 1) % NSEQ), seq_at((p + 7) % NSEQ)
+    ring = ((ga, hop_a, "cols"), (gb, hop_b, "rows"), (gc, hop_c, "cols"), (ge, hop_e, "rows"))
+    owner = s // MICRO
+    slot = s % MICRO
+
+    def give(src, dst, n):
+        def one(j, carry):
+            piece = src.at[j]
+            place = dst.at[slot, pl.ds(pl.multiple_of(d * 32, 32), 32)]
+            same = (owner == d) & (j == s)
+
+            @pl.when(same)
+            def _():
+                pltpu.make_async_copy(piece, place, r_back.at[n]).start()
+
+            @pl.when(jnp.logical_not(same))
+            def _():
+                remote(piece, place, s_back.at[n, j], r_back.at[n], owner, j).start()
+
+            return carry
+
+        lax.fori_loop(0, NSEQ, one, 0)
+
+    give(outs, out_rows, 0)
+
+    def ring_step(k, carry):
+        up_to, down_to = seq_at((p + 7 - k) % NSEQ), seq_at((p + 1 + k) % NSEQ)
+        for n, (ref, hop, kind) in enumerate(ring):
+            for way, (block, peer) in enumerate(((up_to, up), (down_to, down))):
+                mine = ring_halves(ref, kind, block)[way]
+
+                @pl.when(k == 0)
+                def _():
+                    remote(mine, hop.at[way, 0], s_ring.at[n, way, 0], r_ring.at[n, way, 0], d, peer).start()
+
+                @pl.when(k > 0)
+                def _():
+                    here = hop.at[way, k - 1]
+                    remote(here, here, s_ring.at[n, way, k - 1], r_ring.at[n, way, k - 1], d, peer).wait_recv()
+                    here[...] = (here[...].astype(f32) + mine[...].astype(f32)).astype(bf)
+                    remote(here, hop.at[way, k], s_ring.at[n, way, k], r_ring.at[n, way, k], d, peer).start()
+
+        return carry
+
+    lax.fori_loop(0, 2, ring_step, 0)
+    own.wait()
+    d_gain = jnp.zeros((1, D), f32)
+    pack_dp[d] = pack_in[...]
+
+    def finish(i, rows):
+        low = rows_in[i].astype(f32)
+        scale = lax.rsqrt(jnp.mean(low * low, axis=-1, keepdims=True) + EPSILON)
+        unit = low * scale
+        lifted = gain[...] * rows
+        term = jnp.sum(rows * unit, axis=0, keepdims=True)
+        for j in range(8):
+            pack_dp[d, pl.ds(j, 1)] += term[:, 128 * j : 128 * (j + 1)]
+        grad = d_middle[i] + scale * (
+            lifted - unit * jnp.mean(unit * lifted, axis=-1, keepdims=True)
+        )
+        grad_low[i] = grad.astype(bf)
+
+    gather_dp_sum(part, near, sent, got, d, s, ssem, rsem, finish)
+    give(grad_low, grad_rows, 1)
+    pending = []
+    for i in range(1, NDP):
+        q = (d + i) % NDP
+        cp = remote(pack_dp.at[d], pack_dp.at[d], s_pack.at[i], r_pack.at[i], q, s)
+        cp.start()
+        pending.append(cp)
+    for i in range(1, NDP):
+        place = pack_dp.at[(d + NDP - i) % NDP]
+        remote(place, place, s_pack.at[i], r_pack.at[i], d, s).wait_recv()
+    pack_seq[s] = (pack_dp[0] + pack_dp[1]) + (pack_dp[2] + pack_dp[3])
+    for i in range(1, NSEQ):
+        cp = remote(pack_seq.at[s], pack_seq.at[s], s_pack.at[NDP + i], r_pack.at[NDP + i], d, (s + i) % NSEQ)
+        cp.start()
+        pending.append(cp)
+    lax.fori_loop(2, NSEQ - 1, ring_step, 0)
+    for n, (ref, hop, kind) in enumerate(ring):
+        halves = ring_halves(ref, kind, s)
+        for way, peer in enumerate((up, down)):
+            here = hop.at[way, 6]
+            remote(here, here, s_ring.at[n, way, 6], r_ring.at[n, way, 6], d, peer).wait_recv()
+            total = here[...].astype(f32) + halves[way][...].astype(f32)
+            if n == 0:
+                fin_a[pl.ds(2 * way, 2)] = total.astype(bf)
+            elif n == 2:
+                fin_c[pl.ds(2 * way, 2)] = total.astype(bf)
+            else:
+                res = res_b if n == 1 else res_e
+                rows = total.shape[0]
+                res[pl.ds(way * rows, rows)] = total
+    for n, (fin, res) in enumerate(((fin_a, res_a), (fin_c, res_c))):
+        cp = pltpu.make_async_copy(fin.at[d], res.at[d], loc.at[1 + n])
+        cp.start()
+        cp.wait()
+        for i in range(1, NDP):
+            q = (d + i) % NDP
+            cp = remote(fin.at[q], res.at[d], s_col.at[n, i], r_col.at[n, i], q, s)
+            cp.start()
+            pending.append(cp)
+    for i in range(1, NSEQ):
+        place = pack_seq.at[(s + NSEQ - i) % NSEQ]
+        remote(place, place, s_pack.at[NDP + i], r_pack.at[NDP + i], d, s).wait_recv()
+    total = pack_seq[0]
+    for j in range(1, NSEQ):
+        total = total + pack_seq[j]
+    pack_out[...] = total
+    for n, res in enumerate((res_a, res_c)):
+        for i in range(1, NDP):
+            place = res.at[(d + NDP - i) % NDP]
+            remote(place, place, s_col.at[n, i], r_col.at[n, i], d, s).wait_recv()
+    for n, dst in enumerate((out_rows, grad_rows)):
+        pltpu.make_async_copy(dst, dst, r_back.at[n]).wait()
+
+        def sent_back(j, carry):
+            same = (owner == d) & (j == s)
+
+            @pl.when(jnp.logical_not(same))
+            def _():
+                place = grad_low.at[j]
+                remote(place, place, s_back.at[n, j], r_back.at[n], owner, j).wait_send()
+
+            return carry
+
+        lax.fori_loop(0, NSEQ, sent_back, 0)
+
+    def sent_ring(k, carry):
+        for n, (ref, hop, kind) in enumerate(ring):
+            for way, peer in enumerate((up, down)):
+                here = hop.at[way, k]
+                remote(here, here, s_ring.at[n, way, k], r_ring.at[n, way, k], d, peer).wait_send()
+        return carry
+
+    lax.fori_loop(0, NSEQ - 1, sent_ring, 0)
+    for cp in pending:
+        cp.wait_send()
+
+
+def return_stage(part, tree, d_middle, gain, outs, pack_in, ga, gb, gc, ge):
+    bf, f32 = jnp.bfloat16, jnp.float32
+    dma = pltpu.SemaphoreType.DMA
+    shape = jax.ShapeDtypeStruct
+    vmem = pltpu.VMEM
+    anywhere = pl.BlockSpec(memory_space=pl.ANY)
+    here = pl.BlockSpec(memory_space=pltpu.VMEM)
+    return pl.pallas_call(
+        return_kernel,
+        out_shape=(
+            shape((MICRO, 128, D), bf),
+            shape((MICRO, 128, D), bf),
+            shape((24, 128), f32),
+            shape((NDP, 32, 1024), bf),
+            shape((64, D), f32),
+            shape((NDP, 32, 1536), bf),
+            shape((96, D), f32),
+        ),
+        in_specs=[here, anywhere] + [here] * 8,
+        out_specs=[here] * 7,
+        scratch_shapes=[vmem((NSEQ, 32, D), bf)]
+        + sum_scratch()
+        + [
+            vmem((NSEQ, 32, D), bf),
+            vmem((2, 7, 2, 32, 1024), bf),
+            vmem((2, 7, 32, D), bf),
+            vmem((2, 7, 2, 32, 1536), bf),
+            vmem((2, 7, 48, D), bf),
+            vmem((NDP, 32, 1024), bf),
+            vmem((NDP, 32, 1536), bf),
+            vmem((NDP, 24, 128), f32),
+            vmem((NSEQ, 24, 128), f32),
+            dma((3,)), dma((3,)), dma((3,)),
+            dma((2, NSEQ)), dma((2,)),
+            dma((4, 2, 7)), dma((4, 2, 7)),
+            dma((2, NDP)), dma((2, NDP)),
+            dma((12,)), dma((12,)),
+        ],
+        compiler_params=pltpu.CompilerParams(
+            collective_id=4, has_side_effects=True, vmem_limit_bytes=56 << 20
+        ),
+        name="give_back",
+    )(part, tree, d_middle, gain, outs, pack_in, ga, gb, gc, ge)
+
+
+QB = 256
+
+
+def attend_kernel(q_ref, k_ref, v_ref, o_ref, lse_ref):
+    length = q_ref.shape[0]
+    scale = HEAD_DIM ** (-0.5)
+    row = lax.broadcasted_iota(jnp.int32, (QB, QB), 0)
+    col = lax.broadcasted_iota(jnp.int32, (QB, QB), 1)
+    for b in range(length // QB):
+        n = (b + 1) * QB
+        score = against(q_ref[pl.ds(b * QB, QB)], k_ref[pl.ds(0, n)]) * scale
+        diag = jnp.where(col <= row, score[:, n - QB :], NEGATIVE)
+        score = diag if b == 0 else jnp.concatenate([score[:, : n - QB], diag], axis=1)
+        weight = jnp.exp(score)
+        total = jnp.sum(weight, axis=-1, keepdims=True)
+        mixed = product(weight.astype(jnp.bfloat16), v_ref[pl.ds(0, n)])
+        o_ref[pl.ds(b * QB, QB)] = (mixed / total).astype(jnp.bfloat16)
+        lse_ref[pl.ds(b * QB, QB)] = jnp.log(total)
+
+
+def attend(q_aug, k_aug, value):
+    heads, length = q_aug.shape[0], q_aug.shape[1]
+    shape = jax.ShapeDtypeStruct
+    return pl.pallas_call(
+        attend_kernel,
+        grid=(heads,),
+        out_shape=(
+            shape((length, heads * HEAD_DIM), jnp.bfloat16),
+            shape((heads, length, 1), jnp.float32),
+        ),
+        in_specs=[
+            pl.BlockSpec((None, length, 256), lambda h: (h, 0, 0)),
+            pl.BlockSpec((None, length, 256), lambda h: (h // 2, 0, 0)),
+            pl.BlockSpec((length, HEAD_DIM), lambda h: (0, h // 2)),
+        ],
+        out_specs=[
+            pl.BlockSpec((length, HEAD_DIM), lambda h: (0, h)),
+            pl.BlockSpec((None, length, 1), lambda h: (h, 0, 0)),
+        ],
+        compiler_params=pltpu.CompilerParams(vmem_limit_bytes=50 << 20),
+        name="attend",
+    )(q_aug, k_aug, value)
+
+
+def attend_back_kernel(q_ref, k_ref, v_ref, do_ref, lse_ref, dq_ref, dk_ref, dv_ref):
+    length = q_ref.shape[0]
+    scale = HEAD_DIM ** (-0.5)
+    row = lax.broadcasted_iota(jnp.int32, (QB, QB), 0)
+    col = lax.broadcasted_iota(jnp.int32, (QB, QB), 1)
+
+    @pl.when(pl.program_id(0) % 2 == 0)
+    def _():
+        dk_ref[...] = jnp.zeros_like(dk_ref)
+        dv_ref[...] = jnp.zeros_like(dv_ref)
+
+    for b in range(length // QB):
+        n = (b + 1) * QB
+        here, keys = pl.ds(b * QB, QB), pl.ds(0, n)
+        score = against(q_ref[here], k_ref[keys]) * scale
+        diag = jnp.where(col <= row, score[:, n - QB :], NEGATIVE)
+        score = diag if b == 0 else jnp.concatenate([score[:, : n - QB], diag], axis=1)
+        prob = jnp.exp(score - lse_ref[here])
+        d_prob = against(do_ref[here], v_ref[keys])
+        delta = jnp.sum(prob * d_prob, axis=-1, keepdims=True)
+        d_raw = (prob * (d_prob - delta) * scale).astype(jnp.bfloat16)
+        dq_ref[here] = product(d_raw, k_ref[keys, pl.ds(0, HEAD_DIM)])
+        dk_ref[keys] += across(d_raw, q_ref[here, pl.ds(0, HEAD_DIM)])
+        dv_ref[keys] += across(prob.astype(jnp.bfloat16), do_ref[here])
+
+
+def attend_back(q_aug, k_aug, value, d_att, lse):
+    heads, length = q_aug.shape[0], q_aug.shape[1]
+    shape = jax.ShapeDtypeStruct
+    return pl.pallas_call(
+        attend_back_kernel,
+        grid=(heads,),
+        out_shape=(
+            shape((length, heads * HEAD_DIM), jnp.float32),
+            shape((length, heads // 2 * HEAD_DIM), jnp.float32),
+            shape((length, heads // 2 * HEAD_DIM), jnp.float32),
+        ),
+        in_specs=[
+            pl.BlockSpec((None, length, 256), lambda h: (h, 0, 0)),
+            pl.BlockSpec((None, length, 256), lambda h: (h // 2, 0, 0)),
+            pl.BlockSpec((length, HEAD_DIM), lambda h: (0, h // 2)),
+            pl.BlockSpec((length, HEAD_DIM), lambda h: (0, h)),
+            pl.BlockSpec((None, length, 1), lambda h: (h, 0, 0)),
+        ],
+        out_specs=[
+            pl.BlockSpec((length, HEAD_DIM), lambda h: (0, h)),
+            pl.BlockSpec((length, HEAD_DIM), lambda h: (0, h // 2)),
+            pl.BlockSpec((length, HEAD_DIM), lambda h: (0, h // 2)),
+        ],
+        compiler_params=pltpu.CompilerParams(vmem_limit_bytes=50 << 20),
+        name="attend_back",
+    )(q_aug, k_aug, value, d_att, lse)
+
+
+def tree_shards(
+    tokens, cotangent, node_lengths, parents, w_query, w_key, w_value, w_output, w_gate, w_up, w_down,
+    attn_gain, ffn_gain, query_gain, key_gain,
+):
+    f32, bf = jnp.float32, jnp.bfloat16
+    d, s = lax.axis_index("dp"), lax.axis_index("seq")
+    length = NSEQ * tokens.shape[2]
+    heads, kv_heads = HEADS // NDP, KV_HEADS // NDP
+    nodes = node_lengths.shape[2]
+    gains = jnp.concatenate([attn_gain, ffn_gain, query_gain, key_gain]).astype(f32)
+    small = jnp.concatenate(
+        [
+            jnp.pad(gains, (0, 128 - gains.shape[0]))[None],
+            jnp.pad(node_lengths[0].astype(f32), ((0, 0), (0, 128 - nodes))),
+            jnp.pad(parents[0].astype(f32), ((0, 0), (0, 128 - nodes))),
+            jnp.zeros((3, 128), f32),
+        ]
+    )
+    tree, tree_cot, smalls, wa, wb, wc, we = deliver(
+        tokens[0], cotangent[0], small, w_query, w_key, w_value, w_output, w_gate, w_up, w_down
+    )
+    wa, wb = wa.reshape(D, 1024), wb.reshape(512, D)
+    wc, we = wc.reshape(D, 1536), we.reshape(768, D)
+    attn_g = smalls[:, :, 0, :32].reshape(D)
+    ffn_g = smalls[:, :, 0, 32:64].reshape(D)
+    query_g = smalls[:, :, 0, 64:68].reshape(HEAD_DIM)
+    key_g = smalls[:, :, 0, 68:72].reshape(HEAD_DIM)
+    mine = lax.dynamic_index_in_dim(smalls[:, 0], s // MICRO, 0, False)
+    lengths = lax.dynamic_index_in_dim(mine, 1 + s % MICRO, 0, False)[:nodes].astype(jnp.int32)
+    parent_row = lax.dynamic_index_in_dim(mine, 3 + s % MICRO, 0, False)[:nodes].astype(jnp.int32)
+    labels, starts, path_base, ancestry = tree_tables(lengths, parent_row)
+    member, position = token_nodes(jnp.arange(length, dtype=jnp.int32), labels, starts, path_base)
+    cosine_table, sine_table = rope_tables(position, HEAD_DIM)
+    seen = ancestry + jnp.eye(nodes, dtype=f32)
+    hidden = jnp.dot(member, (1.0 - seen) * BLOCKED, precision=PRECISE)
+    pad = ((0, 0), (0, 128 - nodes))
+    hidden, member = jnp.pad(hidden, pad).astype(bf), jnp.pad(member, pad).astype(bf)
+
+    rows_in = tree.reshape(length, D).astype(f32)
+    normed_in = norm_rows(rows_in, attn_g).astype(bf)
+    lin = product(normed_in, wa)
+    query_heads = lin[:, : heads * HEAD_DIM].reshape(length, heads, HEAD_DIM)
+    key_heads = lin[:, heads * HEAD_DIM : (heads + kv_heads) * HEAD_DIM].reshape(
+        length, kv_heads, HEAD_DIM
+    )
+    value = lin[:, (heads + kv_heads) * HEAD_DIM :].astype(bf)
+
+    def turn_rows(heads_in, gain_in):
+        return rotate(norm_rows(heads_in, gain_in), cosine_table, sine_table)
+
+    query_rot, pull_query = jax.vjp(turn_rows, query_heads, query_g)
+    key_rot, pull_key = jax.vjp(turn_rows, key_heads, key_g)
+    wide = lambda side, n: jnp.broadcast_to(side[:, None], (length, n, 128))
+    q_aug = jnp.concatenate([query_rot.astype(bf), wide(hidden, heads)], axis=2).transpose(1, 0, 2)
+    k_aug = jnp.concatenate([key_rot.astype(bf), wide(member, kv_heads)], axis=2).transpose(1, 0, 2)
+    attended, lse = attend(q_aug, k_aug, value)
+    part = product(attended, wb).astype(bf).reshape(NSEQ, NDP, 32, D)
+    middle, normed_mid = middle_stage(part, tree, ffn_g[None])
+    normed_mid = normed_mid.reshape(length, D)
+    both = product(normed_mid, wc)
+    gate_lin, up_lin = both[:, :768], both[:, 768:]
+    sigma_gate = jax.nn.sigmoid(gate_lin)
+    activated = (gate_lin * sigma_gate * up_lin).astype(bf)
+    part_out = product(activated, we).astype(bf).reshape(NSEQ, NDP, 32, D)
+    cot = tree_cot.reshape(length, D)
+    grad_e = across(activated, cot).astype(bf)
+    d_activated = against(cot, we)
+    d_gate = (d_activated * up_lin * sigma_gate * (1.0 + gate_lin * (1.0 - sigma_gate))).astype(bf)
+    d_up = (d_activated * gate_lin * sigma_gate).astype(bf)
+    d_both = jnp.concatenate([d_gate, d_up], axis=1)
+    grad_c = across(normed_mid, d_both).astype(bf)
+    part = against(d_both, wc).astype(bf).reshape(NSEQ, NDP, 32, D)
+    d_middle, d_low, outs, d_ffn_gain = turn_stage(part, part_out, tree_cot, middle, ffn_g[None])
+    d_low = d_low.reshape(length, D)
+    grad_b = across(attended, d_low).astype(bf)
+    d_att = against(d_low, wb).astype(bf)
+    d_query, d_key, d_value = attend_back(q_aug, k_aug, value, d_att, lse)
+    d_query, d_query_gain = pull_query(d_query.reshape(length, heads, HEAD_DIM))
+    d_key, d_key_gain = pull_key(d_key.reshape(length, kv_heads, HEAD_DIM))
+    d_lin = jnp.concatenate(
+        [d_query.reshape(length, -1).astype(bf), d_key.reshape(length, -1).astype(bf), d_value.astype(bf)],
+        axis=1,
+    )
+    grad_a = across(normed_in, d_lin).astype(bf)
+    part = against(d_lin, wa).astype(bf).reshape(NSEQ, NDP, 32, D)
+    pack = jnp.concatenate(
+        [
+            jnp.zeros((8, 128), f32),
+            d_ffn_gain.reshape(8, 128),
+            d_query_gain[None],
+            d_key_gain[None],
+            jnp.zeros((6, 128), f32),
+        ]
+    )
+    out_rows, grad_rows, pack, res_a, res_b, res_c, res_e = return_stage(
+        part, tree, d_middle, attn_g[None], outs, pack,
+        grad_a.reshape(NDP, NSEQ, 32, 1024),
+        grad_b.reshape(NSEQ, 64, D),
+        grad_c.reshape(NDP, NSEQ, 32, 1536),
+        grad_e.reshape(NSEQ, 96, D),
+    )
+    flat = lambda piece: piece.transpose(1, 0, 2).reshape(32, -1).astype(f32)
+    at = d * NSEQ + s
+    own = lambda rows, n: lax.dynamic_slice_in_dim(rows.reshape(-1), at * n, n)
+    return (
+        out_rows[None],
+        grad_rows[None].astype(f32),
+        flat(res_a[:, :, :512]),
+        flat(res_a[:, :, 512:768]),
+        flat(res_a[:, :, 768:]),
+        res_b,
+        flat(res_c[:, :, :768]),
+        flat(res_c[:, :, 768:]),
+        res_e,
+        own(pack[:8], 32),
+        own(pack[8:16], 32),
+        own(pack[16], 4),
+        own(pack[17], 4),
+    )
+
+
 def solution(mesh):
+    ring = mesh.shape["dp"] == NDP and mesh.shape["seq"] == NSEQ
     return jax.shard_map(
-        shards,
+        tree_shards if ring else general_shards,
         mesh=mesh,
         in_specs=(
             P("dp", None, "seq", None),

time: 2190 us -> 526 us (0.24)
  waiting for transfers between devices: 1590 us -> 0 us
  Pallas kernels: 0 us -> 385 us
  matrix products: 228 us -> 40.8 us
  local copies, waits for them, and re-layouts: 183 us -> 55.2 us
  blocking collectives: 82.8 us -> 0 us
  loops' own time: 38.4 us -> 0.39 us
    reduce_scatter x7 -> x0, waiting for transfers between devices: 1060 us -> none  [the longest x1 187 us: shards(): lax.psum_scatter(sums[3], ('dp', 'seq'), scatter_dimension=0, tiled=True)]
    all_gather x11 -> x0, waiting for transfers between devices: 489 us -> none  [the longest x2 82.4 us: shards(): lax.all_gather(value_low, 'seq', axis=0, tiled=True)]
    pallas_call x0 -> x6, Pallas kernels: none -> 385 us  [the longest x1 155 us: deliver(): pl.pallas_call(deliver_kernel, out_shape=(shape((NSEQ, NDP, 32, D), bf),...]
    dot_general x62 -> x1, matrix products: 105 us -> 0.47 us  [tree_shards(): hidden = jnp.dot(member, (1.0 - seen) * BLOCKED, precision=PRECISE)]
    unnamed x2 -> x0, blocking collectives: 82.8 us -> none
    dynamic_slice x64 -> x5, local copies, waits for them, and re-layouts: 82.8 us -> 2.34 us  [the longest x4 2.33 us: tree_shards(): own = lambda rows, n: lax.dynamic_slice_in_dim(rows.reshape(-1), at * n, n)]
    unnamed x273 -> x102, local copies, waits for them, and re-layouts: 58.3 us -> 19.2 us
    unnamed x22 -> x0, waiting for transfers between devices: 37.7 us -> none
  transfers between devices with their start and end apart: 20 -> 0, of which waited for: 19 -> 0; matrix products, arithmetic and copies ran while one was open for 14% -> 0% of each run, Pallas kernels for 0% -> 0%
where the time goes in v1:
time: 526 us; the launch traced here: 517 us
  Pallas kernels  385 us (73%)
  local copies, waits for them, and re-layouts  55.2 us (10%)
  matrix products  40.8 us (8%)
  other arithmetic  33.1 us (6%)
    pallas_call x1, Pallas kernels, deliver(): pl.pallas_call(deliver_kernel, out_shape=(shape((NSEQ, NDP, 32, D), bf),...  155 us
    pallas_call x1, Pallas kernels, return_stage(): pl.pallas_call(return_kernel, out_shape=(shape((MICRO, 128, D), bf), shap...  129 us
    pallas_call x1, Pallas kernels, turn_stage(): pl.pallas_call(turn_kernel, out_shape=(shape((NSEQ, 32, D), f32), shape((...  47.2 us
    pallas_call x1, Pallas kernels, middle_stage(): pl.pallas_call(middle_kernel, out_shape=(shape((NSEQ, 32, D), f32), shape...  32.8 us
    unnamed x102, local copies, waits for them, and re-layouts  19.2 us
    dot_general x4, matrix products, across(): lax.dot_general(left_side, right_side, (((0,), (0,)), ((), ())), preferre...  15.1 us
    dot_general x4, matrix products, against(): lax.dot_general(left_side, right_side, (((1,), (1,)), ((), ())), preferre...  14.9 us
    pallas_call x1, Pallas kernels, attend_back(): pl.pallas_call(attend_back_kernel, grid=(heads,), out_shape=(shape((lengt...  14.2 us

profile of v1, /device:TPU:21, one launch (start us, length us, event | category | flops | bytes accessed | tf_op | source)
XLA Modules:
  0.0 516.8 jit_solution(2300444864372419581)
XLA Ops:
  2.9 155.5 %deliver.1 = (bf16[8,4,32,1024]{3,2,1,0:T(8,128)(2,1)}, bf16[8,4,32,1024]{3,2,1,0:T(8,128)(2,1)}, f32[4,8,8,128]{3,2,1,0:T(8,128)}, bf16[4,8,32,1024]{3,2,1,0:T(...) custom-call(bf16[2,128,1024]{2,1,0:T(8,128)(2,1)} %bitcast.138, ...), custom_call_target="tpu_custom_call" | custom-call | tf_op jit(solution)/shard_map/deliver/pallas_call | solution.py:640
  159.4 2.8 while.13
  163.1 1.9 multiply_cosine_fusion
  168.3 1.0 copy-done.42
  169.3 2.4 fusion.43
  171.8 1.2 slice.110
  174.0 1.5 copy.58
  178.5 1.1 copy-done.28
  179.8 1.4 slice.107
  181.2 2.9 copy.56
  184.2 1.9 multiply_multiply_fusion
  188.0 2.2 fusion.8
  192.1 1.5 maximum_bitcast_fusion.q_ref
  193.6 2.1 slice.113
  195.7 2.1 copy.82.v_ref
  197.8 1.0 copy-done.1
  198.8 6.8 %attend.1 = (bf16[1024,512]{1,0:T(8,128)(2,1)S(1)}, f32[4,1024,1]{2,1,0:T(8,128)}) custom-call(bf16[4,1024,256]{2,1,0:T(8,128)(2,1)} %maximum_bitcast_fusion.q_ref, bf16[2,1024,256]{2,1,0:T(8,128)(2,1)S(1)} %maximum_bitcast_fusion.1.k_ref, bf16[1024,256]{1,0:T(8,128)(2,1)S(1)} %copy-done.1), custom_call_target="tpu_custom_call" | custom-call | tf_op jit(solution)/shard_map/attend/pallas_call | solution.py:994
  205.6 2.6 convolution_convert_fusion.3
  208.3 1.6 copy-done.5
  209.9 32.8 %middle.1 = (f32[8,32,1024]{2,1,0:T(8,128)S(1)}, bf16[8,4,32,1024]{3,2,1,0:T(8,128)(2,1)S(1)}) custom-call(bf16[8,4,32,1024]{3,2,1,0:T(8,128)(2,1)S(1)} %bitcast.117, bf16[8,4,32,1024]{3,2,1,0:T(8,128)(2,1)S(1)} %copy-done, f32[1,1024]{1,0:T(1,128)S(1)} %broadcast_in_dim_reshape_squeeze.4.gain), custom_call_target="tpu_custom_call" | custom-call | tf_op jit(solution)/shard_map/middle/pallas_call | solution.py:699
  242.7 3.5 fusion.44
  246.2 3.3 multiply_convert_fusion.3
  249.5 6.1 %convolution_convert_fusion = bf16[1024,1536]{1,0:T(8,128)(2,1)} fusion(bf16[1024,1024]{1,0:T(8,128)(2,1)S(1)} %bitcast.122, bf16[1024,768]{0,1:T(8,128)(2,1)S(1)} %get-tuple-element.125, bf16[1024,768]{0,1:T(8,128)(2,1)S(1)} %get-tuple-element.124), kind=kOutput, calls=%fused_computation.10 | convolution fusion | flops 3229089792 | bytes 8388608 | tf_op jit(solution)/shard_map/dot_general | solution.py:93
  255.6 1.9 convolution_convert_fusion.4
  257.5 3.7 fusion.10
  261.2 47.2 %turn.1 = (f32[8,32,1024]{2,1,0:T(8,128)S(1)}, bf16[8,4,32,1024]{3,2,1,0:T(8,128)(2,1)S(1)}, bf16[8,32,1024]{2,1,0:T(8,128)(2,1)S(1)}, f32[1,1024]{1,0:T(1,128)S(1)}) custom-call(bf16[8,4,32,1024]{3,2,1,0:T(8,128)(2,1)S(1)} %bitcast.116, bf16[8,4,32,1024]{3,2,1,0:T(8,128)(2,1)S(1)} %bitcast.115, bf16[8,4,32,1024]{3,2,1,0:T(8,128)(2,1)S(1)} %copy-done.3, ...), custom_call_target="tpu_custom_call" | custom-call | tf_op jit(solution)/shard_map/turn/pallas_call | solution.py:753
  308.5 2.3 convolution_convert_fusion.6
  310.7 2.3 convolution_convert_fusion.7.do_ref
  313.0 14.2 %attend_back.1 = (f32[1024,512]{1,0:T(8,128)}, f32[1024,256]{1,0:T(8,128)S(1)}, f32[1024,256]{1,0:T(8,128)S(1)}) custom-call(bf16[4,1024,256]{2,1,0:T(8,128)(2,1)} %maximum_bitcast_fusion.q_ref, bf16[2,1024,256]{2,1,0:T(8,128)(2,1)S(1)} %maximum_bitcast_fusion.1.k_ref, bf16[1024,256]{1,0:T(8,128)(2,1)S(1)} %copy-done.2, ...), custom_call_target="tpu_custom_call" | custom-call | tf_op jit(solution)/shard_map/attend_back/pallas_call | solution.py:1044
  329.2 2.9 copy.62
  332.1 3.0 copy.63
  335.1 1.7 broadcast_multiply_fusion
  339.1 1.8 multiply_reduce_fusion.2
  341.0 2.4 fusion.6
  343.4 2.6 copy.67
  346.0 1.4 copy.68
  347.4 2.6 copy.69
  350.0 1.3 broadcast_multiply_fusion.1
  354.0 1.4 fusion.11
  355.4 2.1 copy.73
  358.3 2.0 copy.74
  361.9 3.7 convolution_convert_fusion.1
  365.7 1.8 concatenate.43.pack_in
  367.5 5.7 %convolution_convert_fusion.2 = bf16[1024,1024]{1,0:T(8,128)(2,1)} fusion(bf16[1024,1024]{1,0:T(8,128)(2,1)} %bitcast.150, bf16[1024,256]{0,1:T(8,128)(2,1)} %copy.74, bf16[1024,256]{0,1:T(8,128)(2,1)} %bitcast.136, bf16[1024,512]{0,1:T(8,128)(2,1)S(1)} %bitcast.134), kind=kOutput, calls=%fused_computation.32 | convolution fusion | flops 2154823680 | bytes 6291456 | tf_op jit(solution)/shard_map/dot_general | solution.py:87
  373.2 3.1 convolution_convert_fusion.5
  376.9 128.9 %give_back.1 = (bf16[2,128,1024]{2,1,0:T(8,128)(2,1)}, bf16[2,128,1024]{2,1,0:T(8,128)(2,1)}, f32[24,128]{1,0:T(8,128)}, bf16[4,32,1024]{2,1,0:T(8,128)(2,1)}, f...) custom-call(bf16[8,4,32,1024]{3,2,1,0:T(8,128)(2,1)} %bitcast.131, ...), custom_call_target="tpu_custom_call" | custom-call | tf_op jit(solution)/shard_map/give_back/pallas_call | solution.py:933
  505.9 1.2 convert_bitcast_fusion
  508.6 1.1 bitcast_convert_fusion
  (218 shorter events, 36.1 us)
Async XLA Ops:
  158.4 8.6 %copy-start.39 = (f32[4,8,8,128]{3,2,1,0:T(8,128)S(1)}, f32[4,8,8,128]{3,2,1,0:T(8,128)}, u32[]{:S(2)}) copy-start(f32[4,8,8,128]{3,2,1,0:T(8,128)} %get-tuple-element.61) | copy-start | bytes 393220
  158.4 8.8 %copy-start = (bf16[8,4,32,1024]{3,2,1,0:T(8,128)(2,1)S(1)}, bf16[8,4,32,1024]{3,2,1,0:T(8,128)(2,1)}, u32[]{:S(2)}) copy-start(bf16[8,4,32,1024]{3,2,1,0:T(8,128)(2,1)} %get-tuple-element.60.tree) | copy-start | bytes 6291460
  167.7 1.6 copy-start.42
  171.7 2.3 copy-start.27
  175.5 1.0 copy-start.16
  176.2 1.0 copy-start.19
  176.2 1.2 copy-start.23
  177.4 2.2 copy-start.28
  186.2 1.6 copy-start.14
  186.2 1.7 copy-start.20
  186.2 1.8 copy-start.24
  190.9 1.2 copy-start.30
  197.8 1.0 copy-start.1
  198.8 6.8 %copy-start.44 = (bf16[8,64,1024]{2,1,0:T(8,128)(2,1)S(1)}, bf16[8,64,1024]{2,1,0:T(8,128)(2,1)}, u32[]{:S(2)}) copy-start(bf16[8,64,1024]{2,1,0:T(8,128)(2,1)} %get-tuple-element.67) | copy-start | bytes 3145732
  205.6 2.6 copy-start.10
  208.3 1.6 copy-start.5
  209.9 32.9 %copy-start.41 = (bf16[4,8,32,1536]{3,2,1,0:T(8,128)(2,1)S(1)}, bf16[4,8,32,1536]{3,2,1,0:T(8,128)(2,1)}, u32[]{:S(2)}) copy-start(bf16[4,8,32,1536]{3,2,1,0:T(8,128)(2,1)} %get-tuple-element.69) | copy-start | bytes 9437188
  242.7 3.5 copy-start.3
  242.7 3.5 copy-start.43
  249.5 6.1 %copy-start.46 = (bf16[1024,768]{0,1:T(8,128)(2,1)}, bf16[1024,768]{0,1:T(8,128)(2,1)S(1)}, u32[]{:S(2)}) copy-start(bf16[1024,768]{0,1:T(8,128)(2,1)S(1)} %get-tuple-element.126) | copy-start | bytes 4718596
  261.2 47.3 %copy-start.11 = (bf16[1024,512]{1,0:T(8,128)(2,1)S(1)}, bf16[1024,512]{1,0:T(8,128)(2,1)}, u32[]{:S(2)}) copy-start(bf16[1024,512]{1,0:T(8,128)(2,1)} %copy-done.10) | copy-start | bytes 3145732
  308.4 2.3 copy-start.12
  308.4 2.3 copy-start.13
  308.5 2.3 copy-start.45
  310.7 2.3 copy-start.2
  327.2 1.0 copy-start.6
  328.2 1.0 copy-start.8
  332.1 3.0 copy-start.25
  336.8 1.6 copy-start.15
  336.9 2.2 copy-start.18
  336.9 2.3 copy-start.21
  343.4 2.6 copy-start.9
  347.4 2.6 copy-start.26
  351.3 1.2 copy-start.17
  351.3 1.3 copy-start.22
  351.3 1.7 copy-start.29
  353.9 3.5 copy-start.7
  360.4 1.2 copy-start.31
  360.4 1.4 copy-start.34
  360.4 1.5 copy-start.35
  367.5 5.7 %copy-start.4 = (bf16[8,4,32,1024]{3,2,1,0:T(8,128)(2,1)S(1)}, bf16[8,4,32,1024]{3,2,1,0:T(8,128)(2,1)}, u32[]{:S(2)}) copy-start(bf16[8,4,32,1024]{3,2,1,0:T(8,128)(2,1)} %get-tuple-element.64.tree_cot) | copy-start | bytes 6291460
  367.5 5.7 %copy-start.47 = (bf16[1024,768]{0,1:T(8,128)(2,1)S(1)}, bf16[1024,768]{0,1:T(8,128)(2,1)}, u32[]{:S(2)}) copy-start(bf16[1024,768]{0,1:T(8,128)(2,1)} %copy-done.46) | copy-start | bytes 4718596
  505.9 2.7 copy-start.32
  505.9 3.8 copy-start.37
  507.8 4.0 copy-start.40
  507.8 6.3 %copy-start.33 = (bf16[2,128,1024]{2,1,0:T(8,128)(2,1)S(1)}, bf16[2,128,1024]{2,1,0:T(8,128)(2,1)}, u32[]{:S(2)}) copy-start(bf16[2,128,1024]{2,1,0:T(8,128)(2,1)} %get-tuple-element.79) | copy-start | bytes 1572868
  508.6 6.3 %copy-start.38 = (f32[64,1024]{1,0:T(8,128)S(1)}, f32[64,1024]{1,0:T(8,128)}, u32[]{:S(2)}) copy-start(f32[64,1024]{1,0:T(8,128)} %get-tuple-element.219) | copy-start | bytes 786436
  509.7 5.9 %copy-start.36 = (f32[96,1024]{1,0:T(8,128)S(1)}, f32[96,1024]{1,0:T(8,128)}, u32[]{:S(2)}) copy-start(f32[96,1024]{1,0:T(8,128)} %get-tuple-element.222) | copy-start | bytes 1179652

commit v2 on v0

--- a/solution.py
+++ b/solution.py
@@ -1,6 +1,10 @@
+import functools
+
 import jax
 import jax.numpy as jnp
 from jax import lax
+from jax.experimental import pallas as pl
+from jax.experimental.pallas import tpu as pltpu
 from jax.sharding import PartitionSpec as P
 
 D = 1024
@@ -91,7 +95,7 @@
     )
 
 
-def shards(
+def general_shards(
     tokens,
     cotangent,
     node_lengths,
@@ -384,9 +388,972 @@
     )
 
 
+MESH = pl.DeviceIdType.MESH
+NDP = 4
+NSEQ = 8
+BLOCKED = -65536.0
+QB = 256
+BLOCKS = (3, 2, 1, 0)
+SOFT = HEAD_DIM ** (-0.5) * 1.4426950408889634
+
+
+def seq_at(position):
+    half = position // 4
+    z = position + half * (7 - 2 * position)
+    return 2 * z + half
+
+
+def greet_all(d, s):
+    barrier = pltpu.get_barrier_semaphore()
+    me = d * NSEQ + s
+
+    def signal(i, carry):
+        other = (me + i) % (NDP * NSEQ)
+        pl.semaphore_signal(
+            barrier, inc=1, device_id=(other // NSEQ, other % NSEQ), device_id_type=MESH
+        )
+        return carry
+
+    lax.fori_loop(1, NDP * NSEQ, signal, 0)
+    pl.semaphore_wait(barrier, NDP * NSEQ - 1)
+
+
+def remote(src, dst, sems, at, d, s):
+    send, recv = sems
+    return pltpu.make_async_remote_copy(
+        src_ref=src,
+        dst_ref=dst,
+        send_sem=send.at[at],
+        recv_sem=recv.at[at],
+        device_id=(d, s),
+        device_id_type=MESH,
+    )
+
+
+class Sum:
+    def __init__(self, part, near, sent, got, sems, n, spot):
+        self.part, self.near, self.sent, self.got = part, near, sent, got
+        self.sems, self.n = sems, n
+        d, self.s = spot
+        x, c = d // 2, d % 2
+        self.d, self.sib, self.far = d, 2 * x + 1 - c, 2 * (1 - x) + c
+        self.far_sib = 2 * (1 - x) + 1 - c
+
+    def copies(self, b):
+        rows = pl.ds(2 * b, 2)
+        return (
+            remote(self.part.at[rows, self.far_sib], self.near.at[0, rows], self.sems, (self.n, 0, b), self.sib, self.s),
+            remote(self.part.at[rows, self.sib], self.near.at[1, rows], self.sems, (self.n, 1, b), self.sib, self.s),
+            remote(self.sent.at[rows], self.got.at[rows], self.sems, (self.n, 2, b), self.far, self.s),
+        )
+
+    def start(self, b):
+        first, second, _ = self.copies(b)
+        first.start()
+        second.start()
+
+    def mid(self, b):
+        first, _, across_x = self.copies(b)
+        first.wait_recv()
+        for i in (2 * b, 2 * b + 1):
+            self.sent[i] = (
+                self.part[i, self.far].astype(jnp.float32) + self.near[0, i].astype(jnp.float32)
+            ).astype(jnp.bfloat16)
+        across_x.start()
+
+    def end(self, b, finish):
+        first, second, across_x = self.copies(b)
+        second.wait_recv()
+        across_x.wait_recv()
+        for i in (2 * b, 2 * b + 1):
+            rows = self.part[i, self.d].astype(jnp.float32) + self.near[1, i].astype(jnp.float32)
+            finish(i, rows + self.got[i].astype(jnp.float32))
+        first.wait_send()
+        second.wait_send()
+        across_x.wait_send()
+
+
+class Spread:
+    def __init__(self, out, sems, at, spot):
+        self.out, self.sems, self.place = out, sems, at
+        d, self.s = spot
+        x, c = d // 2, d % 2
+        self.d, self.sib, self.far = d, 2 * x + 1 - c, 2 * (1 - x) + c
+        self.far_sib = 2 * (1 - x) + 1 - c
+
+    def copy(self, rows, owner, way, to):
+        block = self.out.at[rows, owner]
+        return remote(block, block, self.sems, self.place(way, rows), to, self.s)
+
+    def start(self, rows):
+        self.copy(rows, self.d, 0, self.far).start()
+        self.copy(rows, self.d, 1, self.sib).start()
+
+    def mid(self, rows):
+        self.copy(rows, self.far, 0, self.far).wait_recv()
+        self.copy(rows, self.far, 2, self.sib).start()
+
+    def end(self, rows):
+        self.copy(rows, self.sib, 1, self.sib).wait_recv()
+        self.copy(rows, self.far_sib, 2, self.sib).wait_recv()
+
+    def sent(self, rows):
+        self.copy(rows, self.d, 0, self.far).wait_send()
+        self.copy(rows, self.d, 1, self.sib).wait_send()
+        self.copy(rows, self.far, 2, self.sib).wait_send()
+
+
+def layer_kernel(
+    nodes,
+    tok, cot, small, inv_freq, wq, wk, wv, wo, wg, wu, wd,
+    out_rows, grad_rows, pack_out, g_query, g_key, g_value, g_output, g_gate, g_up, g_down,
+    smalls, wa, wb, wc, we, ge, hop_a, hop_b, hop_c, hop_e,
+    tree, tree_cot, normed_in, normed_mid, d_low, tree_own,
+    lin, query, key, value, hidden, member, cosine, sine, att, d_att,
+    part, part_out, near, sent, got, near_o, sent_o, got_o,
+    middle, d_middle, act, both, d_key, d_value, outs, grad_low,
+    fin_a, fin_c, got_a, got_c, attn_g, ffn_g, head_g, pack_dp, pack_seq,
+    loc, s_small, r_small, s_col, r_col, s_tok, r_tok, s_ag, r_ag, s_rs, r_rs,
+    s_sum, r_sum, s_tree, r_tree, s_spread, r_spread, s_back, r_back, s_fin, r_fin, s_pack, r_pack,
+):
+    f32, bf = jnp.float32, jnp.bfloat16
+    d = lax.axis_index("dp")
+    s = lax.axis_index("seq")
+    z, y = s // 2, s % 2
+    p = z + y * (7 - 2 * z)
+    spot = (d, s)
+    seat = [seq_at((p + i) % NSEQ) for i in range(NSEQ)]
+    up, down = seat[1], seat[7]
+    ag_sems, rs_sems = (s_ag, r_ag), (s_rs, r_rs)
+    small_sems, col_sems, tok_sems = (s_small, r_small), (s_col, r_col), (s_tok, r_tok)
+
+    def aligned(v, n):
+        return pl.multiple_of(v, n)
+
+    def chunk(n, way, j):
+        if n in (0, 1, 3, 4):
+            return pl.ds(aligned((2 * way + (n + (n > 2)) % 2) * 256 + j * 32, 32), 32)
+        if n == 2:
+            return pl.ds(aligned(j * 64 + way * 32, 32), 32)
+        return pl.ds(aligned(j * 96 + way * 48, 16), 48)
+
+    weight = {0: wa, 1: wa, 2: wb, 3: wc, 4: wc, 5: we}
+    grads = {0: wa, 1: wa, 2: wb, 3: wc, 4: wc, 5: ge}
+    hops = {0: hop_a.at[0], 1: hop_a.at[1], 2: hop_b, 3: hop_c.at[0], 4: hop_c.at[1], 5: hop_e}
+
+    def owner_at(way, k):
+        return seq_at((p + NSEQ - k) % NSEQ) if way == 0 else seq_at((p + k) % NSEQ)
+
+    def gather(n, k):
+        for way, peer in enumerate((up, down)):
+            block = weight[n].at[chunk(n, way, owner_at(way, k))]
+            if not (isinstance(k, int) and k == 0):
+                remote(block, block, ag_sems, (n, way, k - 1), d, peer).wait_recv()
+            remote(block, block, ag_sems, (n, way, k), d, peer).start()
+
+    def gather_end(n):
+        for way, peer in enumerate((up, down)):
+            block = weight[n].at[chunk(n, way, owner_at(way, 7))]
+            remote(block, block, ag_sems, (n, way, 6), d, peer).wait_recv()
+
+    def gather_sent(n):
+        for way, peer in enumerate((up, down)):
+            block = weight[n].at[chunk(n, way, s)]
+            for k in range(7):
+                remote(block, block, ag_sems, (n, way, k), d, peer).wait_send()
+
+    def reduce_(n, k):
+        for way, peer in enumerate((up, down)):
+            rows = chunk(n, way, seat[(7 - k) % NSEQ] if way == 0 else seat[(1 + k) % NSEQ])
+            mine = grads[n].at[rows]
+            if k == 0:
+                src = mine
+            else:
+                src = hops[n].at[way, k - 1]
+                remote(src, src, rs_sems, (n, way, k - 1), d, peer).wait_recv()
+                src[...] = (src[...].astype(f32) + mine[...].astype(f32)).astype(bf)
+            remote(src, hops[n].at[way, k], rs_sems, (n, way, k), d, peer).start()
+
+    def reduce_end(n, take):
+        for way, peer in enumerate((up, down)):
+            src = hops[n].at[way, 6]
+            remote(src, src, rs_sems, (n, way, 6), d, peer).wait_recv()
+            take(way, src[...].astype(f32) + grads[n][chunk(n, way, s)].astype(f32))
+
+    def reduce_sent(n):
+        for way, peer in enumerate((up, down)):
+            for k in range(7):
+                src = hops[n].at[way, k]
+                remote(src, src, rs_sems, (n, way, k), d, peer).wait_send()
+
+    greet_all(d, s)
+    pending = []
+
+    def launch(cp):
+        cp.start()
+        pending.append(cp)
+
+    own_small = pltpu.make_async_copy(small, smalls.at[d, s], loc.at[0])
+    own_small.start()
+    pieces = (
+        (wq, wa, 512, 0), (wk, wa, 256, 512), (wv, wa, 256, 768), (wg, wc, 768, 0), (wu, wc, 768, 768)
+    )
+    col_rows = lambda q: pl.ds(aligned(q * 256 + s * 32, 32), 32)
+    local = []
+
+    def columns(n):
+        src, dst, width, at = pieces[n]
+        for i in range(1, NDP):
+            q = (d + i) % NDP
+            launch(
+                remote(
+                    src.at[:, pl.ds(aligned(q * width, 128), width)],
+                    dst.at[col_rows(d), pl.ds(at, width)],
+                    col_sems, (n, i), q, s,
+                )
+            )
+        cp = pltpu.make_async_copy(
+            src.at[:, pl.ds(aligned(d * width, 128), width)],
+            dst.at[col_rows(d), pl.ds(at, width)],
+            loc.at[1 + n],
+        )
+        cp.start()
+        local.append(cp)
+
+    def columns_in(n):
+        _, dst, width, at = pieces[n]
+        local[n].wait()
+        for i in range(1, NDP):
+            place = dst.at[col_rows((d + NDP - i) % NDP), pl.ds(at, width)]
+            remote(place, place, col_sems, (n, i), d, s).wait_recv()
+
+    def rows_out(n, src, dst):
+        for m in range(MICRO):
+            target = MICRO * d + m
+            for i in range(NDP):
+                q = (d + i) % NDP
+                piece = src.at[m, pl.ds(aligned(q * 32, 32), 32)]
+                place = dst.at[s, q]
+                cp = pltpu.make_async_remote_copy(
+                    src_ref=piece, dst_ref=place, send_sem=s_tok.at[n, m, i], recv_sem=r_tok.at[n],
+                    device_id=(q, target), device_id_type=MESH,
+                )
+                if i == 0:
+
+                    @pl.when(target == s)
+                    def _():
+                        pltpu.make_async_copy(piece, place, r_tok.at[n]).start()
+
+                    @pl.when(target != s)
+                    def _():
+                        cp.start()
+                else:
+                    launch(cp)
+
+    def rows_in(dst, n):
+        everything = dst.at[:, d]
+        pltpu.make_async_copy(everything, everything, r_tok.at[n]).wait()
+
+    fill_b = pltpu.make_async_copy(wo, wb.at[pl.ds(aligned(s * 64, 64), 64)], loc.at[6])
+    fill_e = pltpu.make_async_copy(wd, we.at[pl.ds(aligned(s * 96, 16), 96)], loc.at[7])
+    fill_b.start()
+    fill_e.start()
+    for n in range(3):
+        columns(n)
+    rows_out(0, tok, tree)
+    own_small.wait()
+    for i in range(1, NDP):
+        launch(remote(smalls.at[d, s], smalls.at[d, s], small_sems, i, (d + i) % NDP, s))
+    fill_b.wait()
+    gather(2, 0)
+    for n in range(3):
+        columns_in(n)
+    gather(0, 0)
+    gather(1, 0)
+    for n in range(3, 5):
+        columns(n)
+    rows_out(1, cot, tree_cot)
+    for i in range(1, NDP):
+        place = smalls.at[(d + NDP - i) % NDP, s]
+        remote(place, place, small_sems, i, d, s).wait_recv()
+    for i in range(1, NSEQ):
+        launch(remote(smalls.at[:, s], smalls.at[:, s], small_sems, NDP + i, d, (s + i) % NSEQ))
+
+    def gather_ab(k):
+        gather(2, k)
+        gather(0, k)
+        gather(1, k)
+
+    gather_ab(1)
+    everything = pl.ds(0, NSEQ)
+    spread_tree = Spread(tree, (s_tree, r_tree), lambda way, rows: (0, way), spot)
+    spread_cot = Spread(tree_cot, (s_tree, r_tree), lambda way, rows: (1, way), spot)
+    rows_in(tree, 0)
+    spread_tree.start(everything)
+    ir = lax.broadcasted_iota(jnp.int32, (128, 128), 0)
+    ic = lax.broadcasted_iota(jnp.int32, (128, 128), 1)
+    block = smalls.at[s // MICRO, s]
+    length_row = block[pl.ds(4 + s % MICRO, 1), :]
+    parent_row = block[pl.ds(6 + s % MICRO, 1), :]
+    length_col = jnp.sum(jnp.where(ir == ic, length_row, 0.0), axis=1, keepdims=True)
+    over = (parent_row == ir.astype(f32)) & (ic > 0) & (ic < nodes)
+    above = jnp.where(over | (ir == ic), 1.0, 0.0)
+    for _ in range(4):
+        low = above.astype(bf)
+        above = jnp.minimum(product(low, low), 1.0)
+    start_row = jnp.sum(jnp.where(ir < ic, length_col, 0.0), axis=0, keepdims=True)
+    base_row = jnp.sum(
+        jnp.where((above > 0.5) & (ir != ic), length_col, 0.0), axis=0, keepdims=True
+    )
+    shut = jnp.where(above > 0.5, 0.0, BLOCKED).astype(bf)
+    gather_ab(2)
+
+    def tables(i, carry):
+        rows = pl.ds(aligned(i * QB, QB), QB)
+        index = (lax.broadcasted_iota(jnp.int32, (QB, 128), 0) + i * QB).astype(f32)
+        inside = (index >= start_row) & (index < start_row + length_row)
+        position = index[:, :1] + jnp.sum(
+            jnp.where(inside, base_row - start_row, 0.0), axis=1, keepdims=True
+        )
+        hot = jnp.where(inside, 1.0, 0.0).astype(bf)
+        member[rows] = hot
+        hidden[rows] = against(hot, shut).astype(bf)
+        angle = position * inv_freq[...]
+        cosine[rows] = jnp.cos(angle)
+        lane = lax.broadcasted_iota(jnp.int32, (QB, 128), 1)
+        wave = jnp.sin(angle)
+        sine[rows] = jnp.where(lane < 64, -wave, wave)
+        return carry
+
+    lax.fori_loop(0, 2, tables, 0)
+    gather_ab(3)
+    lax.fori_loop(2, 4, tables, 0)
+    spread_tree.mid(everything)
+    gather_ab(4)
+    for i in range(1, NSEQ):
+        place = smalls.at[:, (s + NSEQ - i) % NSEQ]
+        remote(place, place, small_sems, NDP + i, d, s).wait_recv()
+    lane = lax.broadcasted_iota(jnp.int32, (1, 128), 1)
+    for row, dst in ((0, attn_g), (1, ffn_g)):
+        for j in range(8):
+            parts = [smalls[(4 * j + i) // 8, (4 * j + i) % 8, row : row + 1, :] for i in range(4)]
+            joined = jnp.where(lane < 64, jnp.where(lane < 32, parts[0], parts[1]), jnp.where(lane < 96, parts[2], parts[3]))
+            dst[:, 128 * j : 128 * (j + 1)] = joined
+    for row in (2, 3):
+        joined = jnp.zeros((1, 128), f32)
+        for i in range(32):
+            joined = jnp.where(lane // 4 == i, smalls[i // 8, i % 8, row : row + 1, :], joined)
+        head_g[row - 2 : row - 1, :] = joined
+    pack_dp[d] = jnp.zeros((24, 128), f32)
+    spread_tree.end(everything)
+    own_rows = pltpu.make_async_copy(tree.at[:, d], tree_own, loc.at[8])
+    own_rows.start()
+
+    def norm_in(i, carry):
+        rows = tree[i].reshape(128, D).astype(f32)
+        scale = lax.rsqrt(jnp.mean(rows * rows, axis=-1, keepdims=True) + EPSILON)
+        normed_in[pl.ds(aligned(i * 128, 128), 128)] = (rows * scale * attn_g[...]).astype(bf)
+        return carry
+
+    lax.fori_loop(0, 4, norm_in, 0)
+    gather_ab(5)
+    lax.fori_loop(4, 8, norm_in, 0)
+    gather_ab(6)
+    for n in range(3, 5):
+        columns_in(n)
+    gather(3, 0)
+    gather(4, 0)
+    rows_in(tree_cot, 1)
+    spread_cot.start(everything)
+    gather_end(0)
+    gather_end(1)
+
+    def unit_of(v):
+        scale = lax.rsqrt(jnp.mean(v * v, axis=-1, keepdims=True) + EPSILON)
+        return v * scale, scale
+
+    def turn(v, gain, cos, sin):
+        unit, _ = unit_of(v)
+        lifted = unit * gain
+        return lifted * cos + pltpu.roll(lifted, 64, 1) * sin
+
+    def turn_back(dr, v, gain, cos, sin):
+        d_lift = dr * cos + pltpu.roll(dr * sin, 64, 1)
+        unit, scale = unit_of(v)
+        d_unit = d_lift * gain
+        return (
+            scale * (d_unit - unit * jnp.mean(unit * d_unit, axis=-1, keepdims=True)),
+            jnp.sum(d_lift * unit, axis=0, keepdims=True),
+        )
+
+    def project(i, carry):
+        rows = pl.ds(aligned(i * QB, QB), QB)
+        normed = normed_in[rows]
+        cos, sin = cosine[rows], sine[rows]
+        for j in range(3):
+            pair = product(normed, wa[:, 256 * j : 256 * (j + 1)])
+            lin[rows, 256 * j : 256 * (j + 1)] = pair
+            gain = head_g[0:1, :] if j < 2 else head_g[1:2, :]
+            for i2 in range(2):
+                turned = turn(pair[:, 128 * i2 : 128 * (i2 + 1)], gain, cos, sin).astype(bf)
+                if j < 2:
+                    query[2 * j + i2, rows] = turned
+                else:
+                    key[i2, rows] = turned
+        value[rows] = product(normed, wa[:, 768:]).astype(bf)
+        gather(3, 1 + i)
+        gather(4, 1 + i)
+        return carry
+
+    lax.fori_loop(0, 4, project, 0)
+    gather_end(2)
+    spread_cot.mid(everything)
+    fill_e.wait()
+
+    def span(b):
+        return pl.ds(b * QB, QB), (b + 1) * QB
+
+    def weights_of(b, h, n):
+        here = pl.ds(b * QB, QB)
+        q = jnp.concatenate([query[h, here], hidden[here]], axis=1)
+        k = jnp.concatenate([key[h // 2, pl.ds(0, n)], member[pl.ds(0, n)]], axis=1)
+        score = against(q, k) * SOFT
+        row = lax.broadcasted_iota(jnp.int32, (QB, QB), 0)
+        col = lax.broadcasted_iota(jnp.int32, (QB, QB), 1)
+        diag = jnp.where(col <= row, score[:, n - QB :], NEGATIVE)
+        score = diag if b == 0 else jnp.concatenate([score[:, : n - QB], diag], axis=1)
+        grown = jnp.exp2(score)
+        return grown, 1.0 / jnp.sum(grown, axis=-1, keepdims=True)
+
+    def head_lanes(h):
+        return pl.ds(aligned(h * HEAD_DIM, HEAD_DIM), HEAD_DIM)
+
+    def attend(b):
+        here, n = span(b)
+
+        def one(h, carry):
+            grown, inverse = weights_of(b, h, n)
+            mixed = product(grown.astype(bf), value[pl.ds(0, n), head_lanes(h // 2)])
+            att[here, head_lanes(h)] = (mixed * inverse).astype(bf)
+            return carry
+
+        lax.fori_loop(0, HEADS // NDP, one, 0)
+        rows = product(att[here], wb[...]).astype(bf)
+        part[pl.ds(2 * b, 2)] = rows.reshape(2, NDP, 32, D)
+
+    sum_sems, spread_sems = (s_sum, r_sum), (s_spread, r_spread)
+    mixed_sum = Sum(part, near, sent, got, sum_sems, 0, spot)
+    mid_sum = Sum(part, near, sent, got, sum_sems, 1, spot)
+    out_sum = Sum(part_out, near_o, sent_o, got_o, sum_sems, 2, spot)
+    in_sum = Sum(part, near, sent, got, sum_sems, 3, spot)
+    pair_of = {b: pl.ds(2 * b, 2) for b in BLOCKS}
+    spread_mid = Spread(normed_mid, spread_sems, lambda way, rows: (0, way, rows.start // 2), spot)
+    spread_low = Spread(d_low, spread_sems, lambda way, rows: (1, way, rows.start // 2), spot)
+
+    def to_middle(i, rows):
+        rows = rows + tree_own[i].astype(f32)
+        middle[i] = rows
+        scale = lax.rsqrt(jnp.mean(rows * rows, axis=-1, keepdims=True) + EPSILON)
+        normed_mid[i, d] = (rows * scale * ffn_g[...]).astype(bf)
+
+    own_rows.wait()
+    attend(3)
+    mixed_sum.start(3)
+    gather(3, 5)
+    gather(4, 5)
+    attend(2)
+    mixed_sum.mid(3)
+    mixed_sum.start(2)
+    gather(3, 6)
+    gather(4, 6)
+    gather(5, 0)
+    attend(1)
+    mixed_sum.end(3, to_middle)
+    spread_mid.start(pair_of[3])
+    mixed_sum.mid(2)
+    mixed_sum.start(1)
+    gather(5, 1)
+    attend(0)
+    spread_mid.mid(pair_of[3])
+    mixed_sum.end(2, to_middle)
+    spread_mid.start(pair_of[2])
+    mixed_sum.mid(1)
+    mixed_sum.start(0)
+    spread_cot.end(everything)
+    gather_end(3)
+    gather_end(4)
+    gather(5, 2)
+
+    def lift(b):
+        here = pl.ds(b * QB, QB)
+        rows = normed_mid[pl.ds(2 * b, 2)].reshape(QB, D)
+
+        def one(t, carry):
+            left = pl.ds(aligned(t * 256, 256), 256)
+            right = pl.ds(aligned(768 + t * 256, 256), 256)
+            gate = product(rows, wc[:, left])
+            wide = product(rows, wc[:, right])
+            sigma = 1.0 / (1.0 + jnp.exp(-gate))
+            silu = gate * sigma
+            act[here, left] = (silu * wide).astype(bf)
+            both[here, left] = (wide * sigma * (1.0 + gate * (1.0 - sigma))).astype(bf)
+            both[here, right] = silu.astype(bf)
+            return carry
+
+        lax.fori_loop(0, 3, one, 0)
+
+    spread_mid.end(pair_of[3])
+    lift(3)
+    spread_mid.mid(pair_of[2])
+    mixed_sum.end(1, to_middle)
+    spread_mid.start(pair_of[1])
+    mixed_sum.mid(0)
+    gather(5, 3)
+    spread_mid.end(pair_of[2])
+    lift(2)
+    spread_mid.mid(pair_of[1])
+    mixed_sum.end(0, to_middle)
+    spread_mid.start(pair_of[0])
+    gather(5, 4)
+    spread_mid.end(pair_of[1])
+    lift(1)
+    spread_mid.mid(pair_of[0])
+    gather(5, 5)
+    spread_mid.end(pair_of[0])
+    lift(0)
+    gather(5, 6)
+
+    def grad_down(i, carry):
+        cols = pl.ds(aligned(i * 256, 256), 256)
+        ge[cols] = across(act[:, cols], tree_cot[...].reshape(NSEQ * 128, D)).astype(bf)
+        return carry
+
+    lax.fori_loop(0, 3, grad_down, 0)
+    reduce_(5, 0)
+    gather_end(5)
+
+    def sink(b):
+        here = pl.ds(b * QB, QB)
+        cots = tree_cot[pl.ds(2 * b, 2)].reshape(QB, D)
+
+        def one(t, carry):
+            left = pl.ds(aligned(t * 256, 256), 256)
+            right = pl.ds(aligned(768 + t * 256, 256), 256)
+            d_act = against(cots, we[left])
+            both[here, left] = (d_act * both[here, left].astype(f32)).astype(bf)
+            both[here, right] = (d_act * both[here, right].astype(f32)).astype(bf)
+            return carry
+
+        lax.fori_loop(0, 3, one, 0)
+        part[pl.ds(2 * b, 2)] = against(both[here], wc[...]).astype(bf).reshape(2, NDP, 32, D)
+        mid_sum.start(b)
+        part_out[pl.ds(2 * b, 2)] = product(act[here], we[...]).astype(bf).reshape(2, NDP, 32, D)
+        out_sum.start(b)
+
+    def to_turn(i, rows):
+        unit, scale = unit_of(middle[i])
+        lifted = ffn_g[...] * rows
+        term = jnp.sum(rows * unit, axis=0, keepdims=True)
+        for j in range(8):
+            pack_dp[d, 8 + j : 9 + j] += term[:, 128 * j : 128 * (j + 1)]
+        d_mid = tree_cot[i, d].astype(f32) + scale * (
+            lifted - unit * jnp.mean(unit * lifted, axis=-1, keepdims=True)
+        )
+        d_middle[i] = d_mid
+        d_low[i, d] = d_mid.astype(bf)
+
+    def to_outs(i, rows):
+        outs[i] = (middle[i] + rows).astype(bf)
+
+    back_owner, back_slot = s // MICRO, s % MICRO
+
+    def give(n, src, dst, j, begin):
+        place = dst.at[back_slot, pl.ds(aligned(d * 32, 32), 32)]
+        same = (back_owner == d) & (s == j)
+        cp = pltpu.make_async_remote_copy(
+            src_ref=src.at[j], dst_ref=place, send_sem=s_back.at[n, j], recv_sem=r_back.at[n],
+            device_id=(back_owner, j), device_id_type=MESH,
+        )
+
+        @pl.when(same)
+        def _():
+            if begin:
+                pltpu.make_async_copy(src.at[j], place, r_back.at[n]).start()
+
+        @pl.when(jnp.logical_not(same))
+        def _():
+            if begin:
+                cp.start()
+            else:
+                cp.wait_send()
+
+    sink(3)
+    reduce_(5, 1)
+    sink(2)
+    mid_sum.mid(3)
+    reduce_(5, 2)
+    sink(1)
+    mid_sum.end(3, to_turn)
+    spread_low.start(pair_of[3])
+    mid_sum.mid(2)
+    reduce_(5, 3)
+    sink(0)
+    spread_low.mid(pair_of[3])
+    mid_sum.end(2, to_turn)
+    spread_low.start(pair_of[2])
+    mid_sum.mid(1)
+    reduce_(5, 4)
+    gather_sent(3)
+    gather_sent(4)
+
+    def grad_wide(i):
+        cols = pl.ds(i * 256, 256)
+        for t in range(3):
+            lanes = pl.ds(512 * t, 512)
+            wc[cols, lanes] = across(
+                normed_mid[:, :, :, cols].reshape(NSEQ * 128, 256), both[:, lanes]
+            ).astype(bf)
+
+    grad_wide(0)
+    grad_wide(2)
+    reduce_(3, 0)
+    spread_low.mid(pair_of[2])
+    mid_sum.end(1, to_turn)
+    spread_low.start(pair_of[1])
+    mid_sum.mid(0)
+    reduce_(5, 5)
+    grad_wide(1)
+    grad_wide(3)
+    reduce_(4, 0)
+    spread_low.mid(pair_of[1])
+    mid_sum.end(0, to_turn)
+    spread_low.start(pair_of[0])
+    reduce_(5, 6)
+
+    d_key[...] = jnp.zeros_like(d_key)
+    d_value[...] = jnp.zeros_like(d_value)
+    d_lin = tree
+
+    def open_low(b):
+        here = pl.ds(b * QB, QB)
+        rows = d_low[pl.ds(2 * b, 2)].reshape(QB, D)
+        d_att[here] = against(rows, wb[...]).astype(bf)
+
+    def attend_back(b):
+        here, n = span(b)
+        keys = pl.ds(0, n)
+
+        def one(h, carry):
+            kv = h // 2
+            grown, inverse = weights_of(b, h, n)
+            prob = grown * inverse
+            d_out = d_att[here, head_lanes(h)]
+            d_prob = against(d_out, value[keys, head_lanes(kv)])
+            delta = jnp.sum(prob * d_prob, axis=-1, keepdims=True)
+            d_raw = (prob * (d_prob - delta) * HEAD_DIM ** (-0.5)).astype(bf)
+            d_rot = product(d_raw, key[kv, keys])
+            d_key[kv, keys] += across(d_raw, query[h, here])
+            d_value[kv, keys] += across(prob.astype(bf), d_out)
+            back, d_gain = turn_back(
+                d_rot, lin[here, head_lanes(h)], head_g[0:1, :], cosine[here], sine[here]
+            )
+            pack_dp[d, 16:17] += d_gain
+            d_lin[pl.ds(2 * b, 2), :, :, head_lanes(h)] = back.astype(bf).reshape(2, NDP, 32, HEAD_DIM)
+            return carry
+
+        lax.fori_loop(0, HEADS // NDP, one, 0)
+        for kv in range(KV_HEADS // NDP):
+            back, d_gain = turn_back(
+                d_key[kv, here], lin[here, pl.ds(512 + 128 * kv, 128)], head_g[1:2, :], cosine[here], sine[here]
+            )
+            pack_dp[d, 17:18] += d_gain
+            d_lin[pl.ds(2 * b, 2), :, :, pl.ds(512 + 128 * kv, 128)] = back.astype(bf).reshape(2, NDP, 32, 128)
+            d_lin[pl.ds(2 * b, 2), :, :, pl.ds(768 + 128 * kv, 128)] = (
+                d_value[kv, here].astype(bf).reshape(2, NDP, 32, 128)
+            )
+        rows = against(d_lin[pl.ds(2 * b, 2)].reshape(QB, 1024), wa[...])
+        part[pl.ds(2 * b, 2)] = rows.astype(bf).reshape(2, NDP, 32, D)
+        in_sum.start(b)
+
+    spread_tree.sent(everything)
+    gather_sent(0)
+    gather_sent(1)
+    gather_sent(2)
+    spread_low.end(pair_of[3])
+    open_low(3)
+    attend_back(3)
+    reduce_(3, 1)
+    reduce_(4, 1)
+    spread_low.mid(pair_of[0])
+    for b in (2, 1, 0):
+        spread_low.end(pair_of[b])
+        open_low(b)
+    for i in range(2):
+        cols = pl.ds(256 * i, 256)
+        wb[cols] = across(att[:, cols], d_low[...].reshape(NSEQ * 128, D)).astype(bf)
+    reduce_(2, 0)
+    for b in BLOCKS:
+        out_sum.mid(b)
+    attend_back(2)
+    in_sum.mid(3)
+    reduce_(3, 2)
+    reduce_(4, 2)
+    reduce_(2, 1)
+    for b in BLOCKS:
+        out_sum.end(b, to_outs)
+    for j in range(NSEQ):
+        give(0, outs, out_rows, j, True)
+
+    def to_grad(i, rows):
+        unit, scale = unit_of(tree_own[i].astype(f32))
+        lifted = attn_g[...] * rows
+        term = jnp.sum(rows * unit, axis=0, keepdims=True)
+        for j in range(8):
+            pack_dp[d, j : j + 1] += term[:, 128 * j : 128 * (j + 1)]
+        grad = d_middle[i] + scale * (
+            lifted - unit * jnp.mean(unit * lifted, axis=-1, keepdims=True)
+        )
+        grad_low[i] = grad.astype(bf)
+
+    def close_in(b):
+        in_sum.end(b, to_grad)
+        give(1, grad_low, grad_rows, 2 * b, True)
+        give(1, grad_low, grad_rows, 2 * b + 1, True)
+
+    attend_back(1)
+    close_in(3)
+    in_sum.mid(2)
+    reduce_(3, 3)
+    reduce_(4, 3)
+    reduce_(2, 2)
+    attend_back(0)
+    close_in(2)
+    in_sum.mid(1)
+    reduce_(3, 4)
+    reduce_(4, 4)
+    reduce_(2, 3)
+
+    def grad_attn(i):
+        cols = pl.ds(i * 256, 256)
+        for t in range(2):
+            lanes = pl.ds(512 * t, 512)
+            wa[cols, lanes] = across(
+                normed_in[:, cols], d_lin[:, :, :, lanes].reshape(NSEQ * 128, 512)
+            ).astype(bf)
+
+    grad_attn(0)
+    grad_attn(2)
+    reduce_(0, 0)
+    in_sum.mid(0)
+    close_in(1)
+    grad_attn(1)
+    grad_attn(3)
+    reduce_(1, 0)
+    close_in(0)
+
+    pack_sems, fin_sems = (s_pack, r_pack), (s_fin, r_fin)
+    for i in range(1, NDP):
+        launch(remote(pack_dp.at[d], pack_dp.at[d], pack_sems, i, (d + i) % NDP, s))
+
+    def close_cols(n, fin, landed, which):
+        sub = (n + (n > 2)) % 2
+
+        def take(way, total):
+            fin[2 * way + sub] = total.astype(bf)
+
+        reduce_end(n, take)
+        for way in range(2):
+            q = 2 * way + sub
+
+            @pl.when(q == d)
+            def _():
+                landed[d] = fin[q]
+
+            @pl.when(q != d)
+            def _():
+                remote(fin.at[q], landed.at[d], fin_sems, (which, d), q, s).start()
+
+    def land(fin, landed, which, cuts):
+        for i in range(1, NDP):
+            q = (d + i) % NDP
+            remote(landed.at[q], landed.at[q], fin_sems, (which, q), q, s).wait_recv()
+        for q in range(NDP):
+            for at, width, dst in cuts:
+                dst[:, width * q : width * (q + 1)] = landed[q, :, at : at + width].astype(f32)
+
+    reduce_(2, 4)
+    reduce_(3, 5)
+    reduce_(4, 5)
+    reduce_(0, 1)
+    reduce_(1, 1)
+    for i in range(1, NDP):
+        place = pack_dp.at[(d + NDP - i) % NDP]
+        remote(place, place, pack_sems, i, d, s).wait_recv()
+    pack_seq[s] = (pack_dp[0] + pack_dp[1]) + (pack_dp[2] + pack_dp[3])
+    for i in range(1, NSEQ):
+        launch(remote(pack_seq.at[s], pack_seq.at[s], pack_sems, NDP + i, d, (s + i) % NSEQ))
+    reduce_(2, 5)
+    reduce_(3, 6)
+    reduce_(4, 6)
+    reduce_(0, 2)
+    reduce_(1, 2)
+    reduce_(2, 6)
+    reduce_(0, 3)
+    reduce_(1, 3)
+    close_cols(3, fin_c, got_c, 1)
+    close_cols(4, fin_c, got_c, 1)
+
+    def take_down(way, total):
+        g_down[48 * way : 48 * (way + 1)] = total
+
+    def take_output(way, total):
+        g_output[32 * way : 32 * (way + 1)] = total
+
+    reduce_(0, 4)
+    reduce_(1, 4)
+    reduce_end(5, take_down)
+    reduce_end(2, take_output)
+    reduce_(0, 5)
+    reduce_(1, 5)
+    land(fin_c, got_c, 1, ((0, 768, g_gate), (768, 768, g_up)))
+    reduce_(0, 6)
+    reduce_(1, 6)
+    for i in range(1, NSEQ):
+        place = pack_seq.at[(s + NSEQ - i) % NSEQ]
+        remote(place, place, pack_sems, NDP + i, d, s).wait_recv()
+    total = pack_seq[0]
+    for j in range(1, NSEQ):
+        total = total + pack_seq[j]
+    pack_out[...] = total
+    close_cols(0, fin_a, got_a, 0)
+    close_cols(1, fin_a, got_a, 0)
+    land(fin_a, got_a, 0, ((0, 512, g_query), (512, 256, g_key), (768, 256, g_value)))
+
+    for n, dst in enumerate((out_rows, grad_rows)):
+        pltpu.make_async_copy(dst, dst, r_back.at[n]).wait()
+    for j in range(NSEQ):
+        give(0, outs, out_rows, j, False)
+        give(1, grad_low, grad_rows, j, False)
+    for n, (fin, landed) in enumerate(((fin_a, got_a), (fin_c, got_c))):
+        for i in range(1, NDP):
+            q = (d + i) % NDP
+            remote(fin.at[q], landed.at[d], fin_sems, (n, d), q, s).wait_send()
+    gather_sent(5)
+    for n in range(6):
+        reduce_sent(n)
+    spread_cot.sent(everything)
+    for b in BLOCKS:
+        spread_mid.sent(pair_of[b])
+        spread_low.sent(pair_of[b])
+    for cp in pending:
+        cp.wait_send()
+    for n in range(2):
+        for m in range(MICRO):
+
+            @pl.when(MICRO * d + m != s)
+            def _():
+                place = tree.at[s, d]
+                pltpu.make_async_remote_copy(
+                    src_ref=place, dst_ref=place, send_sem=s_tok.at[n, m, 0], recv_sem=r_tok.at[n],
+                    device_id=(d, s), device_id_type=MESH,
+                ).wait_send()
+
+
+def tree_shards(
+    tokens, cotangent, node_lengths, parents, w_query, w_key, w_value, w_output, w_gate, w_up, w_down,
+    attn_gain, ffn_gain, query_gain, key_gain,
+):
+    f32, bf = jnp.float32, jnp.bfloat16
+    d, s = lax.axis_index("dp"), lax.axis_index("seq")
+    nodes = node_lengths.shape[2]
+    wide = ((0, 0), (0, 128 - nodes))
+    small = jnp.concatenate(
+        [
+            jnp.tile(attn_gain.astype(f32), 4)[None],
+            jnp.tile(ffn_gain.astype(f32), 4)[None],
+            jnp.tile(query_gain.astype(f32), 32)[None],
+            jnp.tile(key_gain.astype(f32), 32)[None],
+            jnp.pad(node_lengths[0].astype(f32), wide),
+            jnp.pad(parents[0].astype(f32), wide),
+        ]
+    )
+    half = jnp.arange(HEAD_DIM // 2, dtype=f32)
+    inv_freq = THETA ** (-(half * (2.0 / HEAD_DIM)))
+    inv_freq = jnp.concatenate([inv_freq, inv_freq])[None]
+    shape, vmem, dma = jax.ShapeDtypeStruct, pltpu.VMEM, pltpu.SemaphoreType.DMA
+    anywhere = pl.BlockSpec(memory_space=pl.ANY)
+    here = pl.BlockSpec(memory_space=pltpu.VMEM)
+    rows = NSEQ * 128
+    quarter = (NSEQ, 32, D)
+    twice = lambda *dims: [dma(dims), dma(dims)]
+    results = pl.pallas_call(
+        functools.partial(layer_kernel, nodes),
+        out_shape=(
+            shape((MICRO, 128, D), bf),
+            shape((MICRO, 128, D), bf),
+            shape((24, 128), f32),
+            shape((32, 2048), f32),
+            shape((32, 1024), f32),
+            shape((32, 1024), f32),
+            shape((64, D), f32),
+            shape((32, FF), f32),
+            shape((32, FF), f32),
+            shape((96, D), f32),
+        ),
+        in_specs=[anywhere] * 3 + [here] + [anywhere] * 7,
+        out_specs=[anywhere] * 2 + [here] * 8,
+        scratch_shapes=[
+            vmem((NDP, NSEQ, 8, 128), f32),
+            vmem((D, 1024), bf), vmem((512, D), bf), vmem((D, 1536), bf), vmem((768, D), bf),
+            vmem((768, D), bf),
+            vmem((2, 2, 7, 32, 1024), bf), vmem((2, 7, 32, D), bf),
+            vmem((2, 2, 7, 32, 1536), bf), vmem((2, 7, 48, D), bf),
+            vmem((NSEQ, NDP, 32, D), bf), vmem((NSEQ, NDP, 32, D), bf), vmem((rows, D), bf),
+            vmem((NSEQ, NDP, 32, D), bf), vmem((NSEQ, NDP, 32, D), bf), vmem(quarter, bf),
+            vmem((rows, 768), f32), vmem((4, rows, 128), bf), vmem((2, rows, 128), bf),
+            vmem((rows, 256), bf), vmem((rows, 128), bf), vmem((rows, 128), bf),
+            vmem((rows, 128), f32), vmem((rows, 128), f32), vmem((rows, 512), bf), vmem((rows, 512), bf),
+            vmem((NSEQ, NDP, 32, D), bf), vmem((NSEQ, NDP, 32, D), bf),
+            vmem((2,) + quarter, bf), vmem(quarter, bf), vmem(quarter, bf),
+            vmem((2,) + quarter, bf), vmem(quarter, bf), vmem(quarter, bf),
+            vmem(quarter, f32), vmem(quarter, f32), vmem((rows, 768), bf), vmem((rows, 1536), bf),
+            vmem((2, rows, 128), f32), vmem((2, rows, 128), f32), vmem(quarter, bf), vmem(quarter, bf),
+            vmem((NDP, 32, 1024), bf), vmem((NDP, 32, 1536), bf),
+            vmem((NDP, 32, 1024), bf), vmem((NDP, 32, 1536), bf),
+            vmem((1, D), f32), vmem((1, D), f32), vmem((8, 128), f32),
+            vmem((NDP, 24, 128), f32), vmem((NSEQ, 24, 128), f32),
+            dma((9,)),
+            *twice(12), *twice(5, NDP), dma((2, MICRO, NDP)), dma((2,)),
+            *twice(6, 2, 7), *twice(6, 2, 7),
+            *twice(4, 3, 4), *twice(2, 3), *twice(2, 3, 4),
+            dma((2, NSEQ)), dma((2,)), *twice(2, NDP), *twice(12),
+        ],
+        compiler_params=pltpu.CompilerParams(
+            collective_id=1, has_side_effects=True, vmem_limit_bytes=61 << 20
+        ),
+        name="layer",
+    )(
+        tokens[0], cotangent[0], small, inv_freq,
+        w_query, w_key, w_value, w_output, w_gate, w_up, w_down,
+    )
+    out_rows, grad_rows, pack, g_query, g_key, g_value, g_output, g_gate, g_up, g_down = results
+    at = d * NSEQ + s
+    own = lambda piece, n: lax.dynamic_slice_in_dim(piece.reshape(-1), at * n, n)
+    return (
+        out_rows[None],
+        grad_rows[None].astype(f32),
+        g_query, g_key, g_value, g_output, g_gate, g_up, g_down,
+        own(pack[:8], 32),
+        own(pack[8:16], 32),
+        own(pack[16], 4),
+        own(pack[17], 4),
+    )
+
+
 def solution(mesh):
+    ring = mesh.shape["dp"] == NDP and mesh.shape["seq"] == NSEQ
     return jax.shard_map(
-        shards,
+        tree_shards if ring else general_shards,
         mesh=mesh,
         in_specs=(
             P("dp", None, "seq", None),

time: 2190 us -> 312 us (0.14)
  waiting for transfers between devices: 1590 us -> 0 us
  Pallas kernels: 0 us -> 293 us
  matrix products: 228 us -> 0 us
  local copies, waits for them, and re-layouts: 183 us -> 13.7 us
  blocking collectives: 82.8 us -> 0 us
  loops' own time: 38.4 us -> 0 us
  other arithmetic: 41 us -> 2.78 us
    reduce_scatter x7 -> x0, waiting for transfers between devices: 1060 us -> none  [the longest x1 187 us: shards(): lax.psum_scatter(sums[3], ('dp', 'seq'), scatter_dimension=0, tiled=True)]
    all_gather x11 -> x0, waiting for transfers between devices: 489 us -> none  [the longest x2 82.4 us: shards(): lax.all_gather(value_low, 'seq', axis=0, tiled=True)]
    pallas_call x0 -> x1, Pallas kernels: none -> 293 us  [tree_shards(): pl.pallas_call(functools.partial(layer_kernel, nodes), out_shape=(shape((...]
    dot_general x104 -> x0, matrix products: 228 us -> none  [the longest x14 45.2 us: across(): lax.dot_general(left_side, right_side, (((0,), (0,)), ((), ())), preferre...]
    unnamed x2 -> x0, blocking collectives: 82.8 us -> none
    dynamic_slice x64 -> x3, local copies, waits for them, and re-layouts: 82.8 us -> 1.75 us  [tree_shards(): lax.dynamic_slice_in_dim(piece.reshape(-1), at * n, n)]
    unnamed x273 -> x38, local copies, waits for them, and re-layouts: 58.3 us -> 10.9 us
    another operation x6 -> x0, loops' own time: 38.4 us -> none  [the longest x2 26.5 us: shards(): d_query_pairs, kv_terms = lax.map(back_pair, pair_ids)]
  transfers between devices with their start and end apart: 20 -> 0, of which waited for: 19 -> 0; matrix products, arithmetic and copies ran while one was open for 14% -> 0% of each run, Pallas kernels for 0% -> 0%
where the time goes in v2:
time: 312 us; the launch traced here: 310 us
  Pallas kernels  293 us (94%)
  local copies, waits for them, and re-layouts  13.7 us (4%)
    pallas_call x1, Pallas kernels, tree_shards(): pl.pallas_call(functools.partial(layer_kernel, nodes), out_shape=(shape((...  293 us
    unnamed x38, local copies, waits for them, and re-layouts  10.9 us

profile of v2, /device:TPU:21, one launch (start us, length us, event | category | flops | bytes accessed | tf_op | source)
XLA Modules:
  0.0 309.9 jit_solution(16836114936382739185)
XLA Ops:
  0.7 0.0 copy-start.9
  0.7 0.6 maximum_bitcast_fusion.inv_freq
  1.3 0.1 copy-done.9
  1.3 0.0 copy-start.10
  1.4 0.7 copy-done.10
  2.0 0.0 copy-start.11
  2.0 0.6 copy-done.11
  2.7 0.0 copy-start.12
  2.7 0.1 broadcast_in_dim_tile.12
  2.8 0.6 copy-done.12
  3.4 0.0 copy-start.13
  3.4 0.1 broadcast_in_dim_tile.13
  3.4 0.6 copy-done.13
  4.0 0.0 copy-start.14
  4.0 0.1 broadcast_in_dim_tile.14
  4.1 0.5 copy-done.14
  4.7 0.1 broadcast_in_dim_tile.15
  4.8 0.6 concatenate.6.small
  5.4 292.7 %layer.1 = (bf16[2,128,1024]{2,1,0:T(8,128)(2,1)}, bf16[2,128,1024]{2,1,0:T(8,128)(2,1)}, f32[24,128]{1,0:T(8,128)}, f32[32,2048]{1,0:T(8,128)}, f32[32,1024]{1,...) custom-call(bf16[2,128,1024]{2,1,0:T(8,128)(2,1)} %bitcast.20, ...), custom_call_target="tpu_custom_call" | custom-call | tf_op jit(solution)/shard_map/layer/pallas_call | solution.py:1289
  298.1 0.0 copy-start.8
  298.1 0.7 copy-done.8
  298.8 0.6 dynamic_slice.17
  299.4 0.6 dynamic_slice.16
  300.0 0.6 dynamic-slice_bitcast_fusion
  300.5 0.0 copy-start
  300.5 2.2 bitcast_convert_fusion
  302.7 0.0 copy-done
  302.7 0.0 copy-start.5
  302.7 0.8 copy.36
  303.5 0.3 copy-done.5
  303.8 0.0 copy-start.7
  303.8 0.0 copy-start.6
  303.8 0.7 copy.37
  304.5 0.3 copy-done.7
  304.8 0.0 copy-start.4
  304.8 0.7 copy.38
  305.5 0.0 copy-done.6
  305.5 0.0 copy-start.3
  305.5 0.7 copy.39
  306.1 0.0 copy-done.4
  306.1 0.7 copy.40
  306.8 0.0 copy-done.3
  306.8 0.0 copy-start.2
  306.8 0.7 copy.41
  307.6 0.4 copy-done.2
  308.0 0.7 copy.42
  308.7 0.4 copy-done.1
  309.1 0.7 copy.43
  (12 shorter events, 0.0 us)
Async XLA Ops:
  0.7 0.7 copy-start.9
  1.3 0.7 copy-start.10
  2.0 0.7 copy-start.11
  2.7 0.7 copy-start.12
  3.4 0.7 copy-start.13
  4.0 0.7 copy-start.14
  298.1 0.7 copy-start.8
  300.5 2.2 copy-start
  302.7 1.1 copy-start.5
  303.8 1.0 copy-start.7
  303.8 1.7 copy-start.6
  304.8 1.3 copy-start.4
  305.5 1.4 copy-start.3
  306.8 1.1 copy-start.2
  308.0 1.1 copy-start.1

commit v3 on v0

--- a/solution.py
+++ b/solution.py
@@ -1,6 +1,11 @@
+import functools
+
 import jax
 import jax.numpy as jnp
+import numpy as np
 from jax import lax
+from jax.experimental import pallas as pl
+from jax.experimental.pallas import tpu as pltpu
 from jax.sharding import PartitionSpec as P
 
 D = 1024
@@ -91,7 +96,7 @@
     )
 
 
-def shards(
+def general_shards(
     tokens,
     cotangent,
     node_lengths,
@@ -384,9 +389,1055 @@
     )
 
 
+MESH = pl.DeviceIdType.MESH
+NDP = 4
+NSEQ = 8
+BLOCKED = -65536.0
+QB = 256
+BLOCKS = (3, 2, 1, 0)
+SOFT = HEAD_DIM ** (-0.5) * 1.4426950408889634
+
+A0, A1, B, C0, C1, E = range(0, 60, 10)
+R_A0, R_A1, R_B, R_C0, R_C1, R_E = range(60, 120, 10)
+(
+    ATTEND, MIX_MID, MIX_END, NORM_MID, NORM_END, LIFT, SINK, TURN_MID, TURN_END, LOW_MID, LOW_END,
+    OUT_START, OUT_MID, OUT_END, ATTEND_BACK, IN_START, IN_MID, IN_END, PROJECT, GRAD_WIDE,
+    GRAD_ATTN, TABLES, NORM_IN,
+) = range(200, 430, 10)
+(
+    START, TOKENS, COTANGENT, SMALL_DP, SMALL_SEQ, A_IN, C_OUT, C_IN, TREE_START, COT_START,
+    TREE_MID, COT_MID, COT_END, TREE_END, NODE, GAINS, GRAD_DOWN, GRAD_OUT, PACK_DP, PACK_SEQ,
+    PACK_END, LAND_A, LAND_C, DRAIN,
+) = range(600, 624, 1)
+ORDER = (
+    START, B, TOKENS, SMALL_DP, A_IN, A1, B + 1, A0, C_OUT, A1 + 1, C_IN, TREE_START, B + 2, A0 + 1,
+    SMALL_SEQ, A1 + 2, NODE, B + 3, TABLES, A0 + 2, A1 + 3, C1, A0 + 3, A1 + 4, B + 4, A0 + 4, TREE_MID,
+    A1 + 5, C0, TABLES + 1, A0 + 5, B + 5, TREE_END, GAINS, A1 + 6, A0 + 6, NORM_IN, B + 6, C0 + 1, C1 + 1,
+    NORM_IN + 1, A1 + 7, COTANGENT, B + 7, A0 + 7, PROJECT, PROJECT + 1, PROJECT + 2, PROJECT + 3, ATTEND + 3,
+    ATTEND + 2, C0 + 2, C1 + 2, MIX_MID + 3, MIX_MID + 2, ATTEND + 1, E, MIX_MID + 1, ATTEND, C0 + 3, C1 + 3,
+    MIX_MID, E + 1, MIX_END + 1, MIX_END + 2, C0 + 4, MIX_END + 3, C1 + 4, MIX_END, E + 2, COT_START, C0 + 5,
+    NORM_MID + 2, C1 + 5, NORM_MID + 3, E + 3, NORM_MID, NORM_MID + 1, NORM_END + 3, C0 + 6, NORM_END,
+    NORM_END + 1, C1 + 6, E + 4, NORM_END + 2, C0 + 7, C1 + 7, LIFT + 2, E + 5, COT_MID, LIFT + 1, LIFT + 3,
+    COT_END, E + 6, LIFT, GRAD_DOWN, R_E, E + 7, SINK + 3, OUT_START + 3, SINK + 1, OUT_START + 1, R_E + 1,
+    SINK, OUT_START, TURN_MID + 3, SINK + 2, OUT_START + 2, R_E + 2, OUT_MID + 3, GRAD_WIDE, R_C0,
+    OUT_MID + 1, GRAD_WIDE + 1, R_C1, TURN_END + 3, R_E + 3, TURN_MID + 2, R_C0 + 1, R_C1 + 1, LOW_MID + 3,
+    OUT_END + 1, TURN_MID, LOW_END + 3, TURN_MID + 1, R_C0 + 2, TURN_END + 2, OUT_MID, R_C1 + 2, OUT_END + 3,
+    ATTEND_BACK + 3, IN_START + 3, R_C0 + 3, R_C1 + 3, LOW_MID + 2, TURN_END, TURN_END + 1, IN_MID + 3,
+    LOW_END + 2, R_E + 4, R_C0 + 4, OUT_END, R_C1 + 4, ATTEND_BACK + 2, IN_START + 2, R_C0 + 5, R_E + 5,
+    LOW_MID + 1, LOW_MID, IN_END + 3, IN_MID + 2, R_C1 + 5, LOW_END + 1, ATTEND_BACK + 1, IN_START + 1,
+    R_C0 + 6, R_E + 6, LOW_END, GRAD_OUT, IN_END + 2, R_B, ATTEND_BACK, IN_START, IN_MID + 1, GRAD_ATTN + 1,
+    R_A1, GRAD_ATTN, R_A0, R_C1 + 6, R_A1 + 1, R_A0 + 1, R_B + 1, R_C0 + 7, OUT_MID + 2, R_A1 + 2, R_A0 + 2,
+    IN_END + 1, R_A1 + 3, IN_MID, R_B + 2, R_A0 + 3, R_A1 + 4, R_B + 3, R_A0 + 4, R_C1 + 7, R_A1 + 5, R_E + 7,
+    R_B + 4, R_A0 + 5, R_A1 + 6, R_B + 5, LAND_C, R_A0 + 6, IN_END, PACK_DP, R_A1 + 7, R_B + 6, R_A0 + 7,
+    PACK_SEQ, OUT_END + 2, PACK_END, R_B + 7, LAND_A, DRAIN,
+)
+
+
+def seq_at(position):
+    half = position // 4
+    z = position + half * (7 - 2 * position)
+    return 2 * z + half
+
+
+def tree_seat(d, m):
+    x, c = d // 2, d % 2
+    return 2 * (2 * m + c) + (m + c + x) % 2
+
+
+def greet_all(d, s):
+    barrier = pltpu.get_barrier_semaphore()
+    me = d * NSEQ + s
+
+    def signal(i, carry):
+        other = (me + i) % (NDP * NSEQ)
+        pl.semaphore_signal(
+            barrier, inc=1, device_id=(other // NSEQ, other % NSEQ), device_id_type=MESH
+        )
+        return carry
+
+    lax.fori_loop(1, NDP * NSEQ, signal, 0)
+    pl.semaphore_wait(barrier, NDP * NSEQ - 1)
+
+
+def remote(src, dst, sems, at, d, s):
+    send, recv = sems
+    return pltpu.make_async_remote_copy(
+        src_ref=src,
+        dst_ref=dst,
+        send_sem=send.at[at],
+        recv_sem=recv.at[at],
+        device_id=(d, s),
+        device_id_type=MESH,
+    )
+
+
+class Sum:
+    def __init__(self, part, near, sent, got, sems, n, spot):
+        self.part, self.near, self.sent, self.got = part, near, sent, got
+        self.sems, self.n = sems, n
+        d, self.s = spot
+        x, c = d // 2, d % 2
+        self.d, self.sib, self.far = d, 2 * x + 1 - c, 2 * (1 - x) + c
+        self.far_sib = 2 * (1 - x) + 1 - c
+
+    def copies(self, b):
+        rows = pl.ds(2 * b, 2)
+        return (
+            remote(self.part.at[rows, self.far_sib], self.near.at[0, rows], self.sems, (self.n, 0, b), self.sib, self.s),
+            remote(self.part.at[rows, self.sib], self.near.at[1, rows], self.sems, (self.n, 1, b), self.sib, self.s),
+            remote(self.sent.at[rows], self.got.at[rows], self.sems, (self.n, 2, b), self.far, self.s),
+        )
+
+    def start(self, b):
+        first, second, _ = self.copies(b)
+        first.start()
+        second.start()
+
+    def mid(self, b):
+        first, _, across_x = self.copies(b)
+        first.wait_recv()
+
+        def join(i, carry):
+            self.sent[i] = (
+                self.part[i, self.far].astype(jnp.float32) + self.near[0, i].astype(jnp.float32)
+            ).astype(jnp.bfloat16)
+            return carry
+
+        lax.fori_loop(2 * b, 2 * b + 2, join, 0)
+        across_x.start()
+
+    def end(self, b, finish):
+        first, second, across_x = self.copies(b)
+        second.wait_recv()
+        across_x.wait_recv()
+
+        def close(i, carry):
+            rows = self.part[i, self.d].astype(jnp.float32) + self.near[1, i].astype(jnp.float32)
+            finish(i, rows + self.got[i].astype(jnp.float32))
+            return carry
+
+        lax.fori_loop(2 * b, 2 * b + 2, close, 0)
+        first.wait_send()
+        second.wait_send()
+        across_x.wait_send()
+
+
+class Spread:
+    def __init__(self, out, sems, at, spot):
+        self.out, self.sems, self.place = out, sems, at
+        d, self.s = spot
+        x, c = d // 2, d % 2
+        self.d, self.sib, self.far = d, 2 * x + 1 - c, 2 * (1 - x) + c
+        self.far_sib = 2 * (1 - x) + 1 - c
+
+    def copy(self, rows, owner, way, to):
+        block = self.out.at[rows, owner]
+        return remote(block, block, self.sems, self.place(way, rows), to, self.s)
+
+    def start(self, rows):
+        self.copy(rows, self.d, 0, self.far).start()
+        self.copy(rows, self.d, 1, self.sib).start()
+
+    def mid(self, rows):
+        self.copy(rows, self.far, 0, self.far).wait_recv()
+        self.copy(rows, self.far, 2, self.sib).start()
+
+    def end(self, rows):
+        self.copy(rows, self.sib, 1, self.sib).wait_recv()
+        self.copy(rows, self.far_sib, 2, self.sib).wait_recv()
+
+    def sent(self, rows):
+        self.copy(rows, self.d, 0, self.far).wait_send()
+        self.copy(rows, self.d, 1, self.sib).wait_send()
+        self.copy(rows, self.far, 2, self.sib).wait_send()
+
+
+def layer_kernel(
+    nodes,
+    tok, cot, lengths, parents, gain_a, gain_f, gain_q, gain_k, inv_freq, wq, wk, wv, wo, wg, wu, wd,
+    out_rows, grad_rows, res_a, res_c, g_output, g_down, pack_out,
+    raw_lengths, raw_parents, raw_a, raw_f, raw_q, raw_k, smalls, wa, wb, wc, we, ge, hop_a, hop_b, hop_c, hop_e,
+    tree, tree_cot, normed_in, normed_mid, d_low, tree_own,
+    lin, heads, value, hidden, member, cosine, sine, att, d_att,
+    part, part_out, near, sent, got, near_o, sent_o, got_o,
+    middle, d_middle, act, both, d_key, d_value, outs, grad_low,
+    fin_a, fin_c, attn_g, ffn_g, head_g, pack_dp, pack_seq, pack_sum,
+    loc, s_small, r_small, s_col, r_col, s_tok, r_tok, s_ag, r_ag, s_rs, r_rs,
+    s_sum, r_sum, s_tree, r_tree, s_spread, r_spread, s_back, r_back, s_fin, r_fin, s_pack, r_pack,
+):
+    f32, bf = jnp.float32, jnp.bfloat16
+    d = lax.axis_index("dp")
+    s = lax.axis_index("seq")
+    z, y = s // 2, s % 2
+    p = z + y * (7 - 2 * z)
+    spot = (d, s)
+    seat = [seq_at((p + i) % NSEQ) for i in range(NSEQ)]
+    up, down = seat[1], seat[7]
+    ag_sems, rs_sems = (s_ag, r_ag), (s_rs, r_rs)
+    small_sems, col_sems, tok_sems = (s_small, r_small), (s_col, r_col), (s_tok, r_tok)
+
+    def aligned(v, n):
+        return pl.multiple_of(v, n)
+
+    def chunk(n, way, j):
+        if n in (0, 1, 3, 4):
+            return pl.ds(aligned((2 * way + (n + (n > 2)) % 2) * 256 + j * 32, 32), 32)
+        if n == 2:
+            return pl.ds(aligned(j * 64 + way * 32, 32), 32)
+        return pl.ds(aligned(j * 96 + way * 48, 16), 48)
+
+    weight = {0: wa, 1: wa, 2: wb, 3: wc, 4: wc, 5: we}
+    grads = {0: wa, 1: wa, 2: wb, 3: wc, 4: wc, 5: ge}
+    hops = {0: hop_a.at[0], 1: hop_a.at[1], 2: hop_b, 3: hop_c.at[0], 4: hop_c.at[1], 5: hop_e}
+
+    def owner_at(way, k):
+        return seq_at((p + NSEQ - k) % NSEQ) if way == 0 else seq_at((p + k) % NSEQ)
+
+    def gather(n, k):
+        for way, peer in enumerate((up, down)):
+            block = weight[n].at[chunk(n, way, owner_at(way, k))]
+            if not (isinstance(k, int) and k == 0):
+                remote(block, block, ag_sems, (n, way, k - 1), d, peer).wait_recv()
+            remote(block, block, ag_sems, (n, way, k), d, peer).start()
+
+    def gather_end(n):
+        for way, peer in enumerate((up, down)):
+            block = weight[n].at[chunk(n, way, owner_at(way, 7))]
+            remote(block, block, ag_sems, (n, way, 6), d, peer).wait_recv()
+
+    def gather_sent(n):
+        for way, peer in enumerate((up, down)):
+            block = weight[n].at[chunk(n, way, s)]
+            for k in range(7):
+                remote(block, block, ag_sems, (n, way, k), d, peer).wait_send()
+
+    def add_rows(into, other):
+        def one(i, carry):
+            at = pl.ds(aligned(i * 16, 16), 16)
+            into[at] = (into[at].astype(f32) + other[at].astype(f32)).astype(bf)
+            return carry
+
+        lax.fori_loop(0, into.shape[0] // 16, one, 0)
+
+    def reduce_(n, k):
+        for way, peer in enumerate((up, down)):
+            rows = chunk(n, way, seat[(7 - k) % NSEQ] if way == 0 else seat[(1 + k) % NSEQ])
+            mine = grads[n].at[rows]
+            if k == 0:
+                src = mine
+            else:
+                src = hops[n].at[way, k - 1]
+                remote(src, src, rs_sems, (n, way, k - 1), d, peer).wait_recv()
+                add_rows(src, mine)
+            remote(src, hops[n].at[way, k], rs_sems, (n, way, k), d, peer).start()
+
+    def reduce_end(n, take):
+        for way, peer in enumerate((up, down)):
+            src = hops[n].at[way, 6]
+            remote(src, src, rs_sems, (n, way, 6), d, peer).wait_recv()
+            take(way, src[...].astype(f32) + grads[n][chunk(n, way, s)].astype(f32))
+
+    def reduce_sent(n):
+        for way, peer in enumerate((up, down)):
+            for k in range(7):
+                src = hops[n].at[way, k]
+                remote(src, src, rs_sems, (n, way, k), d, peer).wait_send()
+
+    ops = {}
+    tree_slot, tree_core = z // 2, z % 2
+    tree_owner = 2 * ((y + tree_slot + tree_core) % 2) + tree_core
+    pending = []
+    held = {}
+
+    def stage(name):
+        def keep(run):
+            ops[name] = run
+            return run
+
+        return keep
+
+    def launch(cp):
+        cp.start()
+        pending.append(cp)
+
+    raws = [
+        pltpu.make_async_copy(src, dst, loc.at[9 + n])
+        for n, (src, dst) in enumerate(
+            (
+                (lengths, raw_lengths), (parents, raw_parents),
+                (gain_a, raw_a), (gain_f, raw_f), (gain_q, raw_q), (gain_k, raw_k),
+            )
+        )
+    ]
+    pieces = (
+        (wq, wa, 512, 0), (wk, wa, 256, 512), (wv, wa, 256, 768), (wg, wc, 768, 0), (wu, wc, 768, 768)
+    )
+    col_rows = lambda q: pl.ds(aligned(q * 256 + s * 32, 32), 32)
+
+    def column_copy(n):
+        src, dst, width, at = pieces[n]
+        return pltpu.make_async_copy(
+            src.at[:, pl.ds(aligned(d * width, 128), width)],
+            dst.at[col_rows(d), pl.ds(at, width)],
+            loc.at[2 + n],
+        )
+
+    def columns(n):
+        src, dst, width, at = pieces[n]
+        for i in range(1, NDP):
+            q = (d + i) % NDP
+            launch(
+                remote(
+                    src.at[:, pl.ds(aligned(q * width, 128), width)],
+                    dst.at[col_rows(d), pl.ds(at, width)],
+                    col_sems, (n, i), q, s,
+                )
+            )
+        column_copy(n).start()
+
+    def columns_in(n):
+        _, dst, width, at = pieces[n]
+        column_copy(n).wait()
+        for i in range(1, NDP):
+            place = dst.at[col_rows((d + NDP - i) % NDP), pl.ds(at, width)]
+            remote(place, place, col_sems, (n, i), d, s).wait_recv()
+
+    def row_copy(n, m, i):
+        src, dst = ((tok, tree), (cot, tree_cot))[n]
+        q = (d + i) % NDP
+        return pltpu.make_async_remote_copy(
+            src_ref=src.at[m, pl.ds(aligned(q * 32, 32), 32)],
+            dst_ref=dst.at[s, q],
+            send_sem=s_tok.at[n, m, i],
+            recv_sem=r_tok.at[n],
+            device_id=(q, tree_seat(d, m)),
+            device_id_type=MESH,
+        )
+
+    def rows_out(n):
+        src, dst = ((tok, tree), (cot, tree_cot))[n]
+        for m in range(MICRO):
+            target = tree_seat(d, m)
+
+            @pl.when(target == s)
+            def _():
+                piece = src.at[m, pl.ds(aligned(d * 32, 32), 32)]
+                pltpu.make_async_copy(piece, dst.at[s, d], r_tok.at[n]).start()
+
+            @pl.when(target != s)
+            def _():
+                row_copy(n, m, 0).start()
+
+            for i in range(1, NDP):
+                row_copy(n, m, i).start()
+
+    def rows_in(dst, n):
+        everything = dst.at[:, d]
+        pltpu.make_async_copy(everything, everything, r_tok.at[n]).wait()
+
+    fill_b = pltpu.make_async_copy(wo, wb.at[pl.ds(aligned(s * 64, 64), 64)], loc.at[7])
+    fill_e = pltpu.make_async_copy(wd, we.at[pl.ds(aligned(s * 96, 16), 96)], loc.at[15])
+
+    @stage(START)
+    def _():
+        for cp in raws:
+            cp.start()
+        greet_all(d, s)
+        fill_b.start()
+        fill_e.start()
+        for n in range(3):
+            columns(n)
+
+    stage(TOKENS)(lambda: rows_out(0))
+    stage(COTANGENT)(lambda: rows_out(1))
+
+    @stage(SMALL_DP)
+    def _():
+        for cp in raws:
+            cp.wait()
+        for row, ref in enumerate((raw_a, raw_f, raw_q, raw_k)):
+            count = ref.shape[0]
+            line = ref[...].astype(f32).reshape(1, count)
+            smalls[d, s, row : row + 1, :] = jnp.concatenate([line] * (128 // count), axis=1)
+        smalls[d, s, 4:8, :] = jnp.zeros((4, 128), f32)
+        smalls[d, s, 4:6, 0:nodes] = raw_lengths[0].astype(f32)
+        smalls[d, s, 6:8, 0:nodes] = raw_parents[0].astype(f32)
+        for i in range(1, NDP):
+            launch(remote(smalls.at[d, s], smalls.at[d, s], small_sems, i, (d + i) % NDP, s))
+
+    @stage(SMALL_SEQ)
+    def _():
+        for i in range(1, NDP):
+            place = smalls.at[(d + NDP - i) % NDP, s]
+            remote(place, place, small_sems, i, d, s).wait_recv()
+        for i in range(1, NSEQ):
+            launch(remote(smalls.at[:, s], smalls.at[:, s], small_sems, NDP + i, d, (s + i) % NSEQ))
+
+    @stage(A_IN)
+    def _():
+        for n in range(3):
+            columns_in(n)
+
+    @stage(C_OUT)
+    def _():
+        for n in range(3, 5):
+            columns(n)
+
+    @stage(C_IN)
+    def _():
+        for n in range(3, 5):
+            columns_in(n)
+
+    streams = ((A0, 0), (A1, 1), (B, 2), (C0, 3), (C1, 4), (E, 5))
+
+    def ring_first(n):
+        if n == 2:
+            fill_b.wait()
+        if n == 5:
+            fill_e.wait()
+        gather(n, 0)
+
+    for label, n in streams:
+        stage(label)(functools.partial(ring_first, n))
+        stage(label + 7)(functools.partial(gather_end, n))
+        for k in range(1, 7):
+            stage(label + k)(functools.partial(gather, n, k))
+        for k in range(7):
+            stage(R_A0 + label + k)(functools.partial(reduce_, n, k))
+
+    everything = pl.ds(0, NSEQ)
+    spread_tree = Spread(tree, (s_tree, r_tree), lambda way, rows: (0, way), spot)
+    spread_cot = Spread(tree_cot, (s_tree, r_tree), lambda way, rows: (1, way), spot)
+
+    @stage(TREE_START)
+    def _():
+        rows_in(tree, 0)
+        spread_tree.start(everything)
+
+    @stage(COT_START)
+    def _():
+        rows_in(tree_cot, 1)
+        spread_cot.start(everything)
+
+    stage(TREE_MID)(lambda: spread_tree.mid(everything))
+    stage(COT_MID)(lambda: spread_cot.mid(everything))
+    stage(COT_END)(lambda: spread_cot.end(everything))
+    own_rows = pltpu.make_async_copy(tree.at[:, d], tree_own, loc.at[8])
+
+    @stage(TREE_END)
+    def _():
+        spread_tree.end(everything)
+        own_rows.start()
+
+    @stage(NODE)
+    def _():
+        ir = lax.broadcasted_iota(jnp.int32, (128, 128), 0)
+        ic = lax.broadcasted_iota(jnp.int32, (128, 128), 1)
+        block = smalls.at[tree_owner, s]
+        length_row = block[pl.ds(4 + tree_slot, 1), :]
+        parent_row = block[pl.ds(6 + tree_slot, 1), :]
+        length_col = jnp.sum(jnp.where(ir == ic, length_row, 0.0), axis=1, keepdims=True)
+        over = (parent_row == ir.astype(f32)) & (ic > 0) & (ic < nodes)
+        above = jnp.where(over | (ir == ic), 1.0, 0.0)
+        for _ in range(4):
+            low = above.astype(bf)
+            above = jnp.minimum(product(low, low), 1.0)
+        start_row = jnp.sum(jnp.where(ir < ic, length_col, 0.0), axis=0, keepdims=True)
+        base_row = jnp.sum(
+            jnp.where((above > 0.5) & (ir != ic), length_col, 0.0), axis=0, keepdims=True
+        )
+        shut = jnp.where(above > 0.5, 0.0, BLOCKED).astype(bf)
+        held["node"] = (start_row, start_row + length_row, base_row - start_row, shut)
+
+    def tables(i, carry):
+        start_row, end_row, offset_row, shut = held["node"]
+        rows = pl.ds(aligned(i * QB, QB), QB)
+        index = (lax.broadcasted_iota(jnp.int32, (QB, 128), 0) + i * QB).astype(f32)
+        inside = (index >= start_row) & (index < end_row)
+        position = index[:, :1] + jnp.sum(
+            jnp.where(inside, offset_row, 0.0), axis=1, keepdims=True
+        )
+        hot = jnp.where(inside, 1.0, 0.0).astype(bf)
+        member[rows] = hot
+        hidden[rows] = against(hot, shut).astype(bf)
+        angle = position * inv_freq[...]
+        cosine[rows] = jnp.cos(angle)
+        lane = lax.broadcasted_iota(jnp.int32, (QB, 128), 1)
+        wave = jnp.sin(angle)
+        sine[rows] = jnp.where(lane < 64, -wave, wave)
+        return carry
+
+    stage(TABLES + 0)(lambda: lax.fori_loop(0, 2, tables, 0))
+    stage(TABLES + 1)(lambda: lax.fori_loop(2, 4, tables, 0))
+
+    @stage(GAINS)
+    def _():
+        for i in range(1, NSEQ):
+            place = smalls.at[:, (s + NSEQ - i) % NSEQ]
+            remote(place, place, small_sems, NDP + i, d, s).wait_recv()
+        lane = lax.broadcasted_iota(jnp.int32, (1, 128), 1)
+        for row, dst in ((0, attn_g), (1, ffn_g)):
+            for j in range(8):
+                parts = [
+                    smalls[(4 * j + i) // 8, (4 * j + i) % 8, row : row + 1, :] for i in range(4)
+                ]
+                dst[:, 128 * j : 128 * (j + 1)] = jnp.where(
+                    lane < 64,
+                    jnp.where(lane < 32, parts[0], parts[1]),
+                    jnp.where(lane < 96, parts[2], parts[3]),
+                )
+        for row in (2, 3):
+            joined = jnp.zeros((1, 128), f32)
+            for i in range(32):
+                joined = jnp.where(lane // 4 == i, smalls[i // 8, i % 8, row : row + 1, :], joined)
+            head_g[row - 2 : row - 1, :] = joined
+        pack_dp[d] = jnp.zeros((24, 128), f32)
+
+    def norm_in(i, carry):
+        rows = tree[i].reshape(128, D).astype(f32)
+        scale = lax.rsqrt(jnp.mean(rows * rows, axis=-1, keepdims=True) + EPSILON)
+        normed_in[pl.ds(aligned(i * 128, 128), 128)] = (rows * scale * attn_g[...]).astype(bf)
+        return carry
+
+    stage(NORM_IN + 0)(lambda: lax.fori_loop(0, 4, norm_in, 0))
+    stage(NORM_IN + 1)(lambda: lax.fori_loop(4, 8, norm_in, 0))
+
+    def unit_of(v):
+        scale = lax.rsqrt(jnp.mean(v * v, axis=-1, keepdims=True) + EPSILON)
+        return v * scale, scale
+
+    def turn(v, gain, cos, sin):
+        unit, _ = unit_of(v)
+        lifted = unit * gain
+        return lifted * cos + pltpu.roll(lifted, 64, 1) * sin
+
+    def turn_back(dr, v, gain, cos, sin):
+        d_lift = dr * cos + pltpu.roll(dr * sin, 64, 1)
+        unit, scale = unit_of(v)
+        d_unit = d_lift * gain
+        return (
+            scale * (d_unit - unit * jnp.mean(unit * d_unit, axis=-1, keepdims=True)),
+            jnp.sum(d_lift * unit, axis=0, keepdims=True),
+        )
+
+    def project(i):
+        rows = pl.ds(i * QB, QB)
+        cos, sin = cosine[rows], sine[rows]
+
+        def one(j, carry):
+            lanes = pl.ds(aligned(j * 256, 256), 256)
+            pair = product(normed_in[rows], wa[:, lanes])
+            lin[rows, lanes] = pair
+            gain = head_g[pl.ds(j // 2, 1), :]
+            for i2 in range(2):
+                turned = turn(pair[:, 128 * i2 : 128 * (i2 + 1)], gain, cos, sin)
+                heads[2 * j + i2, rows] = turned.astype(bf)
+            return carry
+
+        lax.fori_loop(0, 3, one, 0)
+        value[rows] = product(normed_in[rows], wa[:, 768:]).astype(bf)
+
+    for i in range(4):
+        stage(PROJECT + i)(functools.partial(project, i))
+
+    def span(b):
+        return pl.ds(b * QB, QB), (b + 1) * QB
+
+    def weights_of(b, h, n):
+        here = pl.ds(b * QB, QB)
+        q = jnp.concatenate([heads[h, here], hidden[here]], axis=1)
+        k = jnp.concatenate([heads[4 + h // 2, pl.ds(0, n)], member[pl.ds(0, n)]], axis=1)
+        score = against(q, k) * SOFT
+        row = lax.broadcasted_iota(jnp.int32, (QB, QB), 0)
+        col = lax.broadcasted_iota(jnp.int32, (QB, QB), 1)
+        diag = jnp.where(col <= row, score[:, n - QB :], NEGATIVE)
+        score = diag if b == 0 else jnp.concatenate([score[:, : n - QB], diag], axis=1)
+        grown = jnp.exp2(score)
+        return grown, 1.0 / jnp.sum(grown, axis=-1, keepdims=True)
+
+    def head_lanes(h):
+        return pl.ds(aligned(h * HEAD_DIM, HEAD_DIM), HEAD_DIM)
+
+    sum_sems, spread_sems = (s_sum, r_sum), (s_spread, r_spread)
+    mixed_sum = Sum(part, near, sent, got, sum_sems, 0, spot)
+    mid_sum = Sum(part, near, sent, got, sum_sems, 1, spot)
+    out_sum = Sum(part_out, near_o, sent_o, got_o, sum_sems, 2, spot)
+    in_sum = Sum(part, near, sent, got, sum_sems, 3, spot)
+    pair_of = {b: pl.ds(2 * b, 2) for b in BLOCKS}
+    spread_mid = Spread(normed_mid, spread_sems, lambda way, rows: (0, way, rows.start // 2), spot)
+    spread_low = Spread(d_low, spread_sems, lambda way, rows: (1, way, rows.start // 2), spot)
+
+    def attend(b):
+        here, n = span(b)
+        if b == BLOCKS[0]:
+            own_rows.wait()
+
+        def one(h, carry):
+            grown, inverse = weights_of(b, h, n)
+            mixed = product(grown.astype(bf), value[pl.ds(0, n), head_lanes(h // 2)])
+            att[here, head_lanes(h)] = (mixed * inverse).astype(bf)
+            return carry
+
+        lax.fori_loop(0, HEADS // NDP, one, 0)
+        rows = product(att[here], wb[...]).astype(bf)
+        part[pair_of[b]] = rows.reshape(2, NDP, 32, D)
+        mixed_sum.start(b)
+
+    def to_middle(i, rows):
+        rows = rows + tree_own[i].astype(f32)
+        middle[i] = rows
+        scale = lax.rsqrt(jnp.mean(rows * rows, axis=-1, keepdims=True) + EPSILON)
+        normed_mid[i, d] = (rows * scale * ffn_g[...]).astype(bf)
+
+    def close_mixed(b):
+        mixed_sum.end(b, to_middle)
+        spread_mid.start(pair_of[b])
+
+    def lift(b):
+        here = pl.ds(b * QB, QB)
+        rows = normed_mid[pair_of[b]].reshape(QB, D)
+
+        def one(t, carry):
+            left = pl.ds(aligned(t * 256, 256), 256)
+            right = pl.ds(aligned(768 + t * 256, 256), 256)
+            gate = product(rows, wc[:, left])
+            wide = product(rows, wc[:, right])
+            sigma = 1.0 / (1.0 + jnp.exp(-gate))
+            silu = gate * sigma
+            act[here, left] = (silu * wide).astype(bf)
+            both[here, left] = (wide * sigma * (1.0 + gate * (1.0 - sigma))).astype(bf)
+            both[here, right] = silu.astype(bf)
+            return carry
+
+        lax.fori_loop(0, 3, one, 0)
+
+    @stage(GRAD_DOWN)
+    def _():
+        def one(i, carry):
+            cols = pl.ds(aligned(i * 256, 256), 256)
+            ge[cols] = across(act[:, cols], tree_cot[...].reshape(NSEQ * 128, D)).astype(bf)
+            return carry
+
+        lax.fori_loop(0, 3, one, 0)
+
+    def sink(b):
+        here = pl.ds(b * QB, QB)
+        cots = tree_cot[pair_of[b]].reshape(QB, D)
+
+        def one(t, carry):
+            left = pl.ds(aligned(t * 256, 256), 256)
+            right = pl.ds(aligned(768 + t * 256, 256), 256)
+            d_act = against(cots, we[left])
+            both[here, left] = (d_act * both[here, left].astype(f32)).astype(bf)
+            both[here, right] = (d_act * both[here, right].astype(f32)).astype(bf)
+            return carry
+
+        lax.fori_loop(0, 3, one, 0)
+        part[pair_of[b]] = against(both[here], wc[...]).astype(bf).reshape(2, NDP, 32, D)
+        mid_sum.start(b)
+
+    def settle(b):
+        here = pl.ds(b * QB, QB)
+        part_out[pair_of[b]] = product(act[here], we[...]).astype(bf).reshape(2, NDP, 32, D)
+        out_sum.start(b)
+
+    def to_turn(i, rows):
+        unit, scale = unit_of(middle[i])
+        lifted = ffn_g[...] * rows
+        term = jnp.sum(rows * unit, axis=0, keepdims=True)
+        for j in range(8):
+            pack_dp[d, 8 + j : 9 + j] += term[:, 128 * j : 128 * (j + 1)]
+        d_mid = tree_cot[i, d].astype(f32) + scale * (
+            lifted - unit * jnp.mean(unit * lifted, axis=-1, keepdims=True)
+        )
+        d_middle[i] = d_mid
+        d_low[i, d] = d_mid.astype(bf)
+
+    def close_mid(b):
+        mid_sum.end(b, to_turn)
+        spread_low.start(pair_of[b])
+
+    def to_outs(i, rows):
+        outs[i] = (middle[i] + rows).astype(bf)
+
+    back_owner, back_slot = tree_owner, tree_slot
+    back = ((outs, out_rows), (grad_low, grad_rows))
+
+    def give_copy(n, j):
+        src, dst = back[n]
+        return pltpu.make_async_remote_copy(
+            src_ref=src.at[j],
+            dst_ref=dst.at[back_slot, pl.ds(aligned(d * 32, 32), 32)],
+            send_sem=s_back.at[n, j],
+            recv_sem=r_back.at[n],
+            device_id=(back_owner, j),
+            device_id_type=MESH,
+        )
+
+    def give(n, b):
+        src, dst = back[n]
+
+        def one(j, carry):
+            same = (back_owner == d) & (s == j)
+
+            @pl.when(same)
+            def _():
+                place = dst.at[back_slot, pl.ds(aligned(d * 32, 32), 32)]
+                pltpu.make_async_copy(src.at[j], place, r_back.at[n]).start()
+
+            @pl.when(jnp.logical_not(same))
+            def _():
+                give_copy(n, j).start()
+
+            return carry
+
+        lax.fori_loop(2 * b, 2 * b + 2, one, 0)
+
+    def close_out(b):
+        out_sum.end(b, to_outs)
+        give(0, b)
+
+    def grad_wide(sub):
+        gather_sent(3 + sub)
+        for i in (sub, 2 + sub):
+            cols = pl.ds(i * 256, 256)
+
+            def one(t, carry):
+                lanes = pl.ds(aligned(512 * t, 512), 512)
+                wc[cols, lanes] = across(
+                    normed_mid[:, :, :, cols].reshape(NSEQ * 128, 256), both[:, lanes]
+                ).astype(bf)
+                return carry
+
+            lax.fori_loop(0, 3, one, 0)
+
+    d_lin = tree
+
+    def close_low(b):
+        spread_low.end(pair_of[b])
+        here = pl.ds(b * QB, QB)
+        rows = d_low[pair_of[b]].reshape(QB, D)
+        d_att[here] = against(rows, wb[...]).astype(bf)
+
+    def attend_back(b):
+        here, n = span(b)
+        keys = pl.ds(0, n)
+        if b == BLOCKS[0]:
+            spread_tree.sent(everything)
+            d_key[...] = jnp.zeros_like(d_key)
+            d_value[...] = jnp.zeros_like(d_value)
+
+        def one(h, carry):
+            kv = h // 2
+            grown, inverse = weights_of(b, h, n)
+            prob = grown * inverse
+            d_out = d_att[here, head_lanes(h)]
+            d_prob = against(d_out, value[keys, head_lanes(kv)])
+            delta = jnp.sum(prob * d_prob, axis=-1, keepdims=True)
+            d_raw = (prob * (d_prob - delta) * HEAD_DIM ** (-0.5)).astype(bf)
+            d_rot = product(d_raw, heads[4 + kv, keys])
+            d_key[kv, keys] += across(d_raw, heads[h, here])
+            d_value[kv, keys] += across(prob.astype(bf), d_out)
+            back, d_gain = turn_back(
+                d_rot, lin[here, head_lanes(h)], head_g[0:1, :], cosine[here], sine[here]
+            )
+            pack_dp[d, 16:17] += d_gain
+            d_lin[pair_of[b], :, :, head_lanes(h)] = back.astype(bf).reshape(2, NDP, 32, HEAD_DIM)
+            return carry
+
+        lax.fori_loop(0, HEADS // NDP, one, 0)
+        for kv in range(KV_HEADS // NDP):
+            at = 512 + 128 * kv
+            back, d_gain = turn_back(
+                d_key[kv, here], lin[here, pl.ds(at, 128)], head_g[1:2, :], cosine[here], sine[here]
+            )
+            pack_dp[d, 17:18] += d_gain
+            d_lin[pair_of[b], :, :, pl.ds(at, 128)] = back.astype(bf).reshape(2, NDP, 32, 128)
+            d_lin[pair_of[b], :, :, pl.ds(at + 256, 128)] = (
+                d_value[kv, here].astype(bf).reshape(2, NDP, 32, 128)
+            )
+
+    def sink_in(b):
+        rows = against(d_lin[pair_of[b]].reshape(QB, 1024), wa[...])
+        part[pair_of[b]] = rows.astype(bf).reshape(2, NDP, 32, D)
+        in_sum.start(b)
+
+    @stage(GRAD_OUT)
+    def _():
+        gather_sent(2)
+        for i in range(2):
+            cols = pl.ds(256 * i, 256)
+            wb[cols] = across(att[:, cols], d_low[...].reshape(NSEQ * 128, D)).astype(bf)
+
+    def grad_attn(sub):
+        gather_sent(sub)
+        for i in (sub, 2 + sub):
+            cols = pl.ds(i * 256, 256)
+
+            def one(t, carry):
+                lanes = pl.ds(aligned(512 * t, 512), 512)
+                wa[cols, lanes] = across(
+                    normed_in[:, cols], d_lin[:, :, :, lanes].reshape(NSEQ * 128, 512)
+                ).astype(bf)
+                return carry
+
+            lax.fori_loop(0, 2, one, 0)
+
+    def to_grad(i, rows):
+        unit, scale = unit_of(tree_own[i].astype(f32))
+        lifted = attn_g[...] * rows
+        term = jnp.sum(rows * unit, axis=0, keepdims=True)
+        for j in range(8):
+            pack_dp[d, j : j + 1] += term[:, 128 * j : 128 * (j + 1)]
+        grad = d_middle[i] + scale * (
+            lifted - unit * jnp.mean(unit * lifted, axis=-1, keepdims=True)
+        )
+        grad_low[i] = grad.astype(bf)
+
+    def close_in(b):
+        in_sum.end(b, to_grad)
+        give(1, b)
+
+    per_block = (
+        (ATTEND, attend), (MIX_MID, mixed_sum.mid), (MIX_END, close_mixed),
+        (NORM_MID, lambda b: spread_mid.mid(pair_of[b])), (NORM_END, lambda b: spread_mid.end(pair_of[b])),
+        (LIFT, lift), (SINK, sink), (TURN_MID, mid_sum.mid), (TURN_END, close_mid),
+        (LOW_MID, lambda b: spread_low.mid(pair_of[b])), (LOW_END, close_low),
+        (OUT_START, settle), (OUT_MID, out_sum.mid), (OUT_END, close_out),
+        (ATTEND_BACK, attend_back), (IN_START, sink_in), (IN_MID, in_sum.mid), (IN_END, close_in),
+    )
+    for label, run in per_block:
+        for b in BLOCKS:
+            stage(label + b)(functools.partial(run, b))
+    for sub in range(2):
+        stage(GRAD_WIDE + sub)(functools.partial(grad_wide, sub))
+        stage(GRAD_ATTN + sub)(functools.partial(grad_attn, sub))
+
+    pack_sems, fin_sems = (s_pack, r_pack), (s_fin, r_fin)
+
+    @stage(PACK_DP)
+    def _():
+        for i in range(1, NDP):
+            launch(remote(pack_dp.at[d], pack_dp.at[d], pack_sems, i, (d + i) % NDP, s))
+
+    @stage(PACK_SEQ)
+    def _():
+        for i in range(1, NDP):
+            place = pack_dp.at[(d + NDP - i) % NDP]
+            remote(place, place, pack_sems, i, d, s).wait_recv()
+        pack_seq[s] = (pack_dp[0] + pack_dp[1]) + (pack_dp[2] + pack_dp[3])
+        for i in range(1, NSEQ):
+            launch(remote(pack_seq.at[s], pack_seq.at[s], pack_sems, NDP + i, d, (s + i) % NSEQ))
+
+    @stage(PACK_END)
+    def _():
+        for i in range(1, NSEQ):
+            place = pack_seq.at[(s + NSEQ - i) % NSEQ]
+            remote(place, place, pack_sems, NDP + i, d, s).wait_recv()
+        total = pack_seq[0]
+        for j in range(1, NSEQ):
+            total = total + pack_seq[j]
+        pack_sum[...] = total
+        at = d * NSEQ + s
+        for n, (row, count) in enumerate(
+            ((at // 4, 32), (8 + at // 4, 32), (16, 4), (17, 4))
+        ):
+            line = pack_sum[pl.ds(row, 1), :]
+            shift = (128 - (at * count) % 128) % 128
+            pack_out[n : n + 1, :] = pltpu.roll(line, shift, 1)
+
+    def close_cols(n, fin, landed, which):
+        sub = (n + (n > 2)) % 2
+
+        def take(way, total):
+            fin[2 * way + sub] = total.astype(bf)
+
+        reduce_end(n, take)
+        for way in range(2):
+            q = 2 * way + sub
+
+            @pl.when(q == d)
+            def _():
+                pltpu.make_async_copy(fin.at[q], landed.at[d], loc.at[which]).start()
+
+            @pl.when(q != d)
+            def _():
+                remote(fin.at[q], landed.at[d], fin_sems, (which, d), q, s).start()
+
+    for label, n, fin, landed, which in (
+        (A0, 0, fin_a, res_a, 0), (A1, 1, fin_a, res_a, 0),
+        (C0, 3, fin_c, res_c, 1), (C1, 4, fin_c, res_c, 1),
+    ):
+        stage(R_A0 + label + 7)(functools.partial(close_cols, n, fin, landed, which))
+
+    def land(landed, which):
+        for i in range(1, NDP):
+            q = (d + i) % NDP
+            remote(landed.at[q], landed.at[q], fin_sems, (which, q), q, s).wait_recv()
+        pltpu.make_async_copy(landed.at[d], landed.at[d], loc.at[which]).wait()
+
+    stage(LAND_A)(lambda: land(res_a, 0))
+    stage(LAND_C)(lambda: land(res_c, 1))
+
+    def take_rows(dst, rows, way, total):
+        dst[rows * way : rows * (way + 1)] = total
+
+    stage(R_B + 7)(lambda: reduce_end(2, functools.partial(take_rows, g_output, 32)))
+    stage(R_E + 7)(lambda: reduce_end(5, functools.partial(take_rows, g_down, 48)))
+
+    @stage(DRAIN)
+    def _():
+        for n, (src, dst) in enumerate(back):
+            pltpu.make_async_copy(dst, dst, r_back.at[n]).wait()
+
+            def one(j, carry):
+                @pl.when(jnp.logical_not((back_owner == d) & (s == j)))
+                def _():
+                    give_copy(n, j).wait_send()
+
+                return carry
+
+            lax.fori_loop(0, NSEQ, one, 0)
+        for n, (fin, landed) in enumerate(((fin_a, res_a), (fin_c, res_c))):
+            for i in range(1, NDP):
+                q = (d + i) % NDP
+                remote(fin.at[q], landed.at[d], fin_sems, (n, d), q, s).wait_send()
+        gather_sent(5)
+        for n in range(6):
+            reduce_sent(n)
+        spread_cot.sent(everything)
+        for b in BLOCKS:
+            spread_mid.sent(pair_of[b])
+            spread_low.sent(pair_of[b])
+        for cp in pending:
+            cp.wait_send()
+        for n in range(2):
+            for m in range(MICRO):
+
+                @pl.when(tree_seat(d, m) != s)
+                def _():
+                    row_copy(n, m, 0).wait_send()
+
+                for i in range(1, NDP):
+                    row_copy(n, m, i).wait_send()
+
+    for name in ORDER:
+        ops[name]()
+
+
+def finish_kernel(
+    out_rows, grad_rows, res_a, res_c, g_output, g_down, pack,
+    outs, grads, g_query, g_key, g_value, out_output, g_gate, g_up, out_down, g_attn, g_ffn, g_qg, g_kg,
+    sems,
+):
+    through = [
+        pltpu.make_async_copy(src, dst, sems.at[n])
+        for n, (src, dst) in enumerate(
+            ((out_rows, outs), (g_output, out_output), (g_down, out_down))
+        )
+    ]
+    for cp in through:
+        cp.start()
+    grads[...] = grad_rows[...].astype(jnp.float32)
+    for src, cuts in (
+        (res_a, ((0, 512, g_query), (512, 256, g_key), (768, 256, g_value))),
+        (res_c, ((0, 768, g_gate), (768, 768, g_up))),
+    ):
+        for q in range(NDP):
+            for at, width, dst in cuts:
+                dst[:, width * q : width * (q + 1)] = src[q, :, at : at + width].astype(jnp.float32)
+    for n, dst in enumerate((g_attn, g_ffn, g_qg, g_kg)):
+        count = dst.shape[0]
+        dst[...] = pack[n : n + 1, 0:count].reshape(count)
+    for cp in through:
+        cp.wait()
+
+
+def tree_shards(
+    tokens, cotangent, node_lengths, parents, w_query, w_key, w_value, w_output, w_gate, w_up, w_down,
+    attn_gain, ffn_gain, query_gain, key_gain,
+):
+    f32, bf = jnp.float32, jnp.bfloat16
+    nodes = node_lengths.shape[2]
+    half = np.arange(HEAD_DIM // 2, dtype=np.float64)
+    inv_freq = THETA ** (-(half * (2.0 / HEAD_DIM)))
+    inv_freq = np.concatenate([inv_freq, inv_freq])[None].astype(np.float32)
+    shape, vmem, dma = jax.ShapeDtypeStruct, pltpu.VMEM, pltpu.SemaphoreType.DMA
+    anywhere = pl.BlockSpec(memory_space=pl.ANY)
+    here = pl.BlockSpec(memory_space=pltpu.VMEM)
+    rows = NSEQ * 128
+    quarter = (NSEQ, 32, D)
+    twice = lambda *dims: [dma(dims), dma(dims)]
+    results = pl.pallas_call(
+        functools.partial(layer_kernel, nodes),
+        out_shape=(
+            shape((MICRO, 128, D), bf),
+            shape((MICRO, 128, D), bf),
+            shape((NDP, 32, 1024), bf),
+            shape((NDP, 32, 1536), bf),
+            shape((64, D), f32),
+            shape((96, D), f32),
+            shape((8, 128), f32),
+        ),
+        in_specs=[anywhere] * 8 + [here] + [anywhere] * 7,
+        out_specs=[anywhere] * 4 + [here] * 3,
+        scratch_shapes=[
+            vmem(node_lengths.shape, jnp.int32), vmem(parents.shape, jnp.int32),
+            *[vmem(gain.shape, bf) for gain in (attn_gain, ffn_gain, query_gain, key_gain)],
+            vmem((NDP, NSEQ, 8, 128), f32),
+            vmem((D, 1024), bf), vmem((512, D), bf), vmem((D, 1536), bf), vmem((768, D), bf),
+            vmem((768, D), bf),
+            vmem((2, 2, 7, 32, 1024), bf), vmem((2, 7, 32, D), bf),
+            vmem((2, 2, 7, 32, 1536), bf), vmem((2, 7, 48, D), bf),
+            vmem((NSEQ, NDP, 32, D), bf), vmem((NSEQ, NDP, 32, D), bf), vmem((rows, D), bf),
+            vmem((NSEQ, NDP, 32, D), bf), vmem((NSEQ, NDP, 32, D), bf), vmem(quarter, bf),
+            vmem((rows, 768), f32), vmem((6, rows, 128), bf),
+            vmem((rows, 256), bf), vmem((rows, 128), bf), vmem((rows, 128), bf),
+            vmem((rows, 128), f32), vmem((rows, 128), f32), vmem((rows, 512), bf), vmem((rows, 512), bf),
+            vmem((NSEQ, NDP, 32, D), bf), vmem((NSEQ, NDP, 32, D), bf),
+            vmem((2,) + quarter, bf), vmem(quarter, bf), vmem(quarter, bf),
+            vmem((2,) + quarter, bf), vmem(quarter, bf), vmem(quarter, bf),
+            vmem(quarter, f32), vmem(quarter, f32), vmem((rows, 768), bf), vmem((rows, 1536), bf),
+            vmem((2, rows, 128), f32), vmem((2, rows, 128), f32), vmem(quarter, bf), vmem(quarter, bf),
+            vmem((NDP, 32, 1024), bf), vmem((NDP, 32, 1536), bf),
+            vmem((1, D), f32), vmem((1, D), f32), vmem((8, 128), f32),
+            vmem((NDP, 24, 128), f32), vmem((NSEQ, 24, 128), f32), vmem((24, 128), f32),
+            dma((16,)),
+            *twice(12), *twice(5, NDP), dma((2, MICRO, NDP)), dma((2,)),
+            *twice(6, 2, 7), *twice(6, 2, 7),
+            *twice(4, 3, 4), *twice(2, 3), *twice(2, 3, 4),
+            dma((2, NSEQ)), dma((2,)), *twice(2, NDP), *twice(12),
+        ],
+        compiler_params=pltpu.CompilerParams(
+            collective_id=1, has_side_effects=True, vmem_limit_bytes=61 << 20
+        ),
+        name="layer",
+    )(
+        tokens[0], cotangent[0], node_lengths, parents, attn_gain, ffn_gain, query_gain, key_gain, inv_freq,
+        w_query, w_key, w_value, w_output, w_gate, w_up, w_down,
+    )
+    full = lambda *dims: shape(dims, f32)
+    finished = pl.pallas_call(
+        finish_kernel,
+        out_shape=(
+            shape((MICRO, 128, D), bf), full(MICRO, 128, D),
+            full(32, 2048), full(32, 1024), full(32, 1024), full(64, D),
+            full(32, FF), full(32, FF), full(96, D),
+            full(32), full(32), full(4), full(4),
+        ),
+        in_specs=[anywhere, here, here, here, anywhere, anywhere, here],
+        out_specs=[anywhere, here, here, here, here, anywhere, here, here, anywhere] + [here] * 4,
+        scratch_shapes=[dma((3,))],
+        compiler_params=pltpu.CompilerParams(vmem_limit_bytes=32 << 20),
+        name="finish",
+    )(*results)
+    return (finished[0][None], finished[1][None]) + tuple(finished[2:])
+
+
 def solution(mesh):
+    ring = mesh.shape["dp"] == NDP and mesh.shape["seq"] == NSEQ
     return jax.shard_map(
-        shards,
+        tree_shards if ring else general_shards,
         mesh=mesh,
         in_specs=(
             P("dp", None, "seq", None),

time: 2190 us -> 248 us (0.11)
  waiting for transfers between devices: 1590 us -> 0 us
  Pallas kernels: 0 us -> 237 us
  matrix products: 228 us -> 0 us
  local copies, waits for them, and re-layouts: 183 us -> 6.65 us
  blocking collectives: 82.8 us -> 0 us
  other arithmetic: 41 us -> 0 us
  loops' own time: 38.4 us -> 0 us
    reduce_scatter x7 -> x0, waiting for transfers between devices: 1060 us -> none  [the longest x1 187 us: shards(): lax.psum_scatter(sums[3], ('dp', 'seq'), scatter_dimension=0, tiled=True)]
    all_gather x11 -> x0, waiting for transfers between devices: 489 us -> none  [the longest x2 82.4 us: shards(): lax.all_gather(value_low, 'seq', axis=0, tiled=True)]
    pallas_call x0 -> x2, Pallas kernels: none -> 237 us  [the longest x1 235 us: tree_shards(): pl.pallas_call(functools.partial(layer_kernel, nodes), out_shape=(shape((...]
    dot_general x104 -> x0, matrix products: 228 us -> none  [the longest x14 45.2 us: across(): lax.dot_general(left_side, right_side, (((0,), (0,)), ((), ())), preferre...]
    dynamic_slice x64 -> x0, local copies, waits for them, and re-layouts: 82.8 us -> none  [the longest x16 20.8 us: back_pair(): lax.dynamic_slice_in_dim(d_attended, pair_id * width_query, width_query, 1)]
    unnamed x2 -> x0, blocking collectives: 82.8 us -> none
    unnamed x273 -> x14, local copies, waits for them, and re-layouts: 58.3 us -> 6.65 us
    another operation x6 -> x0, loops' own time: 38.4 us -> none  [the longest x2 26.5 us: shards(): d_query_pairs, kv_terms = lax.map(back_pair, pair_ids)]
  transfers between devices with their start and end apart: 20 -> 0, of which waited for: 19 -> 0; matrix products, arithmetic and copies ran while one was open for 14% -> 0% of each run, Pallas kernels for 0% -> 0%
where the time goes in v3:
time: 248 us; the launch traced here: 245 us
  Pallas kernels  237 us (96%)
  local copies, waits for them, and re-layouts  6.65 us (3%)
    pallas_call x1, Pallas kernels, tree_shards(): pl.pallas_call(functools.partial(layer_kernel, nodes), out_shape=(shape((...  235 us
    unnamed x14, local copies, waits for them, and re-layouts  6.65 us

profile of v3, /device:TPU:21, one launch (start us, length us, event | category | flops | bytes accessed | tf_op | source)
XLA Modules:
  0.0 244.8 jit_solution(7861646599698755319)
XLA Ops:
  0.7 234.9 %layer.1 = (bf16[2,128,1024]{2,1,0:T(8,128)(2,1)}, bf16[2,128,1024]{2,1,0:T(8,128)(2,1)}, bf16[4,32,1024]{2,1,0:T(8,128)(2,1)}, bf16[4,32,1536]{2,1,0:T(8,128)(2...) custom-call(bf16[2,128,1024]{2,1,0:T(8,128)(2,1)} %bitcast.4, bf16[2,128,1024]{2,1,0:T(8,128)(2,1)} %bitcast.5, ...), custom_call_target="tpu_custom_call" | custom-call | tf_op jit(solution)/shard_map/layer/pallas_call | solution.py:1371
  235.5 0.0 copy-start.6
  235.5 0.7 copy-done.6
  236.2 0.0 copy-start
  236.2 1.0 copy-done
  237.2 0.0 copy-start.1
  237.3 1.0 copy-done.1
  238.3 0.0 copy-start.2
  238.3 1.0 copy-done.2
  239.3 0.0 copy-start.3
  239.3 1.0 copy-done.3
  240.3 0.0 copy-start.4
  240.3 0.9 copy-done.4
  241.2 0.0 copy-start.5
  241.2 0.9 copy-done.5
  242.2 2.4 finish.1
Async XLA Ops:
  235.5 0.7 copy-start.6
  236.2 1.0 copy-start
  237.2 1.0 copy-start.1
  238.3 1.0 copy-start.2
  239.3 1.0 copy-start.3
  240.3 0.9 copy-start.4
  241.2 0.9 copy-start.5

commit v4 on v3

--- a/solution.py
+++ b/solution.py
@@ -400,36 +400,37 @@
 A0, A1, B, C0, C1, E = range(0, 60, 10)
 R_A0, R_A1, R_B, R_C0, R_C1, R_E = range(60, 120, 10)
 (
-    ATTEND, MIX_MID, MIX_END, NORM_MID, NORM_END, LIFT, SINK, TURN_MID, TURN_END, LOW_MID, LOW_END,
-    OUT_START, OUT_MID, OUT_END, ATTEND_BACK, IN_START, IN_MID, IN_END, PROJECT, GRAD_WIDE,
-    GRAD_ATTN, TABLES, NORM_IN,
-) = range(200, 430, 10)
+    ATTEND, MIX_MID, MIX_END, NORM_MID, NORM_END, LIFT, D_ACT, SINK, TURN_MID, TURN_END, LOW_MID,
+    LOW_END, OUT_START, OUT_MID, OUT_END, ATTEND_BACK, IN_START, IN_MID, IN_END, PROJECT,
+    GRAD_WIDE, GRAD_ATTN, TABLES, NORM_IN, COTANGENT,
+) = range(200, 450, 10)
 (
-    START, TOKENS, COTANGENT, SMALL_DP, SMALL_SEQ, A_IN, C_OUT, C_IN, TREE_START, COT_START,
-    TREE_MID, COT_MID, COT_END, TREE_END, NODE, GAINS, GRAD_DOWN, GRAD_OUT, PACK_DP, PACK_SEQ,
-    PACK_END, LAND_A, LAND_C, DRAIN,
-) = range(600, 624, 1)
+    START, TOKENS, SMALL_DP, SMALL_SEQ, A_IN, C_OUT, C_IN, TREE_START, COT_START, TREE_MID,
+    COT_MID, COT_END, TREE_END, NODE, GAINS, GRAD_DOWN, GRAD_OUT, PACK_DP, PACK_SEQ, PACK_END,
+    LAND_A, LAND_C, GIVE_OUT, GIVE_IN, DRAIN,
+) = range(600, 625, 1)
 ORDER = (
-    START, B, TOKENS, SMALL_DP, A_IN, A1, B + 1, A0, C_OUT, A1 + 1, C_IN, TREE_START, B + 2, A0 + 1,
-    SMALL_SEQ, A1 + 2, NODE, B + 3, TABLES, A0 + 2, A1 + 3, C1, A0 + 3, A1 + 4, B + 4, A0 + 4, TREE_MID,
-    A1 + 5, C0, TABLES + 1, A0 + 5, B + 5, TREE_END, GAINS, A1 + 6, A0 + 6, NORM_IN, B + 6, C0 + 1, C1 + 1,
-    NORM_IN + 1, A1 + 7, COTANGENT, B + 7, A0 + 7, PROJECT, PROJECT + 1, PROJECT + 2, PROJECT + 3, ATTEND + 3,
-    ATTEND + 2, C0 + 2, C1 + 2, MIX_MID + 3, MIX_MID + 2, ATTEND + 1, E, MIX_MID + 1, ATTEND, C0 + 3, C1 + 3,
-    MIX_MID, E + 1, MIX_END + 1, MIX_END + 2, C0 + 4, MIX_END + 3, C1 + 4, MIX_END, E + 2, COT_START, C0 + 5,
-    NORM_MID + 2, C1 + 5, NORM_MID + 3, E + 3, NORM_MID, NORM_MID + 1, NORM_END + 3, C0 + 6, NORM_END,
-    NORM_END + 1, C1 + 6, E + 4, NORM_END + 2, C0 + 7, C1 + 7, LIFT + 2, E + 5, COT_MID, LIFT + 1, LIFT + 3,
-    COT_END, E + 6, LIFT, GRAD_DOWN, R_E, E + 7, SINK + 3, OUT_START + 3, SINK + 1, OUT_START + 1, R_E + 1,
-    SINK, OUT_START, TURN_MID + 3, SINK + 2, OUT_START + 2, R_E + 2, OUT_MID + 3, GRAD_WIDE, R_C0,
-    OUT_MID + 1, GRAD_WIDE + 1, R_C1, TURN_END + 3, R_E + 3, TURN_MID + 2, R_C0 + 1, R_C1 + 1, LOW_MID + 3,
-    OUT_END + 1, TURN_MID, LOW_END + 3, TURN_MID + 1, R_C0 + 2, TURN_END + 2, OUT_MID, R_C1 + 2, OUT_END + 3,
-    ATTEND_BACK + 3, IN_START + 3, R_C0 + 3, R_C1 + 3, LOW_MID + 2, TURN_END, TURN_END + 1, IN_MID + 3,
-    LOW_END + 2, R_E + 4, R_C0 + 4, OUT_END, R_C1 + 4, ATTEND_BACK + 2, IN_START + 2, R_C0 + 5, R_E + 5,
-    LOW_MID + 1, LOW_MID, IN_END + 3, IN_MID + 2, R_C1 + 5, LOW_END + 1, ATTEND_BACK + 1, IN_START + 1,
-    R_C0 + 6, R_E + 6, LOW_END, GRAD_OUT, IN_END + 2, R_B, ATTEND_BACK, IN_START, IN_MID + 1, GRAD_ATTN + 1,
-    R_A1, GRAD_ATTN, R_A0, R_C1 + 6, R_A1 + 1, R_A0 + 1, R_B + 1, R_C0 + 7, OUT_MID + 2, R_A1 + 2, R_A0 + 2,
-    IN_END + 1, R_A1 + 3, IN_MID, R_B + 2, R_A0 + 3, R_A1 + 4, R_B + 3, R_A0 + 4, R_C1 + 7, R_A1 + 5, R_E + 7,
-    R_B + 4, R_A0 + 5, R_A1 + 6, R_B + 5, LAND_C, R_A0 + 6, IN_END, PACK_DP, R_A1 + 7, R_B + 6, R_A0 + 7,
-    PACK_SEQ, OUT_END + 2, PACK_END, R_B + 7, LAND_A, DRAIN,
+    START, B, TOKENS, SMALL_DP, C_OUT, A_IN, A1, A0, B + 1, A1 + 1, A0 + 1, TREE_START, B + 2, SMALL_SEQ,
+    A1 + 2, C_IN, A0 + 2, B + 3, C1, A0 + 3, A1 + 3, C0, TREE_MID, NODE, B + 4, A0 + 4, TREE_END, A1 + 4,
+    TABLES, B + 5, A0 + 5, GAINS, A1 + 5, TABLES + 1, C0 + 1, A0 + 6, NORM_IN, NORM_IN + 1, A1 + 6, C1 + 1,
+    C0 + 2, B + 6, COTANGENT, A0 + 7, A1 + 7, PROJECT, E, C1 + 2, PROJECT + 1, COTANGENT + 1, PROJECT + 2,
+    PROJECT + 3, B + 7, ATTEND + 3, C0 + 3, ATTEND + 2, MIX_MID + 3, C1 + 3, E + 1, MIX_MID + 2, ATTEND + 1,
+    MIX_END + 3, MIX_MID + 1, ATTEND, C0 + 4, MIX_MID, C1 + 4, E + 2, MIX_END + 2, NORM_MID + 3, MIX_END + 1,
+    C0 + 5, NORM_END + 3, MIX_END, C1 + 5, E + 3, COT_START, C0 + 6, NORM_MID + 1, NORM_END + 1, C1 + 6,
+    E + 4, NORM_MID, NORM_END, NORM_MID + 2, C0 + 7, NORM_END + 2, C1 + 7, LIFT + 3, E + 5, LIFT, LIFT + 1,
+    COT_MID, E + 6, LIFT + 2, COT_END, GRAD_DOWN, R_E, E + 7, D_ACT + 3, D_ACT + 2, SINK + 3, D_ACT, R_E + 1,
+    TURN_MID + 3, D_ACT + 1, GRAD_WIDE + 1, R_C1, GRAD_WIDE, R_C0, R_E + 2, TURN_END + 3, SINK + 2, R_C1 + 1,
+    SINK + 1, TURN_MID + 2, R_C0 + 1, LOW_MID + 3, SINK, TURN_MID + 1, LOW_END + 3, R_E + 3, R_C1 + 2,
+    TURN_MID, TURN_END + 2, R_C0 + 2, ATTEND_BACK + 3, R_C1 + 3, TURN_END + 1, IN_START + 3, LOW_MID + 2,
+    R_E + 4, R_C0 + 3, TURN_END, LOW_END + 2, R_C1 + 4, ATTEND_BACK + 2, R_C0 + 4, LOW_MID, LOW_MID + 1,
+    R_C1 + 5, R_E + 5, LOW_END, LOW_END + 1, GRAD_OUT, R_B, R_C0 + 5, ATTEND_BACK + 1, R_C1 + 6, IN_START + 2,
+    IN_START + 1, R_B + 1, R_E + 6, R_C0 + 6, ATTEND_BACK, IN_START, GRAD_ATTN, R_A0, GRAD_ATTN + 1, R_A1,
+    R_B + 2, OUT_START + 3, IN_MID, R_A0 + 1, R_A1 + 1, IN_MID + 1, IN_MID + 2, R_B + 3, OUT_START, R_A0 + 2,
+    OUT_START + 1, R_A1 + 2, OUT_MID, R_B + 4, R_A0 + 3, IN_MID + 3, R_A1 + 3, OUT_START + 2, R_B + 5, IN_END,
+    R_A0 + 4, IN_END + 1, R_A1 + 4, OUT_MID + 3, OUT_MID + 2, R_B + 6, R_A0 + 5, IN_END + 3, R_A1 + 5,
+    IN_END + 2, GIVE_IN, OUT_END + 2, PACK_DP, OUT_END + 3, R_E + 7, OUT_MID + 1, R_A1 + 6, R_A0 + 6, OUT_END,
+    PACK_SEQ, R_C0 + 7, OUT_END + 1, R_C1 + 7, GIVE_OUT, PACK_END, LAND_C, R_A1 + 7, R_A0 + 7, R_B + 7,
+    LAND_A, DRAIN,
 )
 
 
@@ -556,7 +557,7 @@
     nodes,
     tok, cot, lengths, parents, gain_a, gain_f, gain_q, gain_k, inv_freq, wq, wk, wv, wo, wg, wu, wd,
     out_rows, grad_rows, res_a, res_c, g_output, g_down, pack_out,
-    raw_lengths, raw_parents, raw_a, raw_f, raw_q, raw_k, smalls, wa, wb, wc, we, ge, hop_a, hop_b, hop_c, hop_e,
+    raw_lengths, raw_parents, raw_a, raw_f, raw_q, raw_k, smalls, wa, wb, wc, we, gc, ge, hop_a, hop_b, hop_c, hop_e,
     tree, tree_cot, normed_in, normed_mid, d_low, tree_own,
     lin, heads, value, hidden, member, cosine, sine, att, d_att,
     part, part_out, near, sent, got, near_o, sent_o, got_o,
@@ -587,7 +588,7 @@
         return pl.ds(aligned(j * 96 + way * 48, 16), 48)
 
     weight = {0: wa, 1: wa, 2: wb, 3: wc, 4: wc, 5: we}
-    grads = {0: wa, 1: wa, 2: wb, 3: wc, 4: wc, 5: ge}
+    grads = {0: wa, 1: wa, 2: wb, 3: gc, 4: gc, 5: ge}
     hops = {0: hop_a.at[0], 1: hop_a.at[1], 2: hop_b, 3: hop_c.at[0], 4: hop_c.at[1], 5: hop_e}
 
     def owner_at(way, k):
@@ -714,22 +715,25 @@
             device_id_type=MESH,
         )
 
-    def rows_out(n):
+    def rows_out(n, half):
         src, dst = ((tok, tree), (cot, tree_cot))[n]
         for m in range(MICRO):
-            target = tree_seat(d, m)
-
-            @pl.when(target == s)
-            def _():
-                piece = src.at[m, pl.ds(aligned(d * 32, 32), 32)]
-                pltpu.make_async_copy(piece, dst.at[s, d], r_tok.at[n]).start()
-
-            @pl.when(target != s)
-            def _():
-                row_copy(n, m, 0).start()
-
-            for i in range(1, NDP):
-                row_copy(n, m, i).start()
+            if half == 0:
+                target = tree_seat(d, m)
+
+                @pl.when(target == s)
+                def _():
+                    piece = src.at[m, pl.ds(aligned(d * 32, 32), 32)]
+                    pltpu.make_async_copy(piece, dst.at[s, d], r_tok.at[n]).start()
+
+                @pl.when(target != s)
+                def _():
+                    row_copy(n, m, 0).start()
+
+                row_copy(n, m, 1).start()
+            else:
+                row_copy(n, m, 2).start()
+                row_copy(n, m, 3).start()
 
     def rows_in(dst, n):
         everything = dst.at[:, d]
@@ -748,8 +752,14 @@
         for n in range(3):
             columns(n)
 
-    stage(TOKENS)(lambda: rows_out(0))
-    stage(COTANGENT)(lambda: rows_out(1))
+    @stage(TOKENS)
+    def _():
+        rows_out(0, 0)
+        rows_out(0, 1)
+
+    for i in range(2):
+        stage(COTANGENT + i)(functools.partial(rows_out, 1, i))
+
 
     @stage(SMALL_DP)
     def _():
@@ -1020,7 +1030,7 @@
 
         lax.fori_loop(0, 3, one, 0)
 
-    def sink(b):
+    def d_activate(b):
         here = pl.ds(b * QB, QB)
         cots = tree_cot[pair_of[b]].reshape(QB, D)
 
@@ -1033,6 +1043,9 @@
             return carry
 
         lax.fori_loop(0, 3, one, 0)
+
+    def sink(b):
+        here = pl.ds(b * QB, QB)
         part[pair_of[b]] = against(both[here], wc[...]).astype(bf).reshape(2, NDP, 32, D)
         mid_sum.start(b)
 
@@ -1074,7 +1087,7 @@
             device_id_type=MESH,
         )
 
-    def give(n, b):
+    def give(n):
         src, dst = back[n]
 
         def one(j, carry):
@@ -1091,20 +1104,18 @@
 
             return carry
 
-        lax.fori_loop(2 * b, 2 * b + 2, one, 0)
+        lax.fori_loop(0, NSEQ, one, 0)
 
     def close_out(b):
         out_sum.end(b, to_outs)
-        give(0, b)
 
     def grad_wide(sub):
-        gather_sent(3 + sub)
         for i in (sub, 2 + sub):
             cols = pl.ds(i * 256, 256)
 
             def one(t, carry):
                 lanes = pl.ds(aligned(512 * t, 512), 512)
-                wc[cols, lanes] = across(
+                gc[cols, lanes] = across(
                     normed_mid[:, :, :, cols].reshape(NSEQ * 128, 256), both[:, lanes]
                 ).astype(bf)
                 return carry
@@ -1196,12 +1207,11 @@
 
     def close_in(b):
         in_sum.end(b, to_grad)
-        give(1, b)
 
     per_block = (
         (ATTEND, attend), (MIX_MID, mixed_sum.mid), (MIX_END, close_mixed),
         (NORM_MID, lambda b: spread_mid.mid(pair_of[b])), (NORM_END, lambda b: spread_mid.end(pair_of[b])),
-        (LIFT, lift), (SINK, sink), (TURN_MID, mid_sum.mid), (TURN_END, close_mid),
+        (LIFT, lift), (D_ACT, d_activate), (SINK, sink), (TURN_MID, mid_sum.mid), (TURN_END, close_mid),
         (LOW_MID, lambda b: spread_low.mid(pair_of[b])), (LOW_END, close_low),
         (OUT_START, settle), (OUT_MID, out_sum.mid), (OUT_END, close_out),
         (ATTEND_BACK, attend_back), (IN_START, sink_in), (IN_MID, in_sum.mid), (IN_END, close_in),
@@ -1212,6 +1222,9 @@
     for sub in range(2):
         stage(GRAD_WIDE + sub)(functools.partial(grad_wide, sub))
         stage(GRAD_ATTN + sub)(functools.partial(grad_attn, sub))
+
+    stage(GIVE_OUT)(functools.partial(give, 0))
+    stage(GIVE_IN)(functools.partial(give, 1))
 
     pack_sems, fin_sems = (s_pack, r_pack), (s_fin, r_fin)
 
@@ -1302,7 +1315,8 @@
             for i in range(1, NDP):
                 q = (d + i) % NDP
                 remote(fin.at[q], landed.at[d], fin_sems, (n, d), q, s).wait_send()
-        gather_sent(5)
+        for n in (3, 4, 5):
+            gather_sent(n)
         for n in range(6):
             reduce_sent(n)
         spread_cot.sent(everything)
@@ -1328,28 +1342,42 @@
 def finish_kernel(
     out_rows, grad_rows, res_a, res_c, g_output, g_down, pack,
     outs, grads, g_query, g_key, g_value, out_output, g_gate, g_up, out_down, g_attn, g_ffn, g_qg, g_kg,
-    sems,
+    low_rows, low_a, low_c, small, *rest,
 ):
-    through = [
+    *held, sems = rest
+    coming = [
         pltpu.make_async_copy(src, dst, sems.at[n])
         for n, (src, dst) in enumerate(
-            ((out_rows, outs), (g_output, out_output), (g_down, out_down))
+            (
+                (grad_rows, low_rows), (res_a, low_a), (res_c, low_c), (pack, small),
+                (out_rows, held[0]), (g_output, held[1]), (g_down, held[2]),
+            )
         )
     ]
-    for cp in through:
+    for cp in coming:
         cp.start()
-    grads[...] = grad_rows[...].astype(jnp.float32)
+    leaving = [
+        pltpu.make_async_copy(src, dst, sems.at[7 + n])
+        for n, (src, dst) in enumerate(zip(held, (outs, out_output, out_down)))
+    ]
+    for came, goes in zip(coming[4:], leaving):
+        came.wait()
+        goes.start()
+    coming[0].wait()
+    grads[...] = low_rows[...].astype(jnp.float32)
+    for cp in coming[1:4]:
+        cp.wait()
     for src, cuts in (
-        (res_a, ((0, 512, g_query), (512, 256, g_key), (768, 256, g_value))),
-        (res_c, ((0, 768, g_gate), (768, 768, g_up))),
+        (low_a, ((0, 512, g_query), (512, 256, g_key), (768, 256, g_value))),
+        (low_c, ((0, 768, g_gate), (768, 768, g_up))),
     ):
         for q in range(NDP):
             for at, width, dst in cuts:
                 dst[:, width * q : width * (q + 1)] = src[q, :, at : at + width].astype(jnp.float32)
     for n, dst in enumerate((g_attn, g_ffn, g_qg, g_kg)):
         count = dst.shape[0]
-        dst[...] = pack[n : n + 1, 0:count].reshape(count)
-    for cp in through:
+        dst[...] = small[n : n + 1, 0:count].reshape(count)
+    for cp in leaving:
         cp.wait()
 
 
@@ -1386,7 +1414,7 @@
             *[vmem(gain.shape, bf) for gain in (attn_gain, ffn_gain, query_gain, key_gain)],
             vmem((NDP, NSEQ, 8, 128), f32),
             vmem((D, 1024), bf), vmem((512, D), bf), vmem((D, 1536), bf), vmem((768, D), bf),
-            vmem((768, D), bf),
+            vmem((D, 1536), bf), vmem((768, D), bf),
             vmem((2, 2, 7, 32, 1024), bf), vmem((2, 7, 32, D), bf),
             vmem((2, 2, 7, 32, 1536), bf), vmem((2, 7, 48, D), bf),
             vmem((NSEQ, NDP, 32, D), bf), vmem((NSEQ, NDP, 32, D), bf), vmem((rows, D), bf),
@@ -1425,10 +1453,14 @@
             full(32, FF), full(32, FF), full(96, D),
             full(32), full(32), full(4), full(4),
         ),
-        in_specs=[anywhere, here, here, here, anywhere, anywhere, here],
+        in_specs=[pl.BlockSpec(memory_space=pltpu.HBM)] * 7,
         out_specs=[anywhere, here, here, here, here, anywhere, here, here, anywhere] + [here] * 4,
-        scratch_shapes=[dma((3,))],
-        compiler_params=pltpu.CompilerParams(vmem_limit_bytes=32 << 20),
+        scratch_shapes=[
+            vmem((MICRO, 128, D), bf), vmem((NDP, 32, 1024), bf), vmem((NDP, 32, 1536), bf),
+            vmem((8, 128), f32), vmem((MICRO, 128, D), bf), vmem((64, D), f32), vmem((96, D), f32),
+            dma((10,)),
+        ],
+        compiler_params=pltpu.CompilerParams(vmem_limit_bytes=61 << 20),
         name="finish",
     )(*results)
     return (finished[0][None], finished[1][None]) + tuple(finished[2:])

time: 248 us -> 235 us (0.948)
  Pallas kernels: 237 us -> 230 us
  local copies, waits for them, and re-layouts: 6.65 us -> 0 us
    pallas_call x1, Pallas kernels: 235 us -> 226 us  [tree_shards(): pl.pallas_call(functools.partial(layer_kernel, nodes), out_shape=(shape((...]
    unnamed x14 -> x0, local copies, waits for them, and re-layouts: 6.65 us -> none
where the time goes in v4:
time: 235 us; the launch traced here: 231 us
  Pallas kernels  230 us (98%)
    pallas_call x1, Pallas kernels, tree_shards(): pl.pallas_call(functools.partial(layer_kernel, nodes), out_shape=(shape((...  226 us

profile of v4, /device:TPU:21, one launch (start us, length us, event | category | flops | bytes accessed | tf_op | source)
XLA Modules:
  0.0 231.2 jit_solution(978808892528781228)
XLA Ops:
  0.7 226.5 %layer.1 = (bf16[2,128,1024]{2,1,0:T(8,128)(2,1)}, bf16[2,128,1024]{2,1,0:T(8,128)(2,1)}, bf16[4,32,1024]{2,1,0:T(8,128)(2,1)}, bf16[4,32,1536]{2,1,0:T(8,128)(2...) custom-call(bf16[2,128,1024]{2,1,0:T(8,128)(2,1)} %bitcast.4, bf16[2,128,1024]{2,1,0:T(8,128)(2,1)} %bitcast.5, ...), custom_call_target="tpu_custom_call" | custom-call | tf_op jit(solution)/shard_map/layer/pallas_call | solution.py:1399
  227.1 3.9 %finish.1 = (bf16[2,128,1024]{2,1,0:T(8,128)(2,1)}, f32[2,128,1024]{2,1,0:T(8,128)}, f32[32,2048]{1,0:T(8,128)}, f32[32,1024]{1,0:T(8,128)}, f32[32,1024]{1,0:T(...) custom-call(bf16[2,128,1024]{2,1,0:T(8,128)(2,1)} %get-tuple-element, ...), custom_call_target="tpu_custom_call" | custom-call | tf_op jit(solution)/shard_map/finish/pallas_call | solution.py:1448

commit v5 on v4

--- a/solution.py
+++ b/solution.py
@@ -397,8 +397,8 @@
 BLOCKS = (3, 2, 1, 0)
 SOFT = HEAD_DIM ** (-0.5) * 1.4426950408889634
 
-A0, A1, B, C0, C1, E = range(0, 60, 10)
-R_A0, R_A1, R_B, R_C0, R_C1, R_E = range(60, 120, 10)
+A0, A1, B, C0, C1, E0, E1, E2 = range(0, 80, 10)
+R_A0, R_A1, R_B, R_C0, R_C1, R_E0, R_E1, R_E2 = range(80, 160, 10)
 (
     ATTEND, MIX_MID, MIX_END, NORM_MID, NORM_END, LIFT, D_ACT, SINK, TURN_MID, TURN_END, LOW_MID,
     LOW_END, OUT_START, OUT_MID, OUT_END, ATTEND_BACK, IN_START, IN_MID, IN_END, PROJECT,
@@ -410,27 +410,30 @@
     LAND_A, LAND_C, GIVE_OUT, GIVE_IN, DRAIN,
 ) = range(600, 625, 1)
 ORDER = (
-    START, B, TOKENS, SMALL_DP, C_OUT, A_IN, A1, A0, B + 1, A1 + 1, A0 + 1, TREE_START, B + 2, SMALL_SEQ,
-    A1 + 2, C_IN, A0 + 2, B + 3, C1, A0 + 3, A1 + 3, C0, TREE_MID, NODE, B + 4, A0 + 4, TREE_END, A1 + 4,
-    TABLES, B + 5, A0 + 5, GAINS, A1 + 5, TABLES + 1, C0 + 1, A0 + 6, NORM_IN, NORM_IN + 1, A1 + 6, C1 + 1,
-    C0 + 2, B + 6, COTANGENT, A0 + 7, A1 + 7, PROJECT, E, C1 + 2, PROJECT + 1, COTANGENT + 1, PROJECT + 2,
-    PROJECT + 3, B + 7, ATTEND + 3, C0 + 3, ATTEND + 2, MIX_MID + 3, C1 + 3, E + 1, MIX_MID + 2, ATTEND + 1,
-    MIX_END + 3, MIX_MID + 1, ATTEND, C0 + 4, MIX_MID, C1 + 4, E + 2, MIX_END + 2, NORM_MID + 3, MIX_END + 1,
-    C0 + 5, NORM_END + 3, MIX_END, C1 + 5, E + 3, COT_START, C0 + 6, NORM_MID + 1, NORM_END + 1, C1 + 6,
-    E + 4, NORM_MID, NORM_END, NORM_MID + 2, C0 + 7, NORM_END + 2, C1 + 7, LIFT + 3, E + 5, LIFT, LIFT + 1,
-    COT_MID, E + 6, LIFT + 2, COT_END, GRAD_DOWN, R_E, E + 7, D_ACT + 3, D_ACT + 2, SINK + 3, D_ACT, R_E + 1,
-    TURN_MID + 3, D_ACT + 1, GRAD_WIDE + 1, R_C1, GRAD_WIDE, R_C0, R_E + 2, TURN_END + 3, SINK + 2, R_C1 + 1,
-    SINK + 1, TURN_MID + 2, R_C0 + 1, LOW_MID + 3, SINK, TURN_MID + 1, LOW_END + 3, R_E + 3, R_C1 + 2,
-    TURN_MID, TURN_END + 2, R_C0 + 2, ATTEND_BACK + 3, R_C1 + 3, TURN_END + 1, IN_START + 3, LOW_MID + 2,
-    R_E + 4, R_C0 + 3, TURN_END, LOW_END + 2, R_C1 + 4, ATTEND_BACK + 2, R_C0 + 4, LOW_MID, LOW_MID + 1,
-    R_C1 + 5, R_E + 5, LOW_END, LOW_END + 1, GRAD_OUT, R_B, R_C0 + 5, ATTEND_BACK + 1, R_C1 + 6, IN_START + 2,
-    IN_START + 1, R_B + 1, R_E + 6, R_C0 + 6, ATTEND_BACK, IN_START, GRAD_ATTN, R_A0, GRAD_ATTN + 1, R_A1,
-    R_B + 2, OUT_START + 3, IN_MID, R_A0 + 1, R_A1 + 1, IN_MID + 1, IN_MID + 2, R_B + 3, OUT_START, R_A0 + 2,
-    OUT_START + 1, R_A1 + 2, OUT_MID, R_B + 4, R_A0 + 3, IN_MID + 3, R_A1 + 3, OUT_START + 2, R_B + 5, IN_END,
-    R_A0 + 4, IN_END + 1, R_A1 + 4, OUT_MID + 3, OUT_MID + 2, R_B + 6, R_A0 + 5, IN_END + 3, R_A1 + 5,
-    IN_END + 2, GIVE_IN, OUT_END + 2, PACK_DP, OUT_END + 3, R_E + 7, OUT_MID + 1, R_A1 + 6, R_A0 + 6, OUT_END,
-    PACK_SEQ, R_C0 + 7, OUT_END + 1, R_C1 + 7, GIVE_OUT, PACK_END, LAND_C, R_A1 + 7, R_A0 + 7, R_B + 7,
-    LAND_A, DRAIN,
+    START, B, E0, E1, E2, B + 1, A_IN, A0, A1, B + 2, A0 + 1, A1 + 1, C_OUT, B + 3, A0 + 2, SMALL_DP, A1 + 2,
+    B + 4, TOKENS, A1 + 3, A0 + 3, SMALL_SEQ, TREE_START, C_IN, A1 + 4, A0 + 4, NODE, TABLES, B + 5,
+    TABLES + 1, A1 + 5, A0 + 5, C1, A1 + 6, A0 + 6, GAINS, TREE_MID, B + 6, COTANGENT + 1, C0, COTANGENT,
+    C1 + 1, A1 + 7, TREE_END, NORM_IN, NORM_IN + 1, A0 + 7, PROJECT, PROJECT + 1, PROJECT + 2, E2 + 1,
+    PROJECT + 3, C0 + 1, B + 7, ATTEND + 3, COT_START, E1 + 1, E0 + 1, C1 + 2, ATTEND + 2, C0 + 2, E0 + 2,
+    E2 + 2, MIX_MID + 3, MIX_MID + 2, C1 + 3, ATTEND + 1, C0 + 3, ATTEND, E1 + 2, C1 + 4, MIX_MID, C0 + 4,
+    E0 + 3, MIX_END + 3, C1 + 5, C0 + 5, E1 + 3, COT_MID, E2 + 3, MIX_END, MIX_MID + 1, C1 + 6, C0 + 6,
+    E0 + 4, NORM_MID + 3, MIX_END + 2, E1 + 4, COT_END, NORM_MID, C1 + 7, NORM_END + 3, E2 + 4, NORM_END,
+    MIX_END + 1, C0 + 7, LIFT + 3, E0 + 5, E2 + 5, NORM_MID + 2, E1 + 5, LIFT, NORM_MID + 1, NORM_END + 2,
+    LIFT + 2, NORM_END + 1, E0 + 6, E1 + 6, E2 + 6, LIFT + 1, GRAD_DOWN, R_E0, R_E2, E0 + 7, R_E1, E1 + 7,
+    E2 + 7, D_ACT + 3, SINK + 3, R_E0 + 1, D_ACT + 2, R_E2 + 1, D_ACT, D_ACT + 1, TURN_MID + 3, R_E1 + 1,
+    R_E0 + 2, R_E2 + 2, GRAD_WIDE + 1, R_C1, GRAD_WIDE, R_C0, TURN_END + 3, SINK + 2, R_E0 + 3, R_C1 + 1,
+    R_E2 + 3, TURN_MID + 2, SINK, R_C0 + 1, OUT_START + 3, LOW_MID + 3, TURN_MID, R_C1 + 2, SINK + 1,
+    R_E1 + 2, R_E0 + 4, TURN_END + 2, LOW_END + 3, TURN_MID + 1, R_C0 + 2, R_E2 + 4, TURN_END, R_C1 + 3,
+    ATTEND_BACK + 3, R_E1 + 3, R_C0 + 3, LOW_MID + 2, TURN_END + 1, R_E2 + 5, R_E0 + 5, R_C1 + 4, LOW_END + 2,
+    ATTEND_BACK + 2, R_C0 + 4, R_E1 + 4, LOW_MID + 1, LOW_MID, IN_START + 3, IN_START + 2, LOW_END, R_C1 + 5,
+    LOW_END + 1, GRAD_OUT, R_B, R_C0 + 5, R_E0 + 6, R_E2 + 6, R_E1 + 5, ATTEND_BACK + 1, IN_START + 1,
+    R_C1 + 6, R_B + 1, ATTEND_BACK, R_C0 + 6, IN_START, GRAD_ATTN + 1, R_A1, R_B + 2, GRAD_ATTN, R_A0,
+    IN_MID + 1, IN_MID + 2, R_A1 + 1, OUT_START, R_B + 3, R_E0 + 7, IN_MID + 3, R_A0 + 1, IN_MID, OUT_MID,
+    R_A1 + 2, OUT_MID + 3, R_B + 4, R_A0 + 2, R_C0 + 7, R_A1 + 3, R_B + 5, IN_END + 2, R_A0 + 3, IN_END,
+    R_A1 + 4, IN_END + 3, R_B + 6, R_A0 + 4, IN_END + 1, GIVE_IN, PACK_DP, OUT_START + 2, R_A1 + 5,
+    OUT_MID + 2, R_A0 + 5, OUT_START + 1, OUT_MID + 1, OUT_END, R_C1 + 7, PACK_SEQ, R_E2 + 7, OUT_END + 2,
+    R_E1 + 6, OUT_END + 3, R_B + 7, R_A1 + 6, R_A0 + 6, OUT_END + 1, GIVE_OUT, PACK_END, R_E1 + 7, R_A1 + 7,
+    LAND_C, R_A0 + 7, LAND_A, DRAIN,
 )
 
 
@@ -445,19 +448,12 @@
     return 2 * (2 * m + c) + (m + c + x) % 2
 
 
-def greet_all(d, s):
+def greet_near(d, s, up, down):
     barrier = pltpu.get_barrier_semaphore()
-    me = d * NSEQ + s
-
-    def signal(i, carry):
-        other = (me + i) % (NDP * NSEQ)
-        pl.semaphore_signal(
-            barrier, inc=1, device_id=(other // NSEQ, other % NSEQ), device_id_type=MESH
-        )
-        return carry
-
-    lax.fori_loop(1, NDP * NSEQ, signal, 0)
-    pl.semaphore_wait(barrier, NDP * NSEQ - 1)
+    near = [((d + i) % NDP, s) for i in range(1, NDP)] + [(d, up), (d, down)]
+    for other in near:
+        pl.semaphore_signal(barrier, inc=1, device_id=other, device_id_type=MESH)
+    pl.semaphore_wait(barrier, len(near))
 
 
 def remote(src, dst, sems, at, d, s):
@@ -585,11 +581,12 @@
             return pl.ds(aligned((2 * way + (n + (n > 2)) % 2) * 256 + j * 32, 32), 32)
         if n == 2:
             return pl.ds(aligned(j * 64 + way * 32, 32), 32)
-        return pl.ds(aligned(j * 96 + way * 48, 16), 48)
-
-    weight = {0: wa, 1: wa, 2: wb, 3: wc, 4: wc, 5: we}
-    grads = {0: wa, 1: wa, 2: wb, 3: gc, 4: gc, 5: ge}
-    hops = {0: hop_a.at[0], 1: hop_a.at[1], 2: hop_b, 3: hop_c.at[0], 4: hop_c.at[1], 5: hop_e}
+        return pl.ds(aligned(j * 96 + way * 48 + (n - 5) * 16, 16), 16)
+
+    weight = {0: wa, 1: wa, 2: wb, 3: wc, 4: wc, 5: we, 6: we, 7: we}
+    grads = {0: wa, 1: wa, 2: wb, 3: gc, 4: gc, 5: ge, 6: ge, 7: ge}
+    hops = {0: hop_a.at[0], 1: hop_a.at[1], 2: hop_b, 3: hop_c.at[0], 4: hop_c.at[1]}
+    hops.update({5 + i: hop_e.at[i] for i in range(3)})
 
     def owner_at(way, k):
         return seq_at((p + NSEQ - k) % NSEQ) if way == 0 else seq_at((p + k) % NSEQ)
@@ -746,7 +743,7 @@
     def _():
         for cp in raws:
             cp.start()
-        greet_all(d, s)
+        greet_near(d, s, up, down)
         fill_b.start()
         fill_e.start()
         for n in range(3):
@@ -798,7 +795,7 @@
         for n in range(3, 5):
             columns_in(n)
 
-    streams = ((A0, 0), (A1, 1), (B, 2), (C0, 3), (C1, 4), (E, 5))
+    streams = ((A0, 0), (A1, 1), (B, 2), (C0, 3), (C1, 4), (E0, 5), (E1, 6), (E2, 7))
 
     def ring_first(n):
         if n == 2:
@@ -1113,14 +1110,8 @@
         for i in (sub, 2 + sub):
             cols = pl.ds(i * 256, 256)
 
-            def one(t, carry):
-                lanes = pl.ds(aligned(512 * t, 512), 512)
-                gc[cols, lanes] = across(
-                    normed_mid[:, :, :, cols].reshape(NSEQ * 128, 256), both[:, lanes]
-                ).astype(bf)
-                return carry
-
-            lax.fori_loop(0, 3, one, 0)
+            rows = normed_mid[:, :, :, cols].reshape(NSEQ * 128, 256)
+            gc[cols] = across(rows, both[...]).astype(bf)
 
     d_lin = tree
 
@@ -1141,14 +1132,15 @@
         def one(h, carry):
             kv = h // 2
             grown, inverse = weights_of(b, h, n)
-            prob = grown * inverse
             d_out = d_att[here, head_lanes(h)]
+            wide_out = d_out.astype(f32)
             d_prob = against(d_out, value[keys, head_lanes(kv)])
-            delta = jnp.sum(prob * d_prob, axis=-1, keepdims=True)
-            d_raw = (prob * (d_prob - delta) * HEAD_DIM ** (-0.5)).astype(bf)
-            d_rot = product(d_raw, heads[4 + kv, keys])
-            d_key[kv, keys] += across(d_raw, heads[h, here])
-            d_value[kv, keys] += across(prob.astype(bf), d_out)
+            delta = jnp.sum(wide_out * att[here, head_lanes(h)].astype(f32), axis=-1, keepdims=True)
+            d_raw = (grown * (d_prob - delta)).astype(bf)
+            factor = inverse * HEAD_DIM ** (-0.5)
+            d_rot = product(d_raw, heads[4 + kv, keys]) * factor
+            d_key[kv, keys] += across(d_raw, (heads[h, here].astype(f32) * factor).astype(bf))
+            d_value[kv, keys] += across(grown.astype(bf), (wide_out * inverse).astype(bf))
             back, d_gain = turn_back(
                 d_rot, lin[here, head_lanes(h)], head_g[0:1, :], cosine[here], sine[here]
             )
@@ -1185,14 +1177,7 @@
         for i in (sub, 2 + sub):
             cols = pl.ds(i * 256, 256)
 
-            def one(t, carry):
-                lanes = pl.ds(aligned(512 * t, 512), 512)
-                wa[cols, lanes] = across(
-                    normed_in[:, cols], d_lin[:, :, :, lanes].reshape(NSEQ * 128, 512)
-                ).astype(bf)
-                return carry
-
-            lax.fori_loop(0, 2, one, 0)
+            wa[cols] = across(normed_in[:, cols], d_lin[...].reshape(NSEQ * 128, 1024)).astype(bf)
 
     def to_grad(i, rows):
         unit, scale = unit_of(tree_own[i].astype(f32))
@@ -1292,11 +1277,13 @@
     stage(LAND_A)(lambda: land(res_a, 0))
     stage(LAND_C)(lambda: land(res_c, 1))
 
-    def take_rows(dst, rows, way, total):
-        dst[rows * way : rows * (way + 1)] = total
-
-    stage(R_B + 7)(lambda: reduce_end(2, functools.partial(take_rows, g_output, 32)))
-    stage(R_E + 7)(lambda: reduce_end(5, functools.partial(take_rows, g_down, 48)))
+    def take_rows(dst, rows, at, way, total):
+        dst[pl.ds(rows * way + at, total.shape[0])] = total
+
+    stage(R_B + 7)(lambda: reduce_end(2, functools.partial(take_rows, g_output, 32, 0)))
+    for label, n in streams[5:]:
+        take = functools.partial(take_rows, g_down, 48, (n - 5) * 16)
+        stage(R_A0 + label + 7)(functools.partial(reduce_end, n, take))
 
     @stage(DRAIN)
     def _():
@@ -1315,9 +1302,9 @@
             for i in range(1, NDP):
                 q = (d + i) % NDP
                 remote(fin.at[q], landed.at[d], fin_sems, (n, d), q, s).wait_send()
-        for n in (3, 4, 5):
+        for n in range(3, 8):
             gather_sent(n)
-        for n in range(6):
+        for n in range(8):
             reduce_sent(n)
         spread_cot.sent(everything)
         for b in BLOCKS:
@@ -1416,7 +1403,7 @@
             vmem((D, 1024), bf), vmem((512, D), bf), vmem((D, 1536), bf), vmem((768, D), bf),
             vmem((D, 1536), bf), vmem((768, D), bf),
             vmem((2, 2, 7, 32, 1024), bf), vmem((2, 7, 32, D), bf),
-            vmem((2, 2, 7, 32, 1536), bf), vmem((2, 7, 48, D), bf),
+            vmem((2, 2, 7, 32, 1536), bf), vmem((3, 2, 7, 16, D), bf),
             vmem((NSEQ, NDP, 32, D), bf), vmem((NSEQ, NDP, 32, D), bf), vmem((rows, D), bf),
             vmem((NSEQ, NDP, 32, D), bf), vmem((NSEQ, NDP, 32, D), bf), vmem(quarter, bf),
             vmem((rows, 768), f32), vmem((6, rows, 128), bf),
@@ -1432,7 +1419,7 @@
             vmem((NDP, 24, 128), f32), vmem((NSEQ, 24, 128), f32), vmem((24, 128), f32),
             dma((16,)),
             *twice(12), *twice(5, NDP), dma((2, MICRO, NDP)), dma((2,)),
-            *twice(6, 2, 7), *twice(6, 2, 7),
+            *twice(8, 2, 7), *twice(8, 2, 7),
             *twice(4, 3, 4), *twice(2, 3), *twice(2, 3, 4),
             dma((2, NSEQ)), dma((2,)), *twice(2, NDP), *twice(12),
         ],

time: 235 us -> 227 us (0.966)
  Pallas kernels: 230 us -> 223 us
    pallas_call x1, Pallas kernels: 226 us -> 219 us  [tree_shards(): pl.pallas_call(functools.partial(layer_kernel, nodes), out_shape=(shape((...]
where the time goes in v5:
time: 227 us; the launch traced here: 224 us
  Pallas kernels  223 us (98%)
    pallas_call x1, Pallas kernels, tree_shards(): pl.pallas_call(functools.partial(layer_kernel, nodes), out_shape=(shape((...  219 us

profile of v5, /device:TPU:21, one launch (start us, length us, event | category | flops | bytes accessed | tf_op | source)
XLA Modules:
  0.0 223.7 jit_solution(11825641701580077519)
XLA Ops:
  0.7 218.9 %layer.1 = (bf16[2,128,1024]{2,1,0:T(8,128)(2,1)}, bf16[2,128,1024]{2,1,0:T(8,128)(2,1)}, bf16[4,32,1024]{2,1,0:T(8,128)(2,1)}, bf16[4,32,1536]{2,1,0:T(8,128)(2...) custom-call(bf16[2,128,1024]{2,1,0:T(8,128)(2,1)} %bitcast.4, bf16[2,128,1024]{2,1,0:T(8,128)(2,1)} %bitcast.5, ...), custom_call_target="tpu_custom_call" | custom-call | tf_op jit(solution)/shard_map/layer/pallas_call | solution.py:1386
  219.6 3.9 %finish.1 = (bf16[2,128,1024]{2,1,0:T(8,128)(2,1)}, f32[2,128,1024]{2,1,0:T(8,128)}, f32[32,2048]{1,0:T(8,128)}, f32[32,1024]{1,0:T(8,128)}, f32[32,1024]{1,0:T(...) custom-call(bf16[2,128,1024]{2,1,0:T(8,128)(2,1)} %get-tuple-element, ...), custom_call_target="tpu_custom_call" | custom-call | tf_op jit(solution)/shard_map/finish/pallas_call | solution.py:1435

commit v6 on v5

--- a/solution.py
+++ b/solution.py
@@ -558,7 +558,7 @@
     lin, heads, value, hidden, member, cosine, sine, att, d_att,
     part, part_out, near, sent, got, near_o, sent_o, got_o,
     middle, d_middle, act, both, d_key, d_value, outs, grad_low,
-    fin_a, fin_c, attn_g, ffn_g, head_g, pack_dp, pack_seq, pack_sum,
+    fin_a, fin_c, attn_g, ffn_g, head_g, packed, pack_dp, pack_seq, pack_sum, pack_cut,
     loc, s_small, r_small, s_col, r_col, s_tok, r_tok, s_ag, r_ag, s_rs, r_rs,
     s_sum, r_sum, s_tree, r_tree, s_spread, r_spread, s_back, r_back, s_fin, r_fin, s_pack, r_pack,
 ):
@@ -777,8 +777,14 @@
         for i in range(1, NDP):
             place = smalls.at[(d + NDP - i) % NDP, s]
             remote(place, place, small_sems, i, d, s).wait_recv()
+        lane = lax.broadcasted_iota(jnp.int32, (1, 128), 1)
+        for q in range(NDP):
+            rows = [smalls[q, s, row : row + 1, :] for row in range(4)]
+            tail = jnp.where(lane < 68, rows[2], rows[3])
+            packed[s, q : q + 1, :] = jnp.where(lane < 32, rows[0], jnp.where(lane < 64, rows[1], tail))
+            packed[s, q + 4 : q + 5, :] = jnp.zeros((1, 128), f32)
         for i in range(1, NSEQ):
-            launch(remote(smalls.at[:, s], smalls.at[:, s], small_sems, NDP + i, d, (s + i) % NSEQ))
+            launch(remote(packed.at[s], packed.at[s], small_sems, NDP + i, d, (s + i) % NSEQ))
 
     @stage(A_IN)
     def _():
@@ -880,24 +886,28 @@
     @stage(GAINS)
     def _():
         for i in range(1, NSEQ):
-            place = smalls.at[:, (s + NSEQ - i) % NSEQ]
+            place = packed.at[(s + NSEQ - i) % NSEQ]
             remote(place, place, small_sems, NDP + i, d, s).wait_recv()
         lane = lax.broadcasted_iota(jnp.int32, (1, 128), 1)
-        for row, dst in ((0, attn_g), (1, ffn_g)):
+
+        def moved(i, source, target):
+            line = packed[i % NSEQ, i // NSEQ : i // NSEQ + 1, :]
+            shift = (target - source) % 128
+            return pltpu.roll(line, shift, 1) if shift else line
+
+        for source, dst in ((0, attn_g), (32, ffn_g)):
             for j in range(8):
-                parts = [
-                    smalls[(4 * j + i) // 8, (4 * j + i) % 8, row : row + 1, :] for i in range(4)
-                ]
+                parts = [moved(4 * j + i, source, 32 * i) for i in range(4)]
                 dst[:, 128 * j : 128 * (j + 1)] = jnp.where(
                     lane < 64,
                     jnp.where(lane < 32, parts[0], parts[1]),
                     jnp.where(lane < 96, parts[2], parts[3]),
                 )
-        for row in (2, 3):
+        for row in range(2):
             joined = jnp.zeros((1, 128), f32)
             for i in range(32):
-                joined = jnp.where(lane // 4 == i, smalls[i // 8, i % 8, row : row + 1, :], joined)
-            head_g[row - 2 : row - 1, :] = joined
+                joined = jnp.where(lane // 4 == i, moved(i, 64 + 4 * row, 4 * i), joined)
+            head_g[row : row + 1, :] = joined
         pack_dp[d] = jnp.zeros((24, 128), f32)
 
     def norm_in(i, carry):
@@ -1223,9 +1233,18 @@
         for i in range(1, NDP):
             place = pack_dp.at[(d + NDP - i) % NDP]
             remote(place, place, pack_sems, i, d, s).wait_recv()
-        pack_seq[s] = (pack_dp[0] + pack_dp[1]) + (pack_dp[2] + pack_dp[3])
+        pack_sum[...] = (pack_dp[0] + pack_dp[1]) + (pack_dp[2] + pack_dp[3])
+        for j in range(NSEQ):
+            block = 2 * d + j // 4
+            wide = (128 - 32 * (j % 4)) % 128
+            thin = (256 - 32 * d - 4 * j) % 128
+            pack_cut[j] = jnp.zeros((8, 128), f32)
+            for n, (row, shift) in enumerate(((block, wide), (8 + block, wide), (16, thin), (17, thin))):
+                pack_cut[j, n : n + 1, :] = pltpu.roll(pack_sum[pl.ds(row, 1), :], shift, 1)
+        pack_seq[s] = pack_cut[s]
         for i in range(1, NSEQ):
-            launch(remote(pack_seq.at[s], pack_seq.at[s], pack_sems, NDP + i, d, (s + i) % NSEQ))
+            j = (s + i) % NSEQ
+            launch(remote(pack_cut.at[j], pack_seq.at[s], pack_sems, NDP + i, d, j))
 
     @stage(PACK_END)
     def _():
@@ -1235,14 +1254,7 @@
         total = pack_seq[0]
         for j in range(1, NSEQ):
             total = total + pack_seq[j]
-        pack_sum[...] = total
-        at = d * NSEQ + s
-        for n, (row, count) in enumerate(
-            ((at // 4, 32), (8 + at // 4, 32), (16, 4), (17, 4))
-        ):
-            line = pack_sum[pl.ds(row, 1), :]
-            shift = (128 - (at * count) % 128) % 128
-            pack_out[n : n + 1, :] = pltpu.roll(line, shift, 1)
+        pack_out[...] = total
 
     def close_cols(n, fin, landed, which):
         sub = (n + (n > 2)) % 2
@@ -1416,7 +1428,8 @@
             vmem((2, rows, 128), f32), vmem((2, rows, 128), f32), vmem(quarter, bf), vmem(quarter, bf),
             vmem((NDP, 32, 1024), bf), vmem((NDP, 32, 1536), bf),
             vmem((1, D), f32), vmem((1, D), f32), vmem((8, 128), f32),
-            vmem((NDP, 24, 128), f32), vmem((NSEQ, 24, 128), f32), vmem((24, 128), f32),
+            vmem((NSEQ, 8, 128), f32), vmem((NDP, 24, 128), f32), vmem((NSEQ, 8, 128), f32),
+            vmem((24, 128), f32), vmem((NSEQ, 8, 128), f32),
             dma((16,)),
             *twice(12), *twice(5, NDP), dma((2, MICRO, NDP)), dma((2,)),
             *twice(8, 2, 7), *twice(8, 2, 7),

time: 227 us -> 223 us (0.982)
  Pallas kernels: 223 us -> 219 us
    pallas_call x1, Pallas kernels: 219 us -> 215 us  [tree_shards(): pl.pallas_call(functools.partial(layer_kernel, nodes), out_shape=(shape((...]
where the time goes in v6:
time: 223 us; the launch traced here: 220 us
  Pallas kernels  219 us (98%)
    pallas_call x1, Pallas kernels, tree_shards(): pl.pallas_call(functools.partial(layer_kernel, nodes), out_shape=(shape((...  215 us

profile of v6, /device:TPU:21, one launch (start us, length us, event | category | flops | bytes accessed | tf_op | source)
XLA Modules:
  0.0 219.6 jit_solution(3554260843342089026)
XLA Ops:
  0.7 214.9 %layer.1 = (bf16[2,128,1024]{2,1,0:T(8,128)(2,1)}, bf16[2,128,1024]{2,1,0:T(8,128)(2,1)}, bf16[4,32,1024]{2,1,0:T(8,128)(2,1)}, bf16[4,32,1536]{2,1,0:T(8,128)(2...) custom-call(bf16[2,128,1024]{2,1,0:T(8,128)(2,1)} %bitcast.4, bf16[2,128,1024]{2,1,0:T(8,128)(2,1)} %bitcast.5, ...), custom_call_target="tpu_custom_call" | custom-call | tf_op jit(solution)/shard_map/layer/pallas_call | solution.py:1398
  215.5 3.9 %finish.1 = (bf16[2,128,1024]{2,1,0:T(8,128)(2,1)}, f32[2,128,1024]{2,1,0:T(8,128)}, f32[32,2048]{1,0:T(8,128)}, f32[32,1024]{1,0:T(8,128)}, f32[32,1024]{1,0:T(...) custom-call(bf16[2,128,1024]{2,1,0:T(8,128)(2,1)} %get-tuple-element, ...), custom_call_target="tpu_custom_call" | custom-call | tf_op jit(solution)/shard_map/finish/pallas_call | solution.py:1448

commit v7 on v6

--- a/solution.py
+++ b/solution.py
@@ -410,30 +410,30 @@
     LAND_A, LAND_C, GIVE_OUT, GIVE_IN, DRAIN,
 ) = range(600, 625, 1)
 ORDER = (
-    START, B, E0, E1, E2, B + 1, A_IN, A0, A1, B + 2, A0 + 1, A1 + 1, C_OUT, B + 3, A0 + 2, SMALL_DP, A1 + 2,
-    B + 4, TOKENS, A1 + 3, A0 + 3, SMALL_SEQ, TREE_START, C_IN, A1 + 4, A0 + 4, NODE, TABLES, B + 5,
-    TABLES + 1, A1 + 5, A0 + 5, C1, A1 + 6, A0 + 6, GAINS, TREE_MID, B + 6, COTANGENT + 1, C0, COTANGENT,
-    C1 + 1, A1 + 7, TREE_END, NORM_IN, NORM_IN + 1, A0 + 7, PROJECT, PROJECT + 1, PROJECT + 2, E2 + 1,
-    PROJECT + 3, C0 + 1, B + 7, ATTEND + 3, COT_START, E1 + 1, E0 + 1, C1 + 2, ATTEND + 2, C0 + 2, E0 + 2,
-    E2 + 2, MIX_MID + 3, MIX_MID + 2, C1 + 3, ATTEND + 1, C0 + 3, ATTEND, E1 + 2, C1 + 4, MIX_MID, C0 + 4,
-    E0 + 3, MIX_END + 3, C1 + 5, C0 + 5, E1 + 3, COT_MID, E2 + 3, MIX_END, MIX_MID + 1, C1 + 6, C0 + 6,
-    E0 + 4, NORM_MID + 3, MIX_END + 2, E1 + 4, COT_END, NORM_MID, C1 + 7, NORM_END + 3, E2 + 4, NORM_END,
-    MIX_END + 1, C0 + 7, LIFT + 3, E0 + 5, E2 + 5, NORM_MID + 2, E1 + 5, LIFT, NORM_MID + 1, NORM_END + 2,
-    LIFT + 2, NORM_END + 1, E0 + 6, E1 + 6, E2 + 6, LIFT + 1, GRAD_DOWN, R_E0, R_E2, E0 + 7, R_E1, E1 + 7,
-    E2 + 7, D_ACT + 3, SINK + 3, R_E0 + 1, D_ACT + 2, R_E2 + 1, D_ACT, D_ACT + 1, TURN_MID + 3, R_E1 + 1,
-    R_E0 + 2, R_E2 + 2, GRAD_WIDE + 1, R_C1, GRAD_WIDE, R_C0, TURN_END + 3, SINK + 2, R_E0 + 3, R_C1 + 1,
-    R_E2 + 3, TURN_MID + 2, SINK, R_C0 + 1, OUT_START + 3, LOW_MID + 3, TURN_MID, R_C1 + 2, SINK + 1,
-    R_E1 + 2, R_E0 + 4, TURN_END + 2, LOW_END + 3, TURN_MID + 1, R_C0 + 2, R_E2 + 4, TURN_END, R_C1 + 3,
-    ATTEND_BACK + 3, R_E1 + 3, R_C0 + 3, LOW_MID + 2, TURN_END + 1, R_E2 + 5, R_E0 + 5, R_C1 + 4, LOW_END + 2,
-    ATTEND_BACK + 2, R_C0 + 4, R_E1 + 4, LOW_MID + 1, LOW_MID, IN_START + 3, IN_START + 2, LOW_END, R_C1 + 5,
-    LOW_END + 1, GRAD_OUT, R_B, R_C0 + 5, R_E0 + 6, R_E2 + 6, R_E1 + 5, ATTEND_BACK + 1, IN_START + 1,
-    R_C1 + 6, R_B + 1, ATTEND_BACK, R_C0 + 6, IN_START, GRAD_ATTN + 1, R_A1, R_B + 2, GRAD_ATTN, R_A0,
-    IN_MID + 1, IN_MID + 2, R_A1 + 1, OUT_START, R_B + 3, R_E0 + 7, IN_MID + 3, R_A0 + 1, IN_MID, OUT_MID,
-    R_A1 + 2, OUT_MID + 3, R_B + 4, R_A0 + 2, R_C0 + 7, R_A1 + 3, R_B + 5, IN_END + 2, R_A0 + 3, IN_END,
-    R_A1 + 4, IN_END + 3, R_B + 6, R_A0 + 4, IN_END + 1, GIVE_IN, PACK_DP, OUT_START + 2, R_A1 + 5,
-    OUT_MID + 2, R_A0 + 5, OUT_START + 1, OUT_MID + 1, OUT_END, R_C1 + 7, PACK_SEQ, R_E2 + 7, OUT_END + 2,
-    R_E1 + 6, OUT_END + 3, R_B + 7, R_A1 + 6, R_A0 + 6, OUT_END + 1, GIVE_OUT, PACK_END, R_E1 + 7, R_A1 + 7,
-    LAND_C, R_A0 + 7, LAND_A, DRAIN,
+    START, B, SMALL_DP, E0, E2, E1, B + 1, E0 + 1, A_IN, A0, A1, B + 2, A0 + 1, A1 + 1, B + 3, A0 + 2, A1 + 2,
+    B + 4, TOKENS, A1 + 3, C_OUT, A0 + 3, B + 5, TREE_START, A1 + 4, A0 + 4, B + 6, A1 + 5, SMALL_SEQ, A0 + 5,
+    NODE, C_IN, C0, TABLES, TABLES + 1, A1 + 6, A0 + 6, E2 + 1, C1, GAINS, TREE_MID, C0 + 1, B + 7, COTANGENT,
+    COTANGENT + 1, A1 + 7, TREE_END, NORM_IN, A0 + 7, NORM_IN + 1, PROJECT, PROJECT + 1, E2 + 2, PROJECT + 2,
+    PROJECT + 3, ATTEND + 3, C1 + 1, ATTEND + 2, C0 + 2, MIX_MID + 3, MIX_MID + 2, E1 + 1, ATTEND + 1, C1 + 2,
+    E0 + 2, E2 + 3, MIX_MID + 1, MIX_END + 3, C0 + 3, ATTEND, C1 + 3, E1 + 2, MIX_MID, MIX_END + 2, C0 + 4,
+    C1 + 4, NORM_MID + 3, E1 + 3, MIX_END + 1, MIX_END, C0 + 5, C1 + 5, COT_START, E0 + 3, NORM_MID + 1,
+    C0 + 6, C1 + 6, NORM_MID + 2, E1 + 4, E2 + 4, NORM_END + 2, NORM_MID, NORM_END + 1, NORM_END,
+    NORM_END + 3, E0 + 4, C0 + 7, C1 + 7, LIFT + 2, E1 + 5, E2 + 5, E0 + 5, LIFT, LIFT + 1, E1 + 6, COT_MID,
+    E0 + 6, E2 + 6, LIFT + 3, COT_END, GRAD_DOWN, R_E0, E2 + 7, E1 + 7, R_E2, R_E1, E0 + 7, D_ACT + 1,
+    D_ACT + 2, R_E2 + 1, D_ACT + 3, R_E0 + 1, R_E1 + 1, D_ACT, GRAD_WIDE, R_C0, SINK + 3, R_E2 + 2, SINK + 2,
+    TURN_MID + 3, R_E0 + 2, R_E1 + 2, SINK, R_C0 + 1, TURN_MID + 2, R_E2 + 3, GRAD_WIDE + 1, R_C1,
+    TURN_END + 3, R_C0 + 2, R_E1 + 3, SINK + 1, TURN_MID, TURN_END + 2, R_C1 + 1, OUT_START + 3, R_E0 + 3,
+    OUT_START + 2, R_E2 + 4, LOW_MID + 3, R_C0 + 3, TURN_MID + 1, R_E1 + 4, LOW_END + 3, TURN_END, R_C1 + 2,
+    ATTEND_BACK + 3, R_E2 + 5, LOW_MID + 2, R_C0 + 4, R_E1 + 5, TURN_END + 1, R_E0 + 4, R_C1 + 3, LOW_END + 2,
+    ATTEND_BACK + 2, R_C0 + 5, LOW_MID + 1, LOW_MID, R_E0 + 5, R_E2 + 6, IN_START + 2, IN_START + 3,
+    OUT_MID + 2, LOW_END + 1, R_C1 + 4, LOW_END, GRAD_OUT, R_B, R_C0 + 6, ATTEND_BACK + 1, R_C1 + 5,
+    IN_START + 1, R_E1 + 6, R_E0 + 6, R_B + 1, ATTEND_BACK, R_C1 + 6, IN_START, GRAD_ATTN + 1, R_A1,
+    GRAD_ATTN, R_A0, IN_MID + 3, R_B + 2, R_C1 + 7, R_A1 + 1, IN_MID, R_A0 + 1, R_B + 3, R_A1 + 2, IN_MID + 1,
+    R_A0 + 2, OUT_START + 1, R_B + 4, IN_MID + 2, OUT_START, R_A1 + 3, OUT_MID + 3, OUT_MID + 1, R_A0 + 3,
+    R_B + 5, OUT_MID, R_A1 + 4, IN_END, R_A0 + 4, IN_END + 3, R_B + 6, IN_END + 2, R_E1 + 7, R_A1 + 5,
+    IN_END + 1, R_A0 + 5, PACK_DP, GIVE_IN, R_A1 + 6, OUT_END + 2, PACK_SEQ, R_C0 + 7, R_B + 7, OUT_END,
+    LAND_C, R_E0 + 7, OUT_END + 1, R_A0 + 6, OUT_END + 3, GIVE_OUT, R_A1 + 7, R_A0 + 7, R_E2 + 7, PACK_END,
+    LAND_A, DRAIN,
 )
 
 
@@ -1019,7 +1019,7 @@
             right = pl.ds(aligned(768 + t * 256, 256), 256)
             gate = product(rows, wc[:, left])
             wide = product(rows, wc[:, right])
-            sigma = 1.0 / (1.0 + jnp.exp(-gate))
+            sigma = 0.5 + 0.5 * jnp.tanh(0.5 * gate)
             silu = gate * sigma
             act[here, left] = (silu * wide).astype(bf)
             both[here, left] = (wide * sigma * (1.0 + gate * (1.0 - sigma))).astype(bf)

time: 223 us -> 223 us (level)
  no operation moved by 1% of the time
where the time goes in v7:
time: 223 us; the launch traced here: 219 us
  Pallas kernels  218 us (98%)
    pallas_call x1, Pallas kernels, tree_shards(): pl.pallas_call(functools.partial(layer_kernel, nodes), out_shape=(shape((...  214 us

profile of v7, /device:TPU:21, one launch (start us, length us, event | category | flops | bytes accessed | tf_op | source)
XLA Modules:
  0.0 219.1 jit_solution(9291829950569573810)
XLA Ops:
  0.7 214.4 %layer.1 = (bf16[2,128,1024]{2,1,0:T(8,128)(2,1)}, bf16[2,128,1024]{2,1,0:T(8,128)(2,1)}, bf16[4,32,1024]{2,1,0:T(8,128)(2,1)}, bf16[4,32,1536]{2,1,0:T(8,128)(2...) custom-call(bf16[2,128,1024]{2,1,0:T(8,128)(2,1)} %bitcast.4, bf16[2,128,1024]{2,1,0:T(8,128)(2,1)} %bitcast.5, ...), custom_call_target="tpu_custom_call" | custom-call | tf_op jit(solution)/shard_map/layer/pallas_call | solution.py:1398
  215.0 3.9 %finish.1 = (bf16[2,128,1024]{2,1,0:T(8,128)(2,1)}, f32[2,128,1024]{2,1,0:T(8,128)}, f32[32,2048]{1,0:T(8,128)}, f32[32,1024]{1,0:T(8,128)}, f32[32,1024]{1,0:T(...) custom-call(bf16[2,128,1024]{2,1,0:T(8,128)(2,1)} %get-tuple-element, ...), custom_call_target="tpu_custom_call" | custom-call | tf_op jit(solution)/shard_map/finish/pallas_call | solution.py:1448
